TPU v7x, 32 devices: a whole 2x2x4 slice. The times are simulated.
32 devices in a mesh: row: 8 (over z, x), col: 4 (over y, core).
Axes of the slice: x: 2, y: 2, z: 4, core: 2. Of those that a mesh axis runs over, the one named last changes fastest.
Arguments:
- right_side: float32 [6, 8, 64, 128], P(None, 'row'), may hold values from -6 to 6
- inverses: float32 [6, 8, 128, 128], P(None, 'row'), may hold values from -1 to 3
- factor_blocks: bfloat16 [15, 8, 8, 128, 128], P(None, 'row', 'col'), may hold values from -0.15625 to 0.15625
- pattern: int32 [15, 8, 8], P(None, 'row', 'col'), may hold values 0 or 1
Outputs:
- forward_part: float32 [6, 8, 64, 128], P(None, 'row')
- solution: float32 [6, 8, 64, 128], P(None, 'row')
All inputs are finite; a program needn't handle non-finite values. No bound on the sum of `pattern` on one device may be relied on, other than what follows from the above.
Results may differ from a plain program's by a relative error of at most 0.014.
Values may be sent and summed in bfloat16 or wider, within the bound.
No kernel may reach another device: no remote copies, remote signals or barrier semaphores. Data moves between devices by JAX's collectives and lax.ppermute only.
A program may use at most 64 MiB of HBM per device.

v0:
```python
import jax
import jax.numpy as jnp
from jax import lax
from jax.sharding import PartitionSpec as P


def spread(block, axis, holder):
    block = jnp.where(lax.axis_index(axis) == holder, block, jnp.zeros_like(block))
    return lax.psum(block, axis)


def pair_number(higher, lower_level):
    return higher * (higher - 1) // 2 + lower_level


def masked_block(factor_blocks, pattern, pair_index):
    return jnp.where(
        pattern[pair_index][:, :, None, None] != 0,
        factor_blocks[pair_index],
        jnp.zeros((), factor_blocks.dtype),
    )


def shards(right_side, inverses, factor_blocks, pattern):
    levels = right_side.shape[0]
    width_col = factor_blocks.shape[2]
    row_index = lax.axis_index("row")
    col_index = lax.axis_index("col")
    solved = []
    gathered = []
    for height in range(levels):
        remaining = right_side[height]
        if height > 0:
            partial_value = jnp.zeros(remaining.shape, jnp.float32)
            for earlier in range(height):
                masked = masked_block(factor_blocks, pattern, pair_number(height, earlier))
                partial_value = partial_value + jnp.einsum(
                    "ikab,knb->ina", masked, gathered[earlier], preferred_element_type=jnp.float32
                )
            summed = lax.psum(partial_value.astype(jnp.bfloat16), "col").astype(jnp.float32)
            remaining = remaining - summed
        segment = jnp.einsum(
            "inb,iab->ina", remaining, inverses[height], precision=lax.Precision.HIGHEST
        )
        solved.append(segment)
        if height < levels - 1:
            gathered_all = lax.all_gather(segment.astype(jnp.bfloat16), "row", axis=0, tiled=True)
            gathered.append(
                lax.dynamic_slice_in_dim(gathered_all, col_index * width_col, width_col, 0)
            )
    results = [None] * levels
    settled = [None] * levels
    for height in range(levels - 1, -1, -1):
        remaining = solved[height]
        if height < levels - 1:
            partial_value = jnp.zeros((width_col,) + remaining.shape[1:], jnp.float32)
            for later in range(height + 1, levels):
                masked = masked_block(factor_blocks, pattern, pair_number(later, height))
                partial_value = partial_value + jnp.einsum(
                    "ikab,ina->knb", masked, settled[later], preferred_element_type=jnp.float32
                )
            offset = jnp.clip(row_index - col_index * width_col, 0, width_col - 1)
            owner_col = row_index // width_col
            summed = lax.psum(partial_value, "row")
            own_sum = lax.dynamic_slice_in_dim(summed, offset, 1, 0)
            own_sum = spread(own_sum.astype(jnp.bfloat16), "col", owner_col).astype(own_sum.dtype)
            remaining = remaining - own_sum
        segment = jnp.einsum(
            "ina,iab->inb", remaining, inverses[height], precision=lax.Precision.HIGHEST
        )
        results[height] = segment
        settled[height] = segment.astype(jnp.bfloat16)
    return (jnp.stack(solved), jnp.stack(results))


def solution(mesh):
    placed = (
        P(None, "row", None, None),
        P(None, "row", None, None),
        P(None, "row", "col", None, None),
        P(None, "row", "col"),
    )
    return jax.shard_map(
        shards,
        mesh=mesh,
        in_specs=placed,
        out_specs=(P(None, "row", None, None), P(None, "row", None, None)),
        check_vma=False,
    )
```

profile of v0, /device:TPU:0, one launch (start us, length us, event | category | flops | bytes accessed | tf_op | source)
XLA Modules:
  0.0 446.8 jit_solution(956539431709333284)
XLA Ops:
  0.7 1.7 compare_reduce_fusion
  2.3 1.1 bitcast_dynamic-update-slice_fusion.10
  3.5 32.3 %all-gather = bf16[512,128]{1,0:T(8,128)(2,1)S(1)} all-gather(bf16[64,128]{1,0:T(8,128)(2,1)S(1)} %convert_element_type.125), channel_id=2, replica_groups=mesh['row'=8,'col'=4] {'row'}, dimensions={0}, use_global_device_ids=true | all-gather | bytes 147456 | tf_op jit(solution)/shard_map/all_gather | solution.py:47
  36.8 10.1 %psum.105 = bf16[1,64,128]{2,1,0:T(8,128)(2,1)S(1)} all-reduce(bf16[1,64,128]{2,1,0:T(8,128)(2,1)S(1)} %fusion.24), channel_id=1, replica_groups=mesh['row'=8,'col'=4] {'col'}, use_global_device_ids=true, to_apply=%region_0.1 | all-reduce | flops 8192 | bytes 32768 | tf_op jit(solution)/shard_map/psum | solution.py:40
  47.0 1.1 bitcast_dynamic-update-slice_fusion.9
  48.1 1.0 convolution_bitcast_fusion.15
  49.8 30.7 %all-gather.1 = bf16[512,128]{1,0:T(8,128)(2,1)S(1)} all-gather(bf16[64,128]{1,0:T(8,128)(2,1)S(1)} %convert_element_type.130), channel_id=3, replica_groups=mesh['row'=8,'col'=4] {'row'}, dimensions={0}, use_global_device_ids=true | all-gather | bytes 147456 | tf_op jit(solution)/shard_map/all_gather | solution.py:47
  80.7 10.1 %psum.106 = bf16[1,64,128]{2,1,0:T(8,128)(2,1)S(1)} all-reduce(bf16[1,64,128]{2,1,0:T(8,128)(2,1)S(1)} %fusion.23), channel_id=1, replica_groups=mesh['row'=8,'col'=4] {'col'}, use_global_device_ids=true, to_apply=%region_1.2 | all-reduce | flops 8192 | bytes 32768 | tf_op jit(solution)/shard_map/psum | solution.py:40
  92.2 30.5 %all-gather.2 = bf16[512,128]{1,0:T(8,128)(2,1)S(1)} all-gather(bf16[64,128]{1,0:T(8,128)(2,1)S(1)} %convert_element_type.135), channel_id=4, replica_groups=mesh['row'=8,'col'=4] {'row'}, dimensions={0}, use_global_device_ids=true | all-gather | bytes 147456 | tf_op jit(solution)/shard_map/all_gather | solution.py:47
  123.0 10.1 %psum.107 = bf16[1,64,128]{2,1,0:T(8,128)(2,1)S(1)} all-reduce(bf16[1,64,128]{2,1,0:T(8,128)(2,1)S(1)} %fusion.22), channel_id=1, replica_groups=mesh['row'=8,'col'=4] {'col'}, use_global_device_ids=true, to_apply=%region_2.3 | all-reduce | flops 8192 | bytes 32768 | tf_op jit(solution)/shard_map/psum | solution.py:40
  133.8 30.5 %all-gather.3 = bf16[512,128]{1,0:T(8,128)(2,1)S(1)} all-gather(bf16[64,128]{1,0:T(8,128)(2,1)S(1)} %convert_element_type.140), channel_id=5, replica_groups=mesh['row'=8,'col'=4] {'row'}, dimensions={0}, use_global_device_ids=true | all-gather | bytes 147456 | tf_op jit(solution)/shard_map/all_gather | solution.py:47
  164.8 10.1 %psum.108 = bf16[1,64,128]{2,1,0:T(8,128)(2,1)S(1)} all-reduce(bf16[1,64,128]{2,1,0:T(8,128)(2,1)S(1)} %fusion.21), channel_id=1, replica_groups=mesh['row'=8,'col'=4] {'col'}, use_global_device_ids=true, to_apply=%region_3.4 | all-reduce | flops 8192 | bytes 32768 | tf_op jit(solution)/shard_map/psum | solution.py:40
  175.2 30.5 %all-gather.4 = bf16[512,128]{1,0:T(8,128)(2,1)S(1)} all-gather(bf16[64,128]{1,0:T(8,128)(2,1)S(1)} %convert_element_type.145), channel_id=6, replica_groups=mesh['row'=8,'col'=4] {'row'}, dimensions={0}, use_global_device_ids=true | all-gather | bytes 147456 | tf_op jit(solution)/shard_map/all_gather | solution.py:47
  205.9 10.1 %psum.109 = bf16[1,64,128]{2,1,0:T(8,128)(2,1)S(1)} all-reduce(bf16[1,64,128]{2,1,0:T(8,128)(2,1)S(1)} %fusion.20), channel_id=1, replica_groups=mesh['row'=8,'col'=4] {'col'}, use_global_device_ids=true, to_apply=%region_4.5 | all-reduce | flops 8192 | bytes 32768 | tf_op jit(solution)/shard_map/psum | solution.py:40
  216.7 37.5 %psum.110 = bf16[2,64,128]{2,1,0:T(8,128)(2,1)S(1)} all-reduce(f32[2,64,128]{2,1,0:T(8,128)S(1)} %convolution_bitcast_fusion), channel_id=1, replica_groups=mesh['row'=8,'col'=4] {'row'}, use_global_device_ids=true, to_apply=%region_5.6 | all-reduce | flops 16384 | bytes 98304 | tf_op jit(solution)/shard_map/psum | solution.py:64
  254.2 10.1 %psum.111 = bf16[1,64,128]{2,1,0:T(8,128)(2,1)S(1)} all-reduce(bf16[1,64,128]{2,1,0:T(8,128)(2,1)S(1)} %fusion.221), channel_id=1, replica_groups=mesh['row'=8,'col'=4] {'col'}, use_global_device_ids=true, to_apply=%region_6.7 | all-reduce | flops 8192 | bytes 32768 | tf_op jit(solution)/shard_map/psum | solution.py:9
  264.9 33.4 %psum.112 = bf16[2,64,128]{2,1,0:T(8,128)(2,1)S(1)} all-reduce(f32[2,64,128]{2,1,0:T(8,128)S(1)} %fusion.3), channel_id=1, replica_groups=mesh['row'=8,'col'=4] {'row'}, use_global_device_ids=true, to_apply=%region_7.8 | all-reduce | flops 16384 | bytes 98304 | tf_op jit(solution)/shard_map/psum | solution.py:64
  298.3 10.1 %psum.113 = bf16[1,64,128]{2,1,0:T(8,128)(2,1)S(1)} all-reduce(bf16[1,64,128]{2,1,0:T(8,128)(2,1)S(1)} %fusion.222), channel_id=1, replica_groups=mesh['row'=8,'col'=4] {'col'}, use_global_device_ids=true, to_apply=%region_8.9 | all-reduce | flops 8192 | bytes 32768 | tf_op jit(solution)/shard_map/psum | solution.py:9
  309.2 35.3 %psum.114 = bf16[2,64,128]{2,1,0:T(8,128)(2,1)S(1)} all-reduce(f32[2,64,128]{2,1,0:T(8,128)S(1)} %fusion.2), channel_id=1, replica_groups=mesh['row'=8,'col'=4] {'row'}, use_global_device_ids=true, to_apply=%region_9.10 | all-reduce | flops 16384 | bytes 98304 | tf_op jit(solution)/shard_map/psum | solution.py:64
  344.6 10.1 %psum.115 = bf16[1,64,128]{2,1,0:T(8,128)(2,1)S(1)} all-reduce(bf16[1,64,128]{2,1,0:T(8,128)(2,1)S(1)} %fusion.223), channel_id=1, replica_groups=mesh['row'=8,'col'=4] {'col'}, use_global_device_ids=true, to_apply=%region_10.11 | all-reduce | flops 8192 | bytes 32768 | tf_op jit(solution)/shard_map/psum | solution.py:9
  355.7 33.4 %psum.116 = bf16[2,64,128]{2,1,0:T(8,128)(2,1)S(1)} all-reduce(f32[2,64,128]{2,1,0:T(8,128)S(1)} %fusion.1), channel_id=1, replica_groups=mesh['row'=8,'col'=4] {'row'}, use_global_device_ids=true, to_apply=%region_11.12 | all-reduce | flops 16384 | bytes 98304 | tf_op jit(solution)/shard_map/psum | solution.py:64
  389.1 10.1 %psum.117 = bf16[1,64,128]{2,1,0:T(8,128)(2,1)S(1)} all-reduce(bf16[1,64,128]{2,1,0:T(8,128)(2,1)S(1)} %fusion.224), channel_id=1, replica_groups=mesh['row'=8,'col'=4] {'col'}, use_global_device_ids=true, to_apply=%region_12.13 | all-reduce | flops 8192 | bytes 32768 | tf_op jit(solution)/shard_map/psum | solution.py:9
  400.4 35.3 %psum.118 = bf16[2,64,128]{2,1,0:T(8,128)(2,1)S(1)} all-reduce(f32[2,64,128]{2,1,0:T(8,128)S(1)} %fusion), channel_id=1, replica_groups=mesh['row'=8,'col'=4] {'row'}, use_global_device_ids=true, to_apply=%region_13.14 | all-reduce | flops 16384 | bytes 98304 | tf_op jit(solution)/shard_map/psum | solution.py:64
  435.8 10.1 %psum.119 = bf16[1,64,128]{2,1,0:T(8,128)(2,1)S(1)} all-reduce(bf16[1,64,128]{2,1,0:T(8,128)(2,1)S(1)} %fusion.225), channel_id=1, replica_groups=mesh['row'=8,'col'=4] {'col'}, use_global_device_ids=true, to_apply=%region_14.15 | all-reduce | flops 8192 | bytes 32768 | tf_op jit(solution)/shard_map/psum | solution.py:9
  (64 shorter events, 10.2 us)
Async XLA Ops:
  0.6 48.5 %copy-start = (bf16[15,1,2,128,128]{4,3,2,1,0:T(8,128)(2,1)S(1)}, bf16[15,1,2,128,128]{4,3,2,1,0:T(8,128)(2,1)}, u32[]{:S(2)}) copy-start(bf16[15,1,2,128,128]{4,3,2,1,0:T(8,128)(2,1)} %param.6) | copy-start | bytes 2949124
  49.8 41.7 %copy-start.1 = (f32[6,1,128,128]{3,2,1,0:T(8,128)S(1)}, f32[6,1,128,128]{3,2,1,0:T(8,128)}, u32[]{:S(2)}) copy-start(f32[6,1,128,128]{3,2,1,0:T(8,128)} %param.5) | copy-start | bytes 1179652
  91.0 1.0 copy-start.2
  216.3 37.9 %copy-start.3 = (f32[6,1,64,128]{3,2,1,0:T(8,128)}, f32[6,1,64,128]{3,2,1,0:T(8,128)S(1)}, u32[]{:S(2)}) copy-start(f32[6,1,64,128]{3,2,1,0:T(8,128)S(1)} %get-tuple-element.27) | copy-start | bytes 589828
  446.1 0.7 copy-start.4
where the time goes:
time: 448 us; the launch traced here: 447 us
  blocking collectives  431 us (96%)
  matrix products  12.2 us (3%)
    psum x5, blocking collectives, shards(): summed = lax.psum(partial_value, 'row')  175 us
    all_gather x5, blocking collectives, shards(): lax.all_gather(segment.astype(jnp.bfloat16), 'row', axis=0, tiled=True)  155 us
    psum x5, blocking collectives, shards(): lax.psum(partial_value.astype(jnp.bfloat16), 'col').astype(jnp.float32)  50.7 us
    psum x5, blocking collectives, spread(): return lax.psum(block, axis)  50.6 us

commit v1 on v0

v1 whole, which is shorter than its diff:
```python
import functools
import math
import jax
import jax.numpy as jnp
from jax import lax
from jax.experimental import pallas as pl
from jax.experimental.pallas import tpu as pltpu
from jax.sharding import PartitionSpec as P

FINE = lax.Precision.HIGHEST
MERGE_BYTES = 24 << 20
f32, bf16 = jnp.float32, jnp.bfloat16


def pair_number(higher, lower_level):
    return higher * (higher - 1) // 2 + lower_level


def times_transposed(v, g, precision=None):
    return lax.dot_general(
        v, g, (((1,), (1,)), ((), ())), precision=precision, preferred_element_type=f32
    )


def times(v, g, precision=None):
    return lax.dot_general(
        v, g, (((1,), (0,)), ((), ())), precision=precision, preferred_element_type=f32
    )


def split_product(d, g):
    high = d.astype(bf16)
    low = (d - high.astype(f32)).astype(bf16)
    return times(high, g) + times(low, g)


def kernel_call(body, ins, outs):
    in_keys, out_keys = list(ins), list(outs)
    arrays, specs, held = [], [], 0
    for value in ins.values():
        array, at = value if isinstance(value, tuple) else (value, -1)
        if array.dtype == jnp.int32:
            specs.append(pl.BlockSpec(memory_space=pltpu.SMEM))
        elif at is None:
            specs.append(pl.BlockSpec(memory_space=pl.ANY))
        else:
            shape = array.shape
            if at >= 0:
                shape = (1,) + shape[1:]
                array = pltpu.with_memory_space_constraint(array, pltpu.HBM)
            index = (max(at, 0),) + (0,) * (len(shape) - 1)
            specs.append(pl.BlockSpec(shape, lambda *_, index=index: index))
            held += math.prod(shape) * array.dtype.itemsize
        arrays.append(array)
    shapes = list(outs.values())
    if len(shapes) == 1:
        shapes.append(((8, 128), f32))
    held += sum(math.prod(s) * jnp.dtype(d).itemsize for s, d in shapes)

    def kernel(*refs):
        body(dict(zip(in_keys + out_keys, refs)))
        if len(out_keys) == 1:
            refs[-1][...] = jnp.zeros(refs[-1].shape, f32)

    values = pl.pallas_call(
        kernel,
        grid=(1,),
        out_shape=[pltpu.HBM(s, d) for s, d in shapes],
        in_specs=specs,
        out_specs=[pl.BlockSpec(s, lambda *_, d=len(s): (0,) * d) for s, d in shapes],
        compiler_params=pltpu.CompilerParams(vmem_limit_bytes=2 * held + (3 << 20)),
    )(*arrays)
    return dict(zip(out_keys, values))


def exchange(value, step, size):
    return lax.ppermute(value, "col", [(c, c ^ step) for c in range(size)])


def shards(rows, cols, right_side, inverses, factor_blocks, pattern):
    return body_of(rows, cols, right_side, inverses, factor_blocks, pattern)


def body_of(rows, cols, right_side, inverses, factor_blocks, pattern):
    levels, _, rhs, depth = right_side.shape
    width = factor_blocks.shape[2]
    chunk = rhs // cols
    top = levels - 1
    col = lax.axis_index("col").reshape(1).astype(jnp.int32)
    row = lax.axis_index("row").reshape(1).astype(jnp.int32)
    panel, sent = (chunk, depth), (rows, chunk, depth)
    block = depth * depth * factor_blocks.dtype.itemsize
    sizes = factor_blocks.shape[0] * cols * width * block + 6 * rows * width * block
    merging = sizes <= MERGE_BYTES and levels % 2 == 0 and rows & (rows - 1) == 0
    merged = range(0, top - 1, 2) if merging else ()
    steps = [1 << s for s in reversed(range((cols - 1).bit_length()))]

    COL, ROW, PATTERN, BLOCKS, WAIT, PRE, ARRIVED, CARRY, SEND, OUT, ALL = range(11)
    INV, RIGHT, PANEL, X, Y, V, RAW, FAR = range(11, 19)

    def inv(*ms):
        return {(INV, m): (inverses, m) for m in ms}

    def right(m):
        return {(RIGHT, m): (right_side, m)}

    def own(r, m):
        return r[RIGHT, m][0, 0, pl.ds(pl.multiple_of(r[COL][0] * chunk, chunk), chunk), :]

    def swap(value):
        return lax.all_to_all(value, "row", 0, 0)

    def send_all(r, value):
        for k in range(rows):
            r[SEND][k] = value

    cuts = [(1, 2), (2, 4), (4, levels)]
    bundles = {n: [(m, l) for m in range(*cut) for l in range(m)] for n, cut in zip("abc", cuts)}
    place = {pair: (n, s) for n, pairs in bundles.items() for s, pair in enumerate(pairs)}
    held, arrays = {}, {}

    def shape_of(pairs):
        return (len(pairs), width, depth, depth), bf16

    def add_bundle(name):
        found = {0: held[name]}
        for step in steps:
            found |= {q ^ step: exchange(v, step, cols) for q, v in found.items()}
        for q, v in found.items():
            arrays[name, q] = v

    def need(*keys):
        found = {}
        for n, s in sorted({place[k] for k in keys}):
            for q in range(cols):
                v = arrays[n, q]
                found[n, s, q] = v if v.shape[0] == 1 else (v, s)
        return found

    def groups(r, key):
        name, s = place[key]
        return [r[name, s, q].at[0] for q in range(cols)]

    def column(r, q, j):
        return (r[COL][0] ^ q) * width + j

    def sum_over(r, m, lower):
        total = None
        for l in lower:
            for q, blocks in enumerate(groups(r, (m, l))):
                for j in range(width):
                    term = times_transposed(r[PANEL, l][column(r, q, j)], blocks[j])
                    total = term if total is None else total + term
        return total

    def spread_sums(r, terms, out_ref, slot, carried=None):
        for q in range(cols):
            for j in range(width):
                k = column(r, q, j)
                total = None if carried is None else carried[k, slot]
                for value, key in terms:
                    term = times(value, groups(r, key)[q][j])
                    total = term if total is None else total + term
                out_ref[k, slot] = total.astype(out_ref.dtype)

    def masked(r, p, at, j):
        value = r[BLOCKS][at, 0, j]
        return jnp.where(r[PATTERN][p, 0, j] != 0, value, jnp.zeros_like(value))

    def first_body(r):
        value = times_transposed(own(r, 0), r[INV, 0][0, 0], FINE)
        r[X][...] = value
        send_all(r, value.astype(bf16))
        for j in range(width):
            r[OUT][0, j] = masked(r, 0, 0, j)

    out = kernel_call(
        first_body,
        {COL: col, PATTERN: pattern, BLOCKS: (factor_blocks, 0), **right(0), **inv(0)},
        {X: (panel, f32), SEND: (sent, bf16), OUT: shape_of("a")},
    )
    x = {0: out[X]}
    held["a"] = out[OUT]

    def mask_body(r):
        for name, pairs in bundles.items():
            for s, (m, l) in enumerate(pairs):
                for j in range(width):
                    value = masked(r, pair_number(m, l), pair_number(m, l), j)
                    if name in r:
                        r[name][s, j] = value
                    if l in merged and m == l + 1:
                        product = split_product(r[INV, m][0, 0], value)
                        r[OUT][l // 2, :, j * depth : (j + 1) * depth] = product.astype(bf16)

    outs = {n: shape_of(pairs) for n, pairs in bundles.items() if n != "a"}
    if merged:
        outs[OUT] = ((len(merged), depth, width * depth), bf16)
    found = kernel_call(
        mask_body,
        {PATTERN: pattern, BLOCKS: factor_blocks, WAIT: (out[SEND], None), **inv(*[l + 1 for l in merged])}, outs,
    )
    product = found.pop(OUT, None)
    held |= found
    for name in bundles:
        add_bundle(name)

    products = {0: product}
    if merged:
        for d in [1 << s for s in reversed(range((rows - 1).bit_length()))]:
            products |= {s ^ d: lax.ppermute(v, "row", [(r, r ^ d) for r in range(rows)]) for s, v in products.items()}

    gathered = {0: swap(out[SEND])}
    y, rounded = {}, {}

    def panels(lower):
        return {(PANEL, l): gathered[l] for l in lower}

    for m in range(1, levels):
        def pre_body(r):
            r[PRE][...] = own(r, m) - sum_over(r, m, range(m - 1))

        pre = right(m)
        if m > 1:
            pre = kernel_call(
                pre_body,
                {COL: col, **pre, **panels(range(m - 1)), **need(*[(m, l) for l in range(m - 1)])},
                {PRE: (panel, f32)},
            )

        def solve_body(r):
            rest = r[PRE][...] if PRE in r else own(r, m)
            value = times_transposed(rest - sum_over(r, m, [m - 1]), r[INV, m][0, 0], FINE)
            r[X][...] = value
            if m < top:
                send_all(r, value.astype(bf16))
                return
            result = times(value, r[INV, m][0, 0], FINE)
            r[Y][...] = result
            r[V][...] = result.astype(bf16)
            spread_sums(r, [(result.astype(bf16), (m, m - 1))], r[SEND], 0)

        outs = {X: (panel, f32), SEND: (sent, bf16)}
        if m == top:
            outs = {X: (panel, f32), Y: (panel, f32), V: (panel, bf16), SEND: ((rows, 1, chunk, depth), bf16)}
        out = kernel_call(solve_body, {COL: col, **pre, **inv(m), **panels([m - 1]), **need((m, m - 1))}, outs)
        x[m] = out[X]
        if m < top:
            gathered[m] = swap(out[SEND])
    y[top], rounded[top] = out[Y], out[V]

    wanted = [(m, l) for l in merged for m in range(l + 2, levels)]
    if merged:
        def fix_body(r):
            for s in range(rows):
                r[ALL][r[ROW][0] ^ s] = r[FAR, s][...]
            for s, (m, l) in enumerate(wanted):
                total = None
                for q, blocks in enumerate(groups(r, (m, l + 1))):
                    for j in range(width):
                        term = times(blocks[j], r[ALL][column(r, q, j), l // 2])
                        total = term if total is None else total + term
                for j in range(width):
                    raw = r[RAW, m, l][0, j].astype(f32)
                    r[OUT][s, j] = (raw - total[:, j * depth : (j + 1) * depth]).astype(bf16)

        raws = {(RAW, m, l): (held[place[m, l][0]], place[m, l][1]) for m, l in wanted}
        held["d"] = kernel_call(
            fix_body,
            {COL: col, ROW: row, **{(FAR, s): v for s, v in products.items()}, **raws}
            | need(*[(m, l + 1) for m, l in wanted]),
            {OUT: shape_of(wanted), ALL: ((rows,) + product.shape, bf16)},
        )[OUT]
        add_bundle("d")
        for s, (m, l) in enumerate(wanted):
            place[m, l, True] = ("d", s)

    lower = [(l, l + 1) for l in reversed(merged)] if merged else [(l,) for l in range(top - 2, -1, -1)]
    plan = [(top - 1,)] + lower

    def terms_for(l, values):
        return [(v, (m, l, True) if (m, l) in wanted else (m, l)) for m, v in values.items()]

    def pairs_for(targets, upper):
        return need(*[key for l in targets for _, key in terms_for(l, dict.fromkeys(upper))])

    for s, done in enumerate(plan):
        targets = plan[s + 1] if s + 1 < len(plan) else ()
        upper = range(done[-1] + 1, levels)
        arrived = swap(out[SEND])
        slots = (rows, max(len(targets), 1), chunk, depth)
        ins = {COL: col, ARRIVED: arrived, **inv(*done), **{(X, m): x[m] for m in done}}
        if targets:
            odds = [l + 1 for l in targets if l in merged]

            def carry_body(r):
                values = {m: r[V, m][...] for m in upper}
                for slot, l in enumerate(targets):
                    terms = terms_for(l, values)
                    if l + 1 in odds:
                        own_part = times(r[X, l + 1][...], r[INV, l + 1][0, 0], FINE).astype(bf16)
                        terms.append((own_part, (l + 1, l)))
                    spread_sums(r, terms, r[CARRY], slot)

            carry = kernel_call(
                carry_body,
                {COL: col, **{(V, m): rounded[m] for m in upper}, **{(X, m): x[m] for m in odds}, **inv(*odds)}
                | pairs_for(targets, upper) | need(*[(m, m - 1) for m in odds]),
                {CARRY: (slots, f32)},
            )
            ins |= {**carry, **pairs_for(targets, done)}

        def step_body(r):
            values = {}
            for slot, m in enumerate(done):
                total = r[ARRIVED][0, slot].astype(f32)
                for k in range(1, rows):
                    total = total + r[ARRIVED][k, slot].astype(f32)
                result = times(r[X, m][...] - total, r[INV, m][0, 0], FINE)
                if not targets:
                    r[OUT][slot] = result
                    continue
                r[Y, m][...] = result
                values[m] = result.astype(bf16)
                r[V, m][...] = values[m]
            for slot, l in enumerate(targets):
                spread_sums(r, terms_for(l, values), r[SEND], slot, r[CARRY])

        if targets:
            outs = {(Y, m): (panel, f32) for m in done} | {(V, m): (panel, bf16) for m in done} | {SEND: (slots, bf16)}
        else:
            outs = {OUT: ((len(done),) + panel, f32)}
        out = kernel_call(step_body, ins, outs)
        if targets:
            for m in done:
                y[m], rounded[m] = out[Y, m], out[V, m]

    def pieces(value):
        return [value] + [exchange(value, q, cols) for q in range(1, cols)]

    def stacked(values):
        def stack_body(r):
            for s in range(len(values)):
                r[OUT][s] = r[X, s][...]

        return kernel_call(
            stack_body, {(X, s): v for s, v in enumerate(values)}, {OUT: ((len(values),) + panel, f32)}
        )[OUT]

    def joined(*runs):
        def join_body(r):
            at = 0
            for s, run in enumerate(runs):
                count = run[0].shape[0]
                for q in range(cols):
                    where = pl.ds(pl.multiple_of((r[COL][0] ^ q) * chunk, chunk), chunk)
                    r[OUT][pl.ds(at, count), where, :] = r[X, s, q][...]
                at += count

        ins = {(X, s, q): v for s, run in enumerate(runs) for q, v in enumerate(run)}
        return kernel_call(join_body, {COL: col, **ins}, {OUT: ((levels, rhs, depth), f32)})[OUT][:, None]

    high = pieces(stacked([y[m] for m in range(len(plan[-1]), levels)]))
    forward = joined(pieces(stacked([x[m] for m in range(levels)])))
    return forward, joined(pieces(out[OUT]), high)


def solution(mesh):
    rows, cols = mesh.shape["row"], mesh.shape["col"]
    placed = (
        P(None, "row", None, None),
        P(None, "row", None, None),
        P(None, "row", "col", None, None),
        P(None, "row", "col"),
    )
    return jax.shard_map(
        functools.partial(shards, rows, cols),
        mesh=mesh,
        in_specs=placed,
        out_specs=(P(None, "row", None, None), P(None, "row", None, None)),
        check_vma=False,
    )
```

time: 448 us -> 173 us (0.39)
  blocking collectives: 431 us -> 12 us
  waiting for transfers between devices: 0 us -> 58.4 us
  starting transfers between devices: 0 us -> 48.7 us
  Pallas kernels: 0 us -> 41.5 us
  matrix products: 12.2 us -> 0 us
  local copies, waits for them, and re-layouts: 1.22 us -> 9.04 us
    psum x15 -> x0, blocking collectives: 276 us -> none  [the longest x5 175 us: shards(): summed = lax.psum(partial_value, 'row')]
    all_gather x5 -> x0, blocking collectives: 155 us -> none  [shards(): lax.all_gather(segment.astype(jnp.bfloat16), 'row', axis=0, tiled=True)]
    pallas_call x0 -> x21, Pallas kernels: none -> 41.5 us  [kernel_call(): pl.pallas_call(kernel, grid=(1,), out_shape=[pltpu.HBM(s, d) for s, d in...]
    ppermute x0 -> x28, waiting for transfers between devices: none -> 31.6 us  [the longest x21 18.9 us: exchange(): return lax.ppermute(value, 'col', [(c, c ^ step) for c in range(size)])]
    all_to_all x0 -> x7, waiting for transfers between devices: none -> 26.8 us  [swap(): return lax.all_to_all(value, 'row', 0, 0)]
    ppermute x0 -> x28, starting transfers between devices: none -> 25.1 us  [the longest x21 12.5 us: exchange(): return lax.ppermute(value, 'col', [(c, c ^ step) for c in range(size)])]
    all_to_all x0 -> x7, starting transfers between devices: none -> 23.7 us  [swap(): return lax.all_to_all(value, 'row', 0, 0)]
    dot_general x42 -> x0, matrix products: 12.2 us -> none  [the longest x15 4.86 us: shards(): jnp.einsum('ikab,knb->ina', masked, gathered[earlier], preferred_element_...]
  transfers between devices with their start and end apart: 0 -> 35, of which waited for: 0 -> 16; matrix products, arithmetic and copies ran while one was open for 0% -> 0% of each run, Pallas kernels for 0% -> 17%
where the time goes in v1:
time: 173 us; the launch traced here: 171 us
  waiting for transfers between devices  58.4 us (34%)
  starting transfers between devices  48.7 us (28%)
  Pallas kernels  41.5 us (24%)
  blocking collectives  12 us (7%)
  local copies, waits for them, and re-layouts  9.04 us (5%)
    pallas_call x21, Pallas kernels, kernel_call(): pl.pallas_call(kernel, grid=(1,), out_shape=[pltpu.HBM(s, d) for s, d in...  41.5 us
    all_to_all x7, waiting for transfers between devices, swap(): return lax.all_to_all(value, 'row', 0, 0)  26.8 us
    all_to_all x7, starting transfers between devices, swap(): return lax.all_to_all(value, 'row', 0, 0)  23.7 us
    ppermute x21, waiting for transfers between devices, exchange(): return lax.ppermute(value, 'col', [(c, c ^ step) for c in range(size)])  18.9 us
    ppermute x7, waiting for transfers between devices, body_of(): lax.ppermute(v, 'row', [(r, r ^ d) for r in range(rows)])  12.7 us
    ppermute x21, starting transfers between devices, exchange(): return lax.ppermute(value, 'col', [(c, c ^ step) for c in range(size)])  12.5 us
    ppermute x7, starting transfers between devices, body_of(): lax.ppermute(v, 'row', [(r, r ^ d) for r in range(rows)])  12.5 us
    all_to_all x1, blocking collectives, swap(): return lax.all_to_all(value, 'row', 0, 0)  12 us
  transfers between devices with their start and end apart: 35, of which 16 were waited for; matrix products, arithmetic and copies ran while one was open for 0% of the time, Pallas kernels for 17%

profile of v1, /device:TPU:0, one launch (start us, length us, event | category | flops | bytes accessed | tf_op | source)
XLA Modules:
  0.0 170.6 jit_solution(7101120223382830917)
XLA Ops:
  6.1 3.0 %collective-permute-start.7 = (bf16[9,2,128,128]{3,2,1,0:T(8,128)(2,1)}, bf16[9,2,128,128]{3,2,1,0:T(8,128)(2,1)S(1)}, u32[]{:S(2)}, u32[]{:S(2)}) collective-permute-start(bf16[9,2,128,128]{3,2,1,0:T(8,128)(2,1)} %get-tuple-element.49.refs_5_.refs_9_.refs_13_.refs_4_.refs_6_.refs_10_.refs_14_.refs_18_.refs_1, ...), channel_id=1, source_target_pairs={{0,2},{1,3},{2,0},{3,1},{4,6},{5,7},{6,4},{7,5},{8,10},{9,11},{10,... | collective-permute-start | bytes 1769480 | tf_op jit(solution)/shard_map/ppermute | solution.py:77
  13.8 9.7 %collective-permute-done.7.refs_7_.refs_11_.refs_15_.refs_6_.refs_8_.refs_12_.refs_16_.refs_20_.refs_26_.refs_30_.refs_34_.refs_38_ = bf16[9,2,128,128]{3,2,1,0:T(8,128)(2,1)S(1)} collective-permute-done((bf16[9,2,128,128]{3,2,1,0:T(8,128)(2,1)}, bf16[9,2,128,128]{3,2,1,0:T(8,128)(2,1)S(1)}, u32[]{:S(2)}, u32[]{:S(2)}) %collective-permute-start.7) | collective-permute-done | bytes 589856 | tf_op jit(solution)/shard_map/ppermute | solution.py:77
  27.2 2.7 %collective-permute-done.15.refs_6_ = bf16[2,128,256]{2,1,0:T(8,128)(2,1)S(1)} collective-permute-done((bf16[2,128,256]{2,1,0:T(8,128)(2,1)}, bf16[2,128,256]{2,1,0:T(8,128)(2,1)S(1)}, u32[]{:S(2)}, u32[]{:S(2)}) %collective-permute-start.15) | collective-permute-done | bytes 131104 | tf_op jit(solution)/shard_map/ppermute | solution.py:211
  32.2 3.0 %collective-permute-done.16.refs_7_ = bf16[2,128,256]{2,1,0:T(8,128)(2,1)S(1)} collective-permute-done((bf16[2,128,256]{2,1,0:T(8,128)(2,1)S(1)}, bf16[2,128,256]{2,1,0:T(8,128)(2,1)S(1)}, u32[]{:S(2)}, u32[]{:S(2)}) %collective-permute-start.16) | collective-permute-done | bytes 131104 | tf_op jit(solution)/shard_map/ppermute | solution.py:211
  36.6 3.5 %collective-permute-done.17.refs_8_ = bf16[2,128,256]{2,1,0:T(8,128)(2,1)S(1)} collective-permute-done((bf16[2,128,256]{2,1,0:T(8,128)(2,1)S(1)}, bf16[2,128,256]{2,1,0:T(8,128)(2,1)S(1)}, u32[]{:S(2)}, u32[]{:S(2)}) %collective-permute-start.17) | collective-permute-done | bytes 131104 | tf_op jit(solution)/shard_map/ppermute | solution.py:211
  41.6 3.5 %collective-permute-done.18.refs_9_ = bf16[2,128,256]{2,1,0:T(8,128)(2,1)S(1)} collective-permute-done((bf16[2,128,256]{2,1,0:T(8,128)(2,1)S(1)}, bf16[2,128,256]{2,1,0:T(8,128)(2,1)S(1)}, u32[]{:S(2)}, u32[]{:S(2)}) %collective-permute-start.18) | collective-permute-done | bytes 131104 | tf_op jit(solution)/shard_map/ppermute | solution.py:211
  47.0 3.3 %shard_map.72 = (bf16[6,2,128,128]{3,2,1,0:T(8,128)(2,1)}, bf16[8,2,128,256]{3,2,1,0:T(8,128)(2,1)}) custom-call(s32[1]{0:T(128)} %bitcast.refs_0_, s32[1]{0:T(128)} %bitcast.3.refs_1_, bf16[2,128,256]{2,1,0:T(8,128)(2,1)S(1)} %copy-done.2, bf16[2,128,256]{2,1,0:T(8,128)(2,1)S(1)} %collective-permute-done.12.refs_3_, ...), custom_call_target="tpu_custom_call" | custom-call | tf_op jit(solution)/shard_map/pallas_call | solution.py:65
  52.5 6.6 %collective-permute-done.20.refs_10_.refs_11_.refs_15_.refs_19_.refs_17_.refs_21_ = bf16[6,2,128,128]{3,2,1,0:T(8,128)(2,1)S(1)} collective-permute-done((bf16[6,2,128,128]{3,2,1,0:T(8,128)(2,1)}, bf16[6,2,128,128]{3,2,1,0:T(8,128)(2,1)S(1)}, u32[]{:S(2)}, u32[]{:S(2)}) %collective-permute-start.20) | collective-permute-done | bytes 393248 | tf_op jit(solution)/shard_map/ppermute | solution.py:77
  59.7 12.0 %all_to_all.40.refs_3_.refs_2_ = bf16[8,16,128]{2,1,0:T(8,128)(2,1)S(1)} all-to-all(bf16[8,16,128]{2,1,0:T(8,128)(2,1)S(1)} %copy-done.4), channel_id=1, replica_groups=mesh['row'=8,'col'=4] {'row'}, dimensions={0} | all-to-all | bytes 65536 | tf_op jit(solution)/shard_map/all_to_all | solution.py:111
  73.9 3.3 %all-to-all-start.1 = ((bf16[8,16,128]{2,1,0:T(8,128)(2,1)}), bf16[8,16,128]{2,1,0:T(8,128)(2,1)S(1)}, u32[]{:S(2)}, u32[]{:S(2)}) async-start(bf16[8,16,128]{2,1,0:T(8,128)(2,1)} %get-tuple-element.44), calls=%async_computation.1 | async-start | bytes 65536 | tf_op jit(solution)/shard_map/all_to_all | solution.py:111
  79.1 4.8 %all-to-all-done.1.refs_3_ = bf16[8,16,128]{2,1,0:T(8,128)(2,1)S(1)} async-done(((bf16[8,16,128]{2,1,0:T(8,128)(2,1)}), bf16[8,16,128]{2,1,0:T(8,128)(2,1)S(1)}, u32[]{:S(2)}, u32[]{:S(2)}) %all-to-all-start.1) | async-done | bytes 32800 | tf_op jit(solution)/shard_map/all_to_all | solution.py:111
  86.8 3.3 %all-to-all-start.2 = ((bf16[8,16,128]{2,1,0:T(8,128)(2,1)}), bf16[8,16,128]{2,1,0:T(8,128)(2,1)S(1)}, u32[]{:S(2)}, u32[]{:S(2)}) async-start(bf16[8,16,128]{2,1,0:T(8,128)(2,1)} %get-tuple-element.47), calls=%async_computation.2 | async-start | bytes 65536 | tf_op jit(solution)/shard_map/all_to_all | solution.py:111
  92.2 4.5 %all-to-all-done.2.refs_3_.refs_4_ = bf16[8,16,128]{2,1,0:T(8,128)(2,1)S(1)} async-done(((bf16[8,16,128]{2,1,0:T(8,128)(2,1)}), bf16[8,16,128]{2,1,0:T(8,128)(2,1)S(1)}, u32[]{:S(2)}, u32[]{:S(2)}) %all-to-all-start.2) | async-done | bytes 32800 | tf_op jit(solution)/shard_map/all_to_all | solution.py:111
  99.7 3.3 %all-to-all-start.3 = ((bf16[8,16,128]{2,1,0:T(8,128)(2,1)}), bf16[8,16,128]{2,1,0:T(8,128)(2,1)S(1)}, u32[]{:S(2)}, u32[]{:S(2)}) async-start(bf16[8,16,128]{2,1,0:T(8,128)(2,1)} %get-tuple-element.51), calls=%async_computation.3 | async-start | bytes 65536 | tf_op jit(solution)/shard_map/all_to_all | solution.py:111
  105.4 4.3 %all-to-all-done.3.refs_3_.refs_5_ = bf16[8,16,128]{2,1,0:T(8,128)(2,1)S(1)} async-done(((bf16[8,16,128]{2,1,0:T(8,128)(2,1)}), bf16[8,16,128]{2,1,0:T(8,128)(2,1)S(1)}, u32[]{:S(2)}, u32[]{:S(2)}) %all-to-all-start.3) | async-done | bytes 32800 | tf_op jit(solution)/shard_map/all_to_all | solution.py:111
  112.6 3.3 %all-to-all-start.4 = ((bf16[8,16,128]{2,1,0:T(8,128)(2,1)}), bf16[8,16,128]{2,1,0:T(8,128)(2,1)S(1)}, u32[]{:S(2)}, u32[]{:S(2)}) async-start(bf16[8,16,128]{2,1,0:T(8,128)(2,1)} %get-tuple-element.54), calls=%async_computation.4 | async-start | bytes 65536 | tf_op jit(solution)/shard_map/all_to_all | solution.py:111
  118.5 4.1 %all-to-all-done.4.refs_3_ = bf16[8,16,128]{2,1,0:T(8,128)(2,1)S(1)} async-done(((bf16[8,16,128]{2,1,0:T(8,128)(2,1)}), bf16[8,16,128]{2,1,0:T(8,128)(2,1)S(1)}, u32[]{:S(2)}, u32[]{:S(2)}) %all-to-all-start.4) | async-done | bytes 32800 | tf_op jit(solution)/shard_map/all_to_all | solution.py:111
  123.3 2.6 %shard_map.69 = (f32[16,128]{1,0:T(8,128)}, f32[16,128]{1,0:T(8,128)}, bf16[16,128]{1,0:T(8,128)(2,1)}, bf16[8,1,16,128]{3,2,1,0:T(8,128)(2,1)}) custom-call(s32[1]{0:T(128)} %bitcast.refs_0_, f32[16,128]{1,0:T(8,128)S(1)} %copy-done.16, f32[6,1,128,128]{3,2,1,0:T(8,128)} %refs_3_.9, bf16[8,16,128]{2,1,0:T(8,128)(2,1)S(1)} %all-to-all-done.4.refs_3_, ...), custom_call_target="tpu_custom_call" | custom-call | tf_op jit(solution)/shard_map/pallas_call | solution.py:65
  125.9 3.5 %all-to-all-start.5 = ((bf16[8,1,16,128]{3,2,1,0:T(8,128)(2,1)}), bf16[8,1,16,128]{3,2,1,0:T(8,128)(2,1)S(1)}, u32[]{:S(2)}, u32[]{:S(2)}) async-start(bf16[8,1,16,128]{3,2,1,0:T(8,128)(2,1)} %get-tuple-element.58), calls=%async_computation.5 | async-start | bytes 65536 | tf_op jit(solution)/shard_map/all_to_all | solution.py:111
  132.7 3.3 %all-to-all-done.5.refs_1_ = bf16[8,1,16,128]{3,2,1,0:T(8,128)(2,1)S(1)} async-done(((bf16[8,1,16,128]{3,2,1,0:T(8,128)(2,1)}), bf16[8,1,16,128]{3,2,1,0:T(8,128)(2,1)S(1)}, u32[]{:S(2)}, u32[]{:S(2)}) %all-to-all-start.5) | async-done | bytes 32800 | tf_op jit(solution)/shard_map/all_to_all | solution.py:111
  139.2 3.5 %all-to-all-start.6 = ((bf16[8,2,16,128]{3,2,1,0:T(8,128)(2,1)}), bf16[8,2,16,128]{3,2,1,0:T(8,128)(2,1)S(1)}, u32[]{:S(2)}, u32[]{:S(2)}) async-start(bf16[8,2,16,128]{3,2,1,0:T(8,128)(2,1)} %get-tuple-element.63), calls=%async_computation.6 | async-start | bytes 131072 | tf_op jit(solution)/shard_map/all_to_all | solution.py:111
  142.7 2.6 %shard_map.75 = (f32[8,2,16,128]{3,2,1,0:T(8,128)}, f32[8,128]{1,0:T(8,128)}) custom-call(s32[1]{0:T(128)} %bitcast.refs_0_, bf16[16,128]{1,0:T(8,128)(2,1)S(1)} %copy-done.25, bf16[16,128]{1,0:T(8,128)(2,1)S(1)} %copy-done.14, f32[16,128]{1,0:T(8,128)S(1)} %copy-done.8, f32[6,1,128,128]{3,2,1,0:T(8,128)} %refs_3_.9, ...), custom_call_target="tpu_custom_call" | custom-call | tf_op jit(solution)/shard_map/pallas_call | solution.py:65
  145.3 4.2 %all-to-all-done.6.refs_1_ = bf16[8,2,16,128]{3,2,1,0:T(8,128)(2,1)S(1)} async-done(((bf16[8,2,16,128]{3,2,1,0:T(8,128)(2,1)}), bf16[8,2,16,128]{3,2,1,0:T(8,128)(2,1)S(1)}, u32[]{:S(2)}, u32[]{:S(2)}) %all-to-all-start.6) | async-done | bytes 65568 | tf_op jit(solution)/shard_map/all_to_all | solution.py:111
  152.9 3.4 %all-to-all-start.7 = ((bf16[8,2,16,128]{3,2,1,0:T(8,128)(2,1)}), bf16[8,2,16,128]{3,2,1,0:T(8,128)(2,1)S(1)}, u32[]{:S(2)}, u32[]{:S(2)}) async-start(bf16[8,2,16,128]{3,2,1,0:T(8,128)(2,1)} %get-tuple-element.66), calls=%async_computation.7 | async-start | bytes 131072 | tf_op jit(solution)/shard_map/all_to_all | solution.py:111
  (137 shorter events, 68.2 us)
Async XLA Ops:
  6.1 17.4 %collective-permute-start.7 = (bf16[9,2,128,128]{3,2,1,0:T(8,128)(2,1)}, bf16[9,2,128,128]{3,2,1,0:T(8,128)(2,1)S(1)}, u32[]{:S(2)}, u32[]{:S(2)}) collective-permute-start(bf16[9,2,128,128]{3,2,1,0:T(8,128)(2,1)} %get-tuple-element.49.refs_5_.refs_9_.refs_13_.refs_4_.refs_6_.refs_10_.refs_14_.refs_18_.refs_1, ...), channel_id=1, source_target_pairs={{0,2},{1,3},{2,0},{3,1},{4,6},{5,7},{6,4},{7,5},{8,10},{9,11},{10,... | collective-permute-start | bytes 1769480 | tf_op jit(solution)/shard_map/ppermute | solution.py:77
  9.1 14.4 %collective-permute-start.12 = (bf16[2,128,256]{2,1,0:T(8,128)(2,1)}, bf16[2,128,256]{2,1,0:T(8,128)(2,1)S(1)}, u32[]{:S(2)}, u32[]{:S(2)}) collective-permute-start(bf16[2,128,256]{2,1,0:T(8,128)(2,1)} %get-tuple-element.60.refs_2_), channel_id=1, source_target_pairs={{0,16},{4,20},{8,24},{12,28},{16,0},{20,4},{24,8},{28,12},{1,17},{... | collective-permute-start | bytes 393224 | tf_op jit(solution)/shard_map/ppermute | solution.py:211
  11.7 19.9 %collective-permute-start.4 = (bf16[5,2,128,128]{3,2,1,0:T(8,128)(2,1)}, bf16[5,2,128,128]{3,2,1,0:T(8,128)(2,1)S(1)}, u32[]{:S(2)}, u32[]{:S(2)}) collective-permute-start(bf16[5,2,128,128]{3,2,1,0:T(8,128)(2,1)} %get-tuple-element.42.refs_3_.refs_4_.refs_8_.refs_10_.refs_11_.refs_16_.refs_20_.refs_12_.refs_7_), channel_id=1, source_target_pairs={{0,2},{1,3},{2,0},{3,1},{4,6},{5,7},{6,4},{7,5},{8,10},{9,11},{10,... | collective-permute-start | bytes 983048 | tf_op jit(solution)/shard_map/ppermute | solution.py:77
  12.2 13.4 %collective-permute-start.13 = (bf16[2,128,256]{2,1,0:T(8,128)(2,1)}, bf16[2,128,256]{2,1,0:T(8,128)(2,1)S(1)}, u32[]{:S(2)}, u32[]{:S(2)}) collective-permute-start(bf16[2,128,256]{2,1,0:T(8,128)(2,1)} %get-tuple-element.60.refs_2_), channel_id=1, source_target_pairs={{0,8},{4,12},{8,0},{12,4},{16,24},{20,28},{24,16},{28,20},{1,9},{5... | collective-permute-start | bytes 393224 | tf_op jit(solution)/shard_map/ppermute | solution.py:211
  13.8 31.3 %collective-permute-start.6 = (bf16[9,2,128,128]{3,2,1,0:T(8,128)(2,1)}, bf16[9,2,128,128]{3,2,1,0:T(8,128)(2,1)S(1)}, u32[]{:S(2)}, u32[]{:S(2)}) collective-permute-start(bf16[9,2,128,128]{3,2,1,0:T(8,128)(2,1)} %get-tuple-element.49.refs_5_.refs_9_.refs_13_.refs_4_.refs_6_.refs_10_.refs_14_.refs_18_.refs_1, ...), channel_id=1, source_target_pairs={{0,1},{1,0},{2,3},{3,2},{4,5},{5,4},{6,7},{7,6},{8,9},{9,8},{10,11... | collective-permute-start | bytes 1769480 | tf_op jit(solution)/shard_map/ppermute | solution.py:77
  23.5 21.6 %collective-permute-start.8 = (bf16[9,2,128,128]{3,2,1,0:T(8,128)(2,1)S(1)}, bf16[9,2,128,128]{3,2,1,0:T(8,128)(2,1)S(1)}, u32[]{:S(2)}, u32[]{:S(2)}) collective-permute-start(bf16[9,2,128,128]{3,2,1,0:T(8,128)(2,1)S(1)} %collective-permute-done.7.refs_7_.refs_11_.refs_15_.refs_6_.refs_8_.refs_12_.refs_16_.r, ...), channel_id=1, source_target_pairs={{0,1},{1,0},{2,3},{3,2},{4,5},{5,4},{6,7},{7,6},{8,9},{9,8},{10,11... | collective-permute-start | bytes 1769480 | tf_op jit(solution)/shard_map/ppermute | solution.py:77
  31.7 10.0 %collective-permute-start.3 = (bf16[5,2,128,128]{3,2,1,0:T(8,128)(2,1)}, bf16[5,2,128,128]{3,2,1,0:T(8,128)(2,1)S(1)}, u32[]{:S(2)}, u32[]{:S(2)}) collective-permute-start(bf16[5,2,128,128]{3,2,1,0:T(8,128)(2,1)} %get-tuple-element.42.refs_3_.refs_4_.refs_8_.refs_10_.refs_11_.refs_16_.refs_20_.refs_12_.refs_7_), channel_id=1, source_target_pairs={{0,1},{1,0},{2,3},{3,2},{4,5},{5,4},{6,7},{7,6},{8,9},{9,8},{10,11... | collective-permute-start | bytes 983048 | tf_op jit(solution)/shard_map/ppermute | solution.py:77
  31.7 13.4 %collective-permute-start.5 = (bf16[5,2,128,128]{3,2,1,0:T(8,128)(2,1)S(1)}, bf16[5,2,128,128]{3,2,1,0:T(8,128)(2,1)}, u32[]{:S(2)}, u32[]{:S(2)}) collective-permute-start(bf16[5,2,128,128]{3,2,1,0:T(8,128)(2,1)S(1)} %collective-permute-done.4.refs_5_.refs_6_.refs_10_.refs_18_.refs_22_.refs_14_.refs_9_.refs_13_), channel_id=1, source_target_pairs={{0,1},{1,0},{2,3},{3,2},{4,5},{5,4},{6,7},{7,6},{8,9},{9,8},{10,11... | collective-permute-start | bytes 983048 | tf_op jit(solution)/shard_map/ppermute | solution.py:77
  50.4 8.7 %collective-permute-start.20 = (bf16[6,2,128,128]{3,2,1,0:T(8,128)(2,1)}, bf16[6,2,128,128]{3,2,1,0:T(8,128)(2,1)S(1)}, u32[]{:S(2)}, u32[]{:S(2)}) collective-permute-start(bf16[6,2,128,128]{3,2,1,0:T(8,128)(2,1)} %get-tuple-element.61.refs_8_.refs_9_.refs_13_.refs_17_.refs_15_.refs_19_), channel_id=1, source_target_pairs={{0,2},{1,3},{2,0},{3,1},{4,6},{5,7},{6,4},{7,5},{8,10},{9,11},{10,... | collective-permute-start | bytes 1179656 | tf_op jit(solution)/shard_map/ppermute | solution.py:77
  51.9 7.8 %collective-permute-start.1 = (bf16[1,2,128,128]{3,2,1,0:T(8,128)(2,1)S(1)}, bf16[1,2,128,128]{3,2,1,0:T(8,128)(2,1)S(1)}, u32[]{:S(2)}, u32[]{:S(2)}) collective-permute-start(bf16[1,2,128,128]{3,2,1,0:T(8,128)(2,1)S(1)} %copy-done.1), channel_id=1, source_target_pairs={{0,2},{1,3},{2,0},{3,1},{4,6},{5,7},{6,4},{7,5},{8,10},{9,11},{10,... | collective-permute-start | bytes 196616 | tf_op jit(solution)/shard_map/ppermute | solution.py:77
  52.4 76.9 %collective-permute-start.19 = (bf16[6,2,128,128]{3,2,1,0:T(8,128)(2,1)}, bf16[6,2,128,128]{3,2,1,0:T(8,128)(2,1)S(1)}, u32[]{:S(2)}, u32[]{:S(2)}) collective-permute-start(bf16[6,2,128,128]{3,2,1,0:T(8,128)(2,1)} %get-tuple-element.61.refs_8_.refs_9_.refs_13_.refs_17_.refs_15_.refs_19_), channel_id=1, source_target_pairs={{0,1},{1,0},{2,3},{3,2},{4,5},{5,4},{6,7},{7,6},{8,9},{9,8},{10,11... | collective-permute-start | bytes 1179656 | tf_op jit(solution)/shard_map/ppermute | solution.py:77
  59.0 70.4 %collective-permute-start.21 = (bf16[6,2,128,128]{3,2,1,0:T(8,128)(2,1)S(1)}, bf16[6,2,128,128]{3,2,1,0:T(8,128)(2,1)S(1)}, u32[]{:S(2)}, u32[]{:S(2)}) collective-permute-start(bf16[6,2,128,128]{3,2,1,0:T(8,128)(2,1)S(1)} %collective-permute-done.20.refs_10_.refs_11_.refs_15_.refs_19_.refs_17_.refs_21_), channel_id=1, source_target_pairs={{0,1},{1,0},{2,3},{3,2},{4,5},{5,4},{6,7},{7,6},{8,9},{9,8},{10,11... | collective-permute-start | bytes 1179656 | tf_op jit(solution)/shard_map/ppermute | solution.py:77
  59.0 12.7 %collective-permute-start = (bf16[1,2,128,128]{3,2,1,0:T(8,128)(2,1)S(1)}, bf16[1,2,128,128]{3,2,1,0:T(8,128)(2,1)S(1)}, u32[]{:S(2)}, u32[]{:S(2)}) collective-permute-start(bf16[1,2,128,128]{3,2,1,0:T(8,128)(2,1)S(1)} %copy-done.1), channel_id=1, source_target_pairs={{0,1},{1,0},{2,3},{3,2},{4,5},{5,4},{6,7},{7,6},{8,9},{9,8},{10,11... | collective-permute-start | bytes 196616 | tf_op jit(solution)/shard_map/ppermute | solution.py:77
  59.7 12.0 %collective-permute-start.2 = (bf16[1,2,128,128]{3,2,1,0:T(8,128)(2,1)S(1)}, bf16[1,2,128,128]{3,2,1,0:T(8,128)(2,1)S(1)}, u32[]{:S(2)}, u32[]{:S(2)}) collective-permute-start(bf16[1,2,128,128]{3,2,1,0:T(8,128)(2,1)S(1)} %collective-permute-done.1.refs_6_.refs_23_), channel_id=1, source_target_pairs={{0,1},{1,0},{2,3},{3,2},{4,5},{5,4},{6,7},{7,6},{8,9},{9,8},{10,11... | collective-permute-start | bytes 196616 | tf_op jit(solution)/shard_map/ppermute | solution.py:77
  73.9 10.0 %all-to-all-start.1 = ((bf16[8,16,128]{2,1,0:T(8,128)(2,1)}), bf16[8,16,128]{2,1,0:T(8,128)(2,1)S(1)}, u32[]{:S(2)}, u32[]{:S(2)}) async-start(bf16[8,16,128]{2,1,0:T(8,128)(2,1)} %get-tuple-element.44), calls=%async_computation.1 | async-start | bytes 65536 | tf_op jit(solution)/shard_map/all_to_all | solution.py:111
  86.8 10.0 %all-to-all-start.2 = ((bf16[8,16,128]{2,1,0:T(8,128)(2,1)}), bf16[8,16,128]{2,1,0:T(8,128)(2,1)S(1)}, u32[]{:S(2)}, u32[]{:S(2)}) async-start(bf16[8,16,128]{2,1,0:T(8,128)(2,1)} %get-tuple-element.47), calls=%async_computation.2 | async-start | bytes 65536 | tf_op jit(solution)/shard_map/all_to_all | solution.py:111
  99.7 10.0 %all-to-all-start.3 = ((bf16[8,16,128]{2,1,0:T(8,128)(2,1)}), bf16[8,16,128]{2,1,0:T(8,128)(2,1)S(1)}, u32[]{:S(2)}, u32[]{:S(2)}) async-start(bf16[8,16,128]{2,1,0:T(8,128)(2,1)} %get-tuple-element.51), calls=%async_computation.3 | async-start | bytes 65536 | tf_op jit(solution)/shard_map/all_to_all | solution.py:111
  112.6 10.0 %all-to-all-start.4 = ((bf16[8,16,128]{2,1,0:T(8,128)(2,1)}), bf16[8,16,128]{2,1,0:T(8,128)(2,1)S(1)}, u32[]{:S(2)}, u32[]{:S(2)}) async-start(bf16[8,16,128]{2,1,0:T(8,128)(2,1)} %get-tuple-element.54), calls=%async_computation.4 | async-start | bytes 65536 | tf_op jit(solution)/shard_map/all_to_all | solution.py:111
  125.9 10.1 %all-to-all-start.5 = ((bf16[8,1,16,128]{3,2,1,0:T(8,128)(2,1)}), bf16[8,1,16,128]{3,2,1,0:T(8,128)(2,1)S(1)}, u32[]{:S(2)}, u32[]{:S(2)}) async-start(bf16[8,1,16,128]{3,2,1,0:T(8,128)(2,1)} %get-tuple-element.58), calls=%async_computation.5 | async-start | bytes 65536 | tf_op jit(solution)/shard_map/all_to_all | solution.py:111
  139.2 10.3 %all-to-all-start.6 = ((bf16[8,2,16,128]{3,2,1,0:T(8,128)(2,1)}), bf16[8,2,16,128]{3,2,1,0:T(8,128)(2,1)S(1)}, u32[]{:S(2)}, u32[]{:S(2)}) async-start(bf16[8,2,16,128]{3,2,1,0:T(8,128)(2,1)} %get-tuple-element.63), calls=%async_computation.6 | async-start | bytes 131072 | tf_op jit(solution)/shard_map/all_to_all | solution.py:111
  152.9 10.2 %all-to-all-start.7 = ((bf16[8,2,16,128]{3,2,1,0:T(8,128)(2,1)}), bf16[8,2,16,128]{3,2,1,0:T(8,128)(2,1)S(1)}, u32[]{:S(2)}, u32[]{:S(2)}) async-start(bf16[8,2,16,128]{3,2,1,0:T(8,128)(2,1)} %get-tuple-element.66), calls=%async_computation.7 | async-start | bytes 131072 | tf_op jit(solution)/shard_map/all_to_all | solution.py:111
  158.5 6.7 %collective-permute-start.9 = (f32[6,16,128]{2,1,0:T(8,128)}, f32[6,16,128]{2,1,0:T(8,128)S(1)}, u32[]{:S(2)}, u32[]{:S(2)}) collective-permute-start(f32[6,16,128]{2,1,0:T(8,128)} %get-tuple-element.56.refs_1_), channel_id=1, source_target_pairs={{0,1},{1,0},{2,3},{3,2},{4,5},{5,4},{6,7},{7,6},{8,9},{9,8},{10,11... | collective-permute-start | bytes 147464 | tf_op jit(solution)/shard_map/ppermute | solution.py:77
  159.7 6.8 %collective-permute-start.25 = (f32[4,16,128]{2,1,0:T(8,128)}, f32[4,16,128]{2,1,0:T(8,128)S(1)}, u32[]{:S(2)}, u32[]{:S(2)}) collective-permute-start(f32[4,16,128]{2,1,0:T(8,128)} %get-tuple-element.72.refs_5_), channel_id=1, source_target_pairs={{0,1},{1,0},{2,3},{3,2},{4,5},{5,4},{6,7},{7,6},{8,9},{9,8},{10,11... | collective-permute-start | bytes 98312 | tf_op jit(solution)/shard_map/ppermute | solution.py:77
  159.8 7.7 %collective-permute-start.26 = (f32[4,16,128]{2,1,0:T(8,128)}, f32[4,16,128]{2,1,0:T(8,128)S(1)}, u32[]{:S(2)}, u32[]{:S(2)}) collective-permute-start(f32[4,16,128]{2,1,0:T(8,128)} %get-tuple-element.72.refs_5_), channel_id=1, source_target_pairs={{0,2},{1,3},{2,0},{3,1},{4,6},{5,7},{6,4},{7,5},{8,10},{9,11},{10,... | collective-permute-start | bytes 98312 | tf_op jit(solution)/shard_map/ppermute | solution.py:77
  (45 other events, 208.0 us)

commit v2 on v1

--- a/solution.py
+++ b/solution.py
@@ -10,6 +10,7 @@
 FINE = lax.Precision.HIGHEST
 MERGE_BYTES = 24 << 20
 f32, bf16 = jnp.float32, jnp.bfloat16
+ANYWHERE = -2
 
 
 def pair_number(higher, lower_level):
@@ -34,8 +35,8 @@
     return times(high, g) + times(low, g)
 
 
-def kernel_call(body, ins, outs):
-    in_keys, out_keys = list(ins), list(outs)
+def kernel_call(body, ins, outs, scratch=None):
+    in_keys, out_keys, scratch = list(ins), list(outs), scratch or {}
     arrays, specs, held = [], [], 0
     for value in ins.values():
         array, at = value if isinstance(value, tuple) else (value, -1)
@@ -47,6 +48,7 @@
             shape = array.shape
             if at >= 0:
                 shape = (1,) + shape[1:]
+            if at > -2:
                 array = pltpu.with_memory_space_constraint(array, pltpu.HBM)
             index = (max(at, 0),) + (0,) * (len(shape) - 1)
             specs.append(pl.BlockSpec(shape, lambda *_, index=index: index))
@@ -55,20 +57,23 @@
     shapes = list(outs.values())
     if len(shapes) == 1:
         shapes.append(((8, 128), f32))
-    held += sum(math.prod(s) * jnp.dtype(d).itemsize for s, d in shapes)
+    held += sum(math.prod(s[0]) * jnp.dtype(s[1]).itemsize for s in shapes)
 
     def kernel(*refs):
-        body(dict(zip(in_keys + out_keys, refs)))
-        if len(out_keys) == 1:
-            refs[-1][...] = jnp.zeros(refs[-1].shape, f32)
+        spare = [None] * (len(shapes) - len(out_keys))
+        body(dict(zip(in_keys + out_keys + spare + list(scratch), refs)))
+        if spare:
+            last = refs[len(in_keys) + 1]
+            last[...] = jnp.zeros(last.shape, f32)
 
     values = pl.pallas_call(
         kernel,
         grid=(1,),
-        out_shape=[pltpu.HBM(s, d) for s, d in shapes],
+        out_shape=[(pltpu.VMEM if len(s) > 2 else pltpu.HBM)(s[0], s[1]) for s in shapes],
         in_specs=specs,
-        out_specs=[pl.BlockSpec(s, lambda *_, d=len(s): (0,) * d) for s, d in shapes],
-        compiler_params=pltpu.CompilerParams(vmem_limit_bytes=2 * held + (3 << 20)),
+        out_specs=[pl.BlockSpec(s[0], lambda *_, d=len(s[0]): (0,) * d) for s in shapes],
+        scratch_shapes=[pltpu.VMEM(*s) for s in scratch.values()],
+        compiler_params=pltpu.CompilerParams(vmem_limit_bytes=2 * held + (4 << 20)),
     )(*arrays)
     return dict(zip(out_keys, values))
 
@@ -95,8 +100,8 @@
     merged = range(0, top - 1, 2) if merging else ()
     steps = [1 << s for s in reversed(range((cols - 1).bit_length()))]
 
-    COL, ROW, PATTERN, BLOCKS, WAIT, PRE, ARRIVED, CARRY, SEND, OUT, ALL = range(11)
-    INV, RIGHT, PANEL, X, Y, V, RAW, FAR = range(11, 19)
+    COL, ROW, PATTERN, BLOCKS, WAIT, ARRIVED, CARRY, SEND, OUT, ALL = range(10)
+    INV, RIGHT, PANEL, X, Y, V, _, FAR = range(10, 18)
 
     def inv(*ms):
         return {(INV, m): (inverses, m) for m in ms}
@@ -118,6 +123,9 @@
     bundles = {n: [(m, l) for m in range(*cut) for l in range(m)] for n, cut in zip("abc", cuts)}
     place = {pair: (n, s) for n, pairs in bundles.items() for s, pair in enumerate(pairs)}
     held, arrays = {}, {}
+
+    def near(name, q):
+        return merging and q > 0 and name in "bc"
 
     def shape_of(pairs):
         return (len(pairs), width, depth, depth), bf16
@@ -127,19 +135,22 @@
         for step in steps:
             found |= {q ^ step: exchange(v, step, cols) for q, v in found.items()}
         for q, v in found.items():
-            arrays[name, q] = v
+            arrays[name, q] = pltpu.with_memory_space_constraint(v, pltpu.VMEM) if near(name, q) else v
 
     def need(*keys):
         found = {}
         for n, s in sorted({place[k] for k in keys}):
             for q in range(cols):
                 v = arrays[n, q]
-                found[n, s, q] = v if v.shape[0] == 1 else (v, s)
+                if near(n, q):
+                    found[n, q] = (v, ANYWHERE)
+                else:
+                    found[n, s, q] = (v, ANYWHERE if v.shape[0] == 1 else s)
         return found
 
     def groups(r, key):
         name, s = place[key]
-        return [r[name, s, q].at[0] for q in range(cols)]
+        return [r[name, q].at[s] if near(name, q) else r[name, s, q].at[0] for q in range(cols)]
 
     def column(r, q, j):
         return (r[COL][0] ^ q) * width + j
@@ -210,27 +221,15 @@
         for d in [1 << s for s in reversed(range((rows - 1).bit_length()))]:
             products |= {s ^ d: lax.ppermute(v, "row", [(r, r ^ d) for r in range(rows)]) for s, v in products.items()}
 
-    gathered = {0: swap(out[SEND])}
+    gathered = {0: (swap(out[SEND]), ANYWHERE)}
     y, rounded = {}, {}
 
     def panels(lower):
         return {(PANEL, l): gathered[l] for l in lower}
 
     for m in range(1, levels):
-        def pre_body(r):
-            r[PRE][...] = own(r, m) - sum_over(r, m, range(m - 1))
-
-        pre = right(m)
-        if m > 1:
-            pre = kernel_call(
-                pre_body,
-                {COL: col, **pre, **panels(range(m - 1)), **need(*[(m, l) for l in range(m - 1)])},
-                {PRE: (panel, f32)},
-            )
-
         def solve_body(r):
-            rest = r[PRE][...] if PRE in r else own(r, m)
-            value = times_transposed(rest - sum_over(r, m, [m - 1]), r[INV, m][0, 0], FINE)
+            value = times_transposed(own(r, m) - sum_over(r, m, range(m)), r[INV, m][0, 0], FINE)
             r[X][...] = value
             if m < top:
                 send_all(r, value.astype(bf16))
@@ -243,10 +242,13 @@
         outs = {X: (panel, f32), SEND: (sent, bf16)}
         if m == top:
             outs = {X: (panel, f32), Y: (panel, f32), V: (panel, bf16), SEND: ((rows, 1, chunk, depth), bf16)}
-        out = kernel_call(solve_body, {COL: col, **pre, **inv(m), **panels([m - 1]), **need((m, m - 1))}, outs)
+        out = kernel_call(
+            solve_body,
+            {COL: col, **right(m), **inv(m), **panels(range(m)), **need(*[(m, l) for l in range(m)])}, outs,
+        )
         x[m] = out[X]
         if m < top:
-            gathered[m] = swap(out[SEND])
+            gathered[m] = (swap(out[SEND]), ANYWHERE)
     y[top], rounded[top] = out[Y], out[V]
 
     wanted = [(m, l) for l in merged for m in range(l + 2, levels)]
@@ -261,15 +263,14 @@
                         term = times(blocks[j], r[ALL][column(r, q, j), l // 2])
                         total = term if total is None else total + term
                 for j in range(width):
-                    raw = r[RAW, m, l][0, j].astype(f32)
+                    raw = groups(r, (m, l))[0][j].astype(f32)
                     r[OUT][s, j] = (raw - total[:, j * depth : (j + 1) * depth]).astype(bf16)
 
-        raws = {(RAW, m, l): (held[place[m, l][0]], place[m, l][1]) for m, l in wanted}
         held["d"] = kernel_call(
             fix_body,
-            {COL: col, ROW: row, **{(FAR, s): v for s, v in products.items()}, **raws}
-            | need(*[(m, l + 1) for m, l in wanted]),
-            {OUT: shape_of(wanted), ALL: ((rows,) + product.shape, bf16)},
+            {COL: col, ROW: row, **{(FAR, s): (v, ANYWHERE) for s, v in products.items()}}
+            | need(*wanted, *[(m, l + 1) for m, l in wanted]),
+            {OUT: shape_of(wanted)}, {ALL: ((rows,) + product.shape, bf16)},
         )[OUT]
         add_bundle("d")
         for s, (m, l) in enumerate(wanted):
@@ -287,28 +288,29 @@
     for s, done in enumerate(plan):
         targets = plan[s + 1] if s + 1 < len(plan) else ()
         upper = range(done[-1] + 1, levels)
-        arrived = swap(out[SEND])
+        arrived = (swap(out[SEND]), ANYWHERE)
         slots = (rows, max(len(targets), 1), chunk, depth)
         ins = {COL: col, ARRIVED: arrived, **inv(*done), **{(X, m): x[m] for m in done}}
         if targets:
             odds = [l + 1 for l in targets if l in merged]
 
-            def carry_body(r):
+            def carry_terms(r):
                 values = {m: r[V, m][...] for m in upper}
-                for slot, l in enumerate(targets):
-                    terms = terms_for(l, values)
-                    if l + 1 in odds:
-                        own_part = times(r[X, l + 1][...], r[INV, l + 1][0, 0], FINE).astype(bf16)
-                        terms.append((own_part, (l + 1, l)))
-                    spread_sums(r, terms, r[CARRY], slot)
-
-            carry = kernel_call(
-                carry_body,
-                {COL: col, **{(V, m): rounded[m] for m in upper}, **{(X, m): x[m] for m in odds}, **inv(*odds)}
-                | pairs_for(targets, upper) | need(*[(m, m - 1) for m in odds]),
-                {CARRY: (slots, f32)},
-            )
-            ins |= {**carry, **pairs_for(targets, done)}
+                terms = {l: terms_for(l, values) for l in targets}
+                for m in odds:
+                    own_part = times(r[X, m][...], r[INV, m][0, 0], FINE).astype(bf16)
+                    terms[m - 1].append((own_part, (m, m - 1)))
+                return terms
+
+            known = {(V, m): rounded[m] for m in upper} | {(X, m): x[m] for m in odds} | inv(*odds)
+            known |= pairs_for(targets, upper) | need(*[(m, m - 1) for m in odds])
+            if s > 0:
+                def carry_body(r):
+                    for slot, (l, terms) in enumerate(carry_terms(r).items()):
+                        spread_sums(r, terms, r[CARRY], slot)
+
+                known = kernel_call(carry_body, {COL: col, **known}, {CARRY: (slots, f32)})
+            ins |= {**known, **pairs_for(targets, done)}
 
         def step_body(r):
             values = {}
@@ -323,8 +325,9 @@
                 r[Y, m][...] = result
                 values[m] = result.astype(bf16)
                 r[V, m][...] = values[m]
+            folded = carry_terms(r) if targets and s == 0 else {}
             for slot, l in enumerate(targets):
-                spread_sums(r, terms_for(l, values), r[SEND], slot, r[CARRY])
+                spread_sums(r, terms_for(l, values) + folded.get(l, []), r[SEND], slot, r.get(CARRY))
 
         if targets:
             outs = {(Y, m): (panel, f32) for m in done} | {(V, m): (panel, bf16) for m in done} | {SEND: (slots, bf16)}
@@ -336,7 +339,8 @@
                 y[m], rounded[m] = out[Y, m], out[V, m]
 
     def pieces(value):
-        return [value] + [exchange(value, q, cols) for q in range(1, cols)]
+        found = {q: exchange(value, q, cols) for q in range(cols - 1, 0, -1)}
+        return [value] + [found[q] for q in range(1, cols)]
 
     def stacked(values):
         def stack_body(r):
@@ -357,7 +361,7 @@
                     r[OUT][pl.ds(at, count), where, :] = r[X, s, q][...]
                 at += count
 
-        ins = {(X, s, q): v for s, run in enumerate(runs) for q, v in enumerate(run)}
+        ins = {(X, s, q): (v, ANYWHERE if q else -1) for s, run in enumerate(runs) for q, v in enumerate(run)}
         return kernel_call(join_body, {COL: col, **ins}, {OUT: ((levels, rhs, depth), f32)})[OUT][:, None]
 
     high = pieces(stacked([y[m] for m in range(len(plan[-1]), levels)]))

time: 173 us -> 171 us (0.988)
  blocking collectives: 12 us -> 61.7 us
  waiting for transfers between devices: 58.4 us -> 35.1 us
  starting transfers between devices: 48.7 us -> 32.1 us
  Pallas kernels: 41.5 us -> 35.1 us
  local copies, waits for them, and re-layouts: 9.04 us -> 4.87 us
    all_to_all x1 -> x6, blocking collectives: 12 us -> 61.7 us  [swap(): return lax.all_to_all(value, 'row', 0, 0)]
    all_to_all x7 -> x2, waiting for transfers between devices: 26.8 us -> 4.41 us  [swap(): return lax.all_to_all(value, 'row', 0, 0)]
    all_to_all x7 -> x2, starting transfers between devices: 23.7 us -> 6.7 us  [swap(): return lax.all_to_all(value, 'row', 0, 0)]
    pallas_call x21 -> x16, Pallas kernels: 41.5 us -> 35.1 us  [kernel_call(): pl.pallas_call(kernel, grid=(1,), out_shape=[(pltpu.VMEM if len(s) > 2 el...]
    unnamed x69 -> x21, local copies, waits for them, and re-layouts: 9.04 us -> 4.87 us
  transfers between devices with their start and end apart: 35 -> 30, of which waited for: 16 -> 11; matrix products, arithmetic and copies ran while one was open for 0% -> 0% of each run, Pallas kernels for 17% -> 13%
where the time goes in v2:
time: 171 us; the launch traced here: 170 us
  blocking collectives  61.7 us (36%)
  Pallas kernels  35.1 us (21%)
  waiting for transfers between devices  35.1 us (21%)
  starting transfers between devices  32.1 us (19%)
  local copies, waits for them, and re-layouts  4.87 us (3%)
    all_to_all x6, blocking collectives, swap(): return lax.all_to_all(value, 'row', 0, 0)  61.7 us
    pallas_call x16, Pallas kernels, kernel_call(): pl.pallas_call(kernel, grid=(1,), out_shape=[(pltpu.VMEM if len(s) > 2 el...  35.1 us
    ppermute x21, waiting for transfers between devices, exchange(): return lax.ppermute(value, 'col', [(c, c ^ step) for c in range(size)])  17.8 us
    ppermute x21, starting transfers between devices, exchange(): return lax.ppermute(value, 'col', [(c, c ^ step) for c in range(size)])  13 us
    ppermute x7, waiting for transfers between devices, body_of(): lax.ppermute(v, 'row', [(r, r ^ d) for r in range(rows)])  12.9 us
    ppermute x7, starting transfers between devices, body_of(): lax.ppermute(v, 'row', [(r, r ^ d) for r in range(rows)])  12.5 us
    all_to_all x2, starting transfers between devices, swap(): return lax.all_to_all(value, 'row', 0, 0)  6.7 us
    unnamed x21, local copies, waits for them, and re-layouts  4.87 us
  transfers between devices with their start and end apart: 30, of which 11 were waited for; matrix products, arithmetic and copies ran while one was open for 0% of the time, Pallas kernels for 13%

profile of v2, /device:TPU:0, one launch (start us, length us, event | category | flops | bytes accessed | tf_op | source)
XLA Modules:
  0.0 169.6 jit_solution(4555744301936832496)
XLA Ops:
  3.9 2.5 %shard_map.61 = (bf16[5,2,128,128]{3,2,1,0:T(8,128)(2,1)}, bf16[9,2,128,128]{3,2,1,0:T(8,128)(2,1)}, bf16[2,128,256]{2,1,0:T(8,128)(2,1)}) custom-call(s32[15,1,2]{2,1,0:T(1,128)S(1)} %copy.6.refs_1_.refs_0_, bf16[15,1,2,128,128]{4,3,2,1,0:T(8,128)(2,1)} %refs_1_.8, bf16[8,16,128]{2,1,0:T(8,128)(2,1)S(1)} %copy-done.4, f32[6,1,128,128]{3,2,1,0:T(8,128)} %refs_3_.7, ...), custom_call_target="tpu_custom_call" | custom-call | tf_op jit(solution)/shard_map/pallas_call | solution.py:69
  6.4 3.0 %collective-permute-start.7 = (bf16[9,2,128,128]{3,2,1,0:T(8,128)(2,1)}, bf16[9,2,128,128]{3,2,1,0:T(8,128)(2,1)S(1)}, u32[]{:S(2)}, u32[]{:S(2)}) collective-permute-start(bf16[9,2,128,128]{3,2,1,0:T(8,128)(2,1)} %get-tuple-element.43.refs_7_.refs_11_.refs_12_.refs_13_.refs_8_.refs_14_.refs_15_.refs_17_.refs, ...), channel_id=1, source_target_pairs={{0,2},{1,3},{2,0},{3,1},{4,6},{5,7},{6,4},{7,5},{8,10},{9,11},{10,... | collective-permute-start | bytes 1769480 | tf_op jit(solution)/shard_map/ppermute | solution.py:82
  9.4 2.6 %collective-permute-start.12 = (bf16[2,128,256]{2,1,0:T(8,128)(2,1)}, bf16[2,128,256]{2,1,0:T(8,128)(2,1)S(1)}, u32[]{:S(2)}, u32[]{:S(2)}) collective-permute-start(bf16[2,128,256]{2,1,0:T(8,128)(2,1)} %get-tuple-element.51.refs_2_), channel_id=1, source_target_pairs={{0,16},{4,20},{8,24},{12,28},{16,0},{20,4},{24,8},{28,12},{1,17},{... | collective-permute-start | bytes 393224 | tf_op jit(solution)/shard_map/ppermute | solution.py:222
  14.1 9.7 %collective-permute-done.7.refs_9_.refs_10_.refs_19_.refs_7_ = bf16[9,2,128,128]{3,2,1,0:T(8,128)(2,1)S(1)} collective-permute-done((bf16[9,2,128,128]{3,2,1,0:T(8,128)(2,1)}, bf16[9,2,128,128]{3,2,1,0:T(8,128)(2,1)S(1)}, u32[]{:S(2)}, u32[]{:S(2)}) %collective-permute-start.7) | collective-permute-done | bytes 589856 | tf_op jit(solution)/shard_map/ppermute | solution.py:82
  27.4 2.8 %collective-permute-done.15.refs_6_ = bf16[2,128,256]{2,1,0:T(8,128)(2,1)S(1)} collective-permute-done((bf16[2,128,256]{2,1,0:T(8,128)(2,1)}, bf16[2,128,256]{2,1,0:T(8,128)(2,1)S(1)}, u32[]{:S(2)}, u32[]{:S(2)}) %collective-permute-start.15) | collective-permute-done | bytes 131104 | tf_op jit(solution)/shard_map/ppermute | solution.py:222
  32.4 3.0 %collective-permute-done.16.refs_7_ = bf16[2,128,256]{2,1,0:T(8,128)(2,1)S(1)} collective-permute-done((bf16[2,128,256]{2,1,0:T(8,128)(2,1)S(1)}, bf16[2,128,256]{2,1,0:T(8,128)(2,1)S(1)}, u32[]{:S(2)}, u32[]{:S(2)}) %collective-permute-start.16) | collective-permute-done | bytes 131104 | tf_op jit(solution)/shard_map/ppermute | solution.py:222
  37.0 3.5 %collective-permute-done.17.refs_8_ = bf16[2,128,256]{2,1,0:T(8,128)(2,1)S(1)} collective-permute-done((bf16[2,128,256]{2,1,0:T(8,128)(2,1)S(1)}, bf16[2,128,256]{2,1,0:T(8,128)(2,1)S(1)}, u32[]{:S(2)}, u32[]{:S(2)}) %collective-permute-start.17) | collective-permute-done | bytes 131104 | tf_op jit(solution)/shard_map/ppermute | solution.py:222
  42.6 3.6 %collective-permute-done.18.refs_9_ = bf16[2,128,256]{2,1,0:T(8,128)(2,1)} collective-permute-done((bf16[2,128,256]{2,1,0:T(8,128)(2,1)S(1)}, bf16[2,128,256]{2,1,0:T(8,128)(2,1)}, u32[]{:S(2)}, u32[]{:S(2)}) %collective-permute-start.18) | collective-permute-done | bytes 131104 | tf_op jit(solution)/shard_map/ppermute | solution.py:222
  48.0 3.0 %shard_map.68 = (bf16[6,2,128,128]{3,2,1,0:T(8,128)(2,1)}, f32[8,128]{1,0:T(8,128)}) custom-call(s32[1]{0:T(128)} %bitcast.refs_0_, s32[1]{0:T(128)} %bitcast.3.refs_1_, bf16[2,128,256]{2,1,0:T(8,128)(2,1)S(1)} %copy-done.1, bf16[2,128,256]{2,1,0:T(8,128)(2,1)S(1)} %collective-permute-done.12.refs_3_, ...), custom_call_target="tpu_custom_call" | custom-call | tf_op jit(solution)/shard_map/pallas_call | solution.py:69
  53.0 6.6 %collective-permute-done.20.refs_13_.refs_22_.refs_12_.refs_16_.refs_14_.refs_18_ = bf16[6,2,128,128]{3,2,1,0:T(8,128)(2,1)S(1)} collective-permute-done((bf16[6,2,128,128]{3,2,1,0:T(8,128)(2,1)}, bf16[6,2,128,128]{3,2,1,0:T(8,128)(2,1)S(1)}, u32[]{:S(2)}, u32[]{:S(2)}) %collective-permute-start.20) | collective-permute-done | bytes 393248 | tf_op jit(solution)/shard_map/ppermute | solution.py:82
  60.4 12.0 %all_to_all.40.refs_3_ = bf16[8,16,128]{2,1,0:T(8,128)(2,1)S(1)} all-to-all(bf16[8,16,128]{2,1,0:T(8,128)(2,1)S(1)} %copy-done.5), channel_id=1, replica_groups=mesh['row'=8,'col'=4] {'row'}, dimensions={0} | all-to-all | bytes 65536 | tf_op jit(solution)/shard_map/all_to_all | solution.py:116
  74.5 9.9 %all_to_all.41.refs_4_ = bf16[8,16,128]{2,1,0:T(8,128)(2,1)S(1)} all-to-all(bf16[8,16,128]{2,1,0:T(8,128)(2,1)} %get-tuple-element.37), channel_id=1, replica_groups=mesh['row'=8,'col'=4] {'row'}, dimensions={0} | all-to-all | bytes 65536 | tf_op jit(solution)/shard_map/all_to_all | solution.py:116
  86.8 9.9 %all_to_all.42.refs_5_ = bf16[8,16,128]{2,1,0:T(8,128)(2,1)S(1)} all-to-all(bf16[8,16,128]{2,1,0:T(8,128)(2,1)} %get-tuple-element.40), channel_id=1, replica_groups=mesh['row'=8,'col'=4] {'row'}, dimensions={0} | all-to-all | bytes 65536 | tf_op jit(solution)/shard_map/all_to_all | solution.py:116
  96.7 2.5 %shard_map.63 = (f32[16,128]{1,0:T(8,128)}, bf16[8,16,128]{2,1,0:T(8,128)(2,1)}) custom-call(s32[1]{0:T(128)} %bitcast.refs_0_, f32[6,1,64,128]{3,2,1,0:T(8,128)} %refs_1_.12, f32[6,1,128,128]{3,2,1,0:T(8,128)} %refs_3_.7, bf16[8,16,128]{2,1,0:T(8,128)(2,1)S(1)} %all_to_all.40.refs_3_, bf16[8,16,128]{2,1,0:T(8,128)(2,1)S(1)} %all_to_all.41.refs_4_, ...), custom_call_target="tpu_custom_call" | custom-call | tf_op jit(solution)/shard_map/pallas_call | solution.py:69
  99.2 9.9 %all_to_all.43.refs_6_ = bf16[8,16,128]{2,1,0:T(8,128)(2,1)S(1)} all-to-all(bf16[8,16,128]{2,1,0:T(8,128)(2,1)} %get-tuple-element.42), channel_id=1, replica_groups=mesh['row'=8,'col'=4] {'row'}, dimensions={0} | all-to-all | bytes 65536 | tf_op jit(solution)/shard_map/all_to_all | solution.py:116
  109.1 2.6 %shard_map.64 = (f32[16,128]{1,0:T(8,128)}, bf16[8,16,128]{2,1,0:T(8,128)(2,1)}) custom-call(s32[1]{0:T(128)} %bitcast.refs_0_, f32[6,1,64,128]{3,2,1,0:T(8,128)} %refs_1_.12, f32[6,1,128,128]{3,2,1,0:T(8,128)} %refs_3_.7, bf16[8,16,128]{2,1,0:T(8,128)(2,1)S(1)} %all_to_all.40.refs_3_, bf16[8,16,128]{2,1,0:T(8,128)(2,1)S(1)} %all_to_all.41.refs_4_, ...), custom_call_target="tpu_custom_call" | custom-call | tf_op jit(solution)/shard_map/pallas_call | solution.py:69
  111.8 9.9 %all_to_all.44.refs_7_ = bf16[8,16,128]{2,1,0:T(8,128)(2,1)S(1)} all-to-all(bf16[8,16,128]{2,1,0:T(8,128)(2,1)} %get-tuple-element.45), channel_id=1, replica_groups=mesh['row'=8,'col'=4] {'row'}, dimensions={0} | all-to-all | bytes 65536 | tf_op jit(solution)/shard_map/all_to_all | solution.py:116
  121.7 3.4 %shard_map.65 = (f32[16,128]{1,0:T(8,128)}, f32[16,128]{1,0:T(8,128)}, bf16[16,128]{1,0:T(8,128)(2,1)}, bf16[8,1,16,128]{3,2,1,0:T(8,128)(2,1)}) custom-call(s32[1]{0:T(128)} %bitcast.refs_0_, f32[6,1,64,128]{3,2,1,0:T(8,128)} %refs_1_.12, f32[6,1,128,128]{3,2,1,0:T(8,128)} %refs_3_.7, bf16[8,16,128]{2,1,0:T(8,128)(2,1)S(1)} %all_to_all.40.refs_3_, ...), custom_call_target="tpu_custom_call" | custom-call | tf_op jit(solution)/shard_map/pallas_call | solution.py:69
  125.1 9.9 %all_to_all.45.refs_1_ = bf16[8,1,16,128]{3,2,1,0:T(8,128)(2,1)S(1)} all-to-all(bf16[8,1,16,128]{3,2,1,0:T(8,128)(2,1)} %get-tuple-element.49), channel_id=1, replica_groups=mesh['row'=8,'col'=4] {'row'}, dimensions={0} | all-to-all | bytes 65536 | tf_op jit(solution)/shard_map/all_to_all | solution.py:116
  135.9 2.5 %shard_map.69 = (f32[16,128]{1,0:T(8,128)}, bf16[16,128]{1,0:T(8,128)(2,1)}, bf16[8,2,16,128]{3,2,1,0:T(8,128)(2,1)}) custom-call(s32[1]{0:T(128)} %bitcast.refs_0_, bf16[8,1,16,128]{3,2,1,0:T(8,128)(2,1)S(1)} %all_to_all.45.refs_1_, f32[6,1,128,128]{3,2,1,0:T(8,128)} %refs_3_.7, f32[16,128]{1,0:T(8,128)} %get-tuple-element.44.refs_4_.refs_3_, ...), custom_call_target="tpu_custom_call" | custom-call | tf_op jit(solution)/shard_map/pallas_call | solution.py:69
  138.4 3.4 %all-to-all-start.6 = ((bf16[8,2,16,128]{3,2,1,0:T(8,128)(2,1)}), bf16[8,2,16,128]{3,2,1,0:T(8,128)(2,1)S(1)}, u32[]{:S(2)}, u32[]{:S(2)}) async-start(bf16[8,2,16,128]{3,2,1,0:T(8,128)(2,1)} %get-tuple-element.53), calls=%async_computation.6 | async-start | bytes 131072 | tf_op jit(solution)/shard_map/all_to_all | solution.py:116
  141.8 2.5 %shard_map.70 = (f32[8,2,16,128]{3,2,1,0:T(8,128)}, f32[8,128]{1,0:T(8,128)}) custom-call(s32[1]{0:T(128)} %bitcast.refs_0_, bf16[16,128]{1,0:T(8,128)(2,1)} %get-tuple-element.54.refs_1_, bf16[16,128]{1,0:T(8,128)(2,1)} %get-tuple-element.50.refs_4_.refs_2_, f32[16,128]{1,0:T(8,128)} %get-tuple-element.36.refs_1_.refs_3_.refs_5_, ...), custom_call_target="tpu_custom_call" | custom-call | tf_op jit(solution)/shard_map/pallas_call | solution.py:69
  144.3 4.3 %all-to-all-done.6.refs_1_ = bf16[8,2,16,128]{3,2,1,0:T(8,128)(2,1)S(1)} async-done(((bf16[8,2,16,128]{3,2,1,0:T(8,128)(2,1)}), bf16[8,2,16,128]{3,2,1,0:T(8,128)(2,1)S(1)}, u32[]{:S(2)}, u32[]{:S(2)}) %all-to-all-start.6) | async-done | bytes 65568 | tf_op jit(solution)/shard_map/all_to_all | solution.py:116
  151.1 3.4 %all-to-all-start.7 = ((bf16[8,2,16,128]{3,2,1,0:T(8,128)(2,1)}), bf16[8,2,16,128]{3,2,1,0:T(8,128)(2,1)S(1)}, u32[]{:S(2)}, u32[]{:S(2)}) async-start(bf16[8,2,16,128]{3,2,1,0:T(8,128)(2,1)} %get-tuple-element.56), calls=%async_computation.7 | async-start | bytes 131072 | tf_op jit(solution)/shard_map/all_to_all | solution.py:116
  (79 shorter events, 42.3 us)
Async XLA Ops:
  6.4 17.4 %collective-permute-start.7 = (bf16[9,2,128,128]{3,2,1,0:T(8,128)(2,1)}, bf16[9,2,128,128]{3,2,1,0:T(8,128)(2,1)S(1)}, u32[]{:S(2)}, u32[]{:S(2)}) collective-permute-start(bf16[9,2,128,128]{3,2,1,0:T(8,128)(2,1)} %get-tuple-element.43.refs_7_.refs_11_.refs_12_.refs_13_.refs_8_.refs_14_.refs_15_.refs_17_.refs, ...), channel_id=1, source_target_pairs={{0,2},{1,3},{2,0},{3,1},{4,6},{5,7},{6,4},{7,5},{8,10},{9,11},{10,... | collective-permute-start | bytes 1769480 | tf_op jit(solution)/shard_map/ppermute | solution.py:82
  9.4 14.4 %collective-permute-start.12 = (bf16[2,128,256]{2,1,0:T(8,128)(2,1)}, bf16[2,128,256]{2,1,0:T(8,128)(2,1)S(1)}, u32[]{:S(2)}, u32[]{:S(2)}) collective-permute-start(bf16[2,128,256]{2,1,0:T(8,128)(2,1)} %get-tuple-element.51.refs_2_), channel_id=1, source_target_pairs={{0,16},{4,20},{8,24},{12,28},{16,0},{20,4},{24,8},{28,12},{1,17},{... | collective-permute-start | bytes 393224 | tf_op jit(solution)/shard_map/ppermute | solution.py:222
  12.0 19.9 %collective-permute-start.4 = (bf16[5,2,128,128]{3,2,1,0:T(8,128)(2,1)}, bf16[5,2,128,128]{3,2,1,0:T(8,128)(2,1)S(1)}, u32[]{:S(2)}, u32[]{:S(2)}) collective-permute-start(bf16[5,2,128,128]{3,2,1,0:T(8,128)(2,1)} %get-tuple-element.38.refs_5_.refs_9_.refs_6_.refs_10_.refs_11_.refs_14_.refs_15_.refs_16_.refs_7_), channel_id=1, source_target_pairs={{0,2},{1,3},{2,0},{3,1},{4,6},{5,7},{6,4},{7,5},{8,10},{9,11},{10,... | collective-permute-start | bytes 983048 | tf_op jit(solution)/shard_map/ppermute | solution.py:82
  12.5 13.3 %collective-permute-start.13 = (bf16[2,128,256]{2,1,0:T(8,128)(2,1)}, bf16[2,128,256]{2,1,0:T(8,128)(2,1)S(1)}, u32[]{:S(2)}, u32[]{:S(2)}) collective-permute-start(bf16[2,128,256]{2,1,0:T(8,128)(2,1)} %get-tuple-element.51.refs_2_), channel_id=1, source_target_pairs={{0,8},{4,12},{8,0},{12,4},{16,24},{20,28},{24,16},{28,20},{1,9},{5... | collective-permute-start | bytes 393224 | tf_op jit(solution)/shard_map/ppermute | solution.py:222
  14.1 32.1 %collective-permute-start.6 = (bf16[9,2,128,128]{3,2,1,0:T(8,128)(2,1)}, bf16[9,2,128,128]{3,2,1,0:T(8,128)(2,1)S(1)}, u32[]{:S(2)}, u32[]{:S(2)}) collective-permute-start(bf16[9,2,128,128]{3,2,1,0:T(8,128)(2,1)} %get-tuple-element.43.refs_7_.refs_11_.refs_12_.refs_13_.refs_8_.refs_14_.refs_15_.refs_17_.refs, ...), channel_id=1, source_target_pairs={{0,1},{1,0},{2,3},{3,2},{4,5},{5,4},{6,7},{7,6},{8,9},{9,8},{10,11... | collective-permute-start | bytes 1769480 | tf_op jit(solution)/shard_map/ppermute | solution.py:82
  23.8 22.4 %collective-permute-start.8 = (bf16[9,2,128,128]{3,2,1,0:T(8,128)(2,1)S(1)}, bf16[9,2,128,128]{3,2,1,0:T(8,128)(2,1)S(1)}, u32[]{:S(2)}, u32[]{:S(2)}) collective-permute-start(bf16[9,2,128,128]{3,2,1,0:T(8,128)(2,1)S(1)} %collective-permute-done.7.refs_9_.refs_10_.refs_19_.refs_7_), channel_id=1, source_target_pairs={{0,1},{1,0},{2,3},{3,2},{4,5},{5,4},{6,7},{7,6},{8,9},{9,8},{10,11... | collective-permute-start | bytes 1769480 | tf_op jit(solution)/shard_map/ppermute | solution.py:82
  23.8 6.4 %collective-permute-start.15 = (bf16[2,128,256]{2,1,0:T(8,128)(2,1)}, bf16[2,128,256]{2,1,0:T(8,128)(2,1)S(1)}, u32[]{:S(2)}, u32[]{:S(2)}) collective-permute-start(bf16[2,128,256]{2,1,0:T(8,128)(2,1)} %get-tuple-element.51.refs_2_), channel_id=1, source_target_pairs={{0,4},{4,0},{8,12},{12,8},{16,20},{20,16},{24,28},{28,24},{1,5},{5... | collective-permute-start | bytes 393224 | tf_op jit(solution)/shard_map/ppermute | solution.py:222
  25.8 6.1 %collective-permute-start.14 = (bf16[2,128,256]{2,1,0:T(8,128)(2,1)S(1)}, bf16[2,128,256]{2,1,0:T(8,128)(2,1)S(1)}, u32[]{:S(2)}, u32[]{:S(2)}) collective-permute-start(bf16[2,128,256]{2,1,0:T(8,128)(2,1)S(1)} %collective-permute-done.12.refs_3_), channel_id=1, source_target_pairs={{0,8},{4,12},{8,0},{12,4},{16,24},{20,28},{24,16},{28,20},{1,9},{5... | collective-permute-start | bytes 393224 | tf_op jit(solution)/shard_map/ppermute | solution.py:222
  30.2 5.3 %collective-permute-start.16 = (bf16[2,128,256]{2,1,0:T(8,128)(2,1)S(1)}, bf16[2,128,256]{2,1,0:T(8,128)(2,1)S(1)}, u32[]{:S(2)}, u32[]{:S(2)}) collective-permute-start(bf16[2,128,256]{2,1,0:T(8,128)(2,1)S(1)} %collective-permute-done.12.refs_3_), channel_id=1, source_target_pairs={{0,4},{4,0},{8,12},{12,8},{16,20},{20,16},{24,28},{28,24},{1,5},{5... | collective-permute-start | bytes 393224 | tf_op jit(solution)/shard_map/ppermute | solution.py:222
  31.9 10.7 %collective-permute-start.3 = (bf16[5,2,128,128]{3,2,1,0:T(8,128)(2,1)}, bf16[5,2,128,128]{3,2,1,0:T(8,128)(2,1)S(1)}, u32[]{:S(2)}, u32[]{:S(2)}) collective-permute-start(bf16[5,2,128,128]{3,2,1,0:T(8,128)(2,1)} %get-tuple-element.38.refs_5_.refs_9_.refs_6_.refs_10_.refs_11_.refs_14_.refs_15_.refs_16_.refs_7_), channel_id=1, source_target_pairs={{0,1},{1,0},{2,3},{3,2},{4,5},{5,4},{6,7},{7,6},{8,9},{9,8},{10,11... | collective-permute-start | bytes 983048 | tf_op jit(solution)/shard_map/ppermute | solution.py:82
  31.9 14.3 %collective-permute-start.5 = (bf16[5,2,128,128]{3,2,1,0:T(8,128)(2,1)S(1)}, bf16[5,2,128,128]{3,2,1,0:T(8,128)(2,1)S(1)}, u32[]{:S(2)}, u32[]{:S(2)}) collective-permute-start(bf16[5,2,128,128]{3,2,1,0:T(8,128)(2,1)S(1)} %collective-permute-done.4.refs_7_.refs_8_.refs_12_.refs_17_.refs_9_), channel_id=1, source_target_pairs={{0,1},{1,0},{2,3},{3,2},{4,5},{5,4},{6,7},{7,6},{8,9},{9,8},{10,11... | collective-permute-start | bytes 983048 | tf_op jit(solution)/shard_map/ppermute | solution.py:82
  51.0 8.7 %collective-permute-start.20 = (bf16[6,2,128,128]{3,2,1,0:T(8,128)(2,1)}, bf16[6,2,128,128]{3,2,1,0:T(8,128)(2,1)S(1)}, u32[]{:S(2)}, u32[]{:S(2)}) collective-permute-start(bf16[6,2,128,128]{3,2,1,0:T(8,128)(2,1)} %get-tuple-element.52.refs_11_.refs_20_.refs_10_.refs_14_.refs_12_.refs_16_), channel_id=1, source_target_pairs={{0,2},{1,3},{2,0},{3,1},{4,6},{5,7},{6,4},{7,5},{8,10},{9,11},{10,... | collective-permute-start | bytes 1179656 | tf_op jit(solution)/shard_map/ppermute | solution.py:82
  52.5 7.9 %collective-permute-start.1 = (bf16[1,2,128,128]{3,2,1,0:T(8,128)(2,1)S(1)}, bf16[1,2,128,128]{3,2,1,0:T(8,128)(2,1)S(1)}, u32[]{:S(2)}, u32[]{:S(2)}) collective-permute-start(bf16[1,2,128,128]{3,2,1,0:T(8,128)(2,1)S(1)} %copy-done), channel_id=1, source_target_pairs={{0,2},{1,3},{2,0},{3,1},{4,6},{5,7},{6,4},{7,5},{8,10},{9,11},{10,... | collective-permute-start | bytes 196616 | tf_op jit(solution)/shard_map/ppermute | solution.py:82
  53.0 82.0 %collective-permute-start.19 = (bf16[6,2,128,128]{3,2,1,0:T(8,128)(2,1)}, bf16[6,2,128,128]{3,2,1,0:T(8,128)(2,1)S(1)}, u32[]{:S(2)}, u32[]{:S(2)}) collective-permute-start(bf16[6,2,128,128]{3,2,1,0:T(8,128)(2,1)} %get-tuple-element.52.refs_11_.refs_20_.refs_10_.refs_14_.refs_12_.refs_16_), channel_id=1, source_target_pairs={{0,1},{1,0},{2,3},{3,2},{4,5},{5,4},{6,7},{7,6},{8,9},{9,8},{10,11... | collective-permute-start | bytes 1179656 | tf_op jit(solution)/shard_map/ppermute | solution.py:82
  59.7 75.4 %collective-permute-start.21 = (bf16[6,2,128,128]{3,2,1,0:T(8,128)(2,1)S(1)}, bf16[6,2,128,128]{3,2,1,0:T(8,128)(2,1)S(1)}, u32[]{:S(2)}, u32[]{:S(2)}) collective-permute-start(bf16[6,2,128,128]{3,2,1,0:T(8,128)(2,1)S(1)} %collective-permute-done.20.refs_13_.refs_22_.refs_12_.refs_16_.refs_14_.refs_18_), channel_id=1, source_target_pairs={{0,1},{1,0},{2,3},{3,2},{4,5},{5,4},{6,7},{7,6},{8,9},{9,8},{10,11... | collective-permute-start | bytes 1179656 | tf_op jit(solution)/shard_map/ppermute | solution.py:82
  59.7 12.7 %collective-permute-start = (bf16[1,2,128,128]{3,2,1,0:T(8,128)(2,1)S(1)}, bf16[1,2,128,128]{3,2,1,0:T(8,128)(2,1)S(1)}, u32[]{:S(2)}, u32[]{:S(2)}) collective-permute-start(bf16[1,2,128,128]{3,2,1,0:T(8,128)(2,1)S(1)} %copy-done), channel_id=1, source_target_pairs={{0,1},{1,0},{2,3},{3,2},{4,5},{5,4},{6,7},{7,6},{8,9},{9,8},{10,11... | collective-permute-start | bytes 196616 | tf_op jit(solution)/shard_map/ppermute | solution.py:82
  60.4 12.0 %collective-permute-start.2 = (bf16[1,2,128,128]{3,2,1,0:T(8,128)(2,1)S(1)}, bf16[1,2,128,128]{3,2,1,0:T(8,128)(2,1)S(1)}, u32[]{:S(2)}, u32[]{:S(2)}) collective-permute-start(bf16[1,2,128,128]{3,2,1,0:T(8,128)(2,1)S(1)} %collective-permute-done.1.refs_6_.refs_20_), channel_id=1, source_target_pairs={{0,1},{1,0},{2,3},{3,2},{4,5},{5,4},{6,7},{7,6},{8,9},{9,8},{10,11... | collective-permute-start | bytes 196616 | tf_op jit(solution)/shard_map/ppermute | solution.py:82
  138.4 10.2 %all-to-all-start.6 = ((bf16[8,2,16,128]{3,2,1,0:T(8,128)(2,1)}), bf16[8,2,16,128]{3,2,1,0:T(8,128)(2,1)S(1)}, u32[]{:S(2)}, u32[]{:S(2)}) async-start(bf16[8,2,16,128]{3,2,1,0:T(8,128)(2,1)} %get-tuple-element.53), calls=%async_computation.6 | async-start | bytes 131072 | tf_op jit(solution)/shard_map/all_to_all | solution.py:116
  151.1 10.2 %all-to-all-start.7 = ((bf16[8,2,16,128]{3,2,1,0:T(8,128)(2,1)}), bf16[8,2,16,128]{3,2,1,0:T(8,128)(2,1)S(1)}, u32[]{:S(2)}, u32[]{:S(2)}) async-start(bf16[8,2,16,128]{3,2,1,0:T(8,128)(2,1)} %get-tuple-element.56), calls=%async_computation.7 | async-start | bytes 131072 | tf_op jit(solution)/shard_map/all_to_all | solution.py:116
  157.4 5.6 %collective-permute-start.11 = (f32[6,16,128]{2,1,0:T(8,128)}, f32[6,16,128]{2,1,0:T(8,128)S(1)}, u32[]{:S(2)}, u32[]{:S(2)}) collective-permute-start(f32[6,16,128]{2,1,0:T(8,128)} %get-tuple-element.47.refs_1_), channel_id=1, source_target_pairs={{0,3},{1,2},{2,1},{3,0},{4,7},{5,6},{6,5},{7,4},{8,11},{9,10},{10,... | collective-permute-start | bytes 147464 | tf_op jit(solution)/shard_map/ppermute | solution.py:82
  157.4 6.6 %collective-permute-start.9 = (f32[6,16,128]{2,1,0:T(8,128)}, f32[6,16,128]{2,1,0:T(8,128)S(1)}, u32[]{:S(2)}, u32[]{:S(2)}) collective-permute-start(f32[6,16,128]{2,1,0:T(8,128)} %get-tuple-element.47.refs_1_), channel_id=1, source_target_pairs={{0,1},{1,0},{2,3},{3,2},{4,5},{5,4},{6,7},{7,6},{8,9},{9,8},{10,11... | collective-permute-start | bytes 147464 | tf_op jit(solution)/shard_map/ppermute | solution.py:82
  159.4 5.4 %collective-permute-start.25 = (f32[4,16,128]{2,1,0:T(8,128)}, f32[4,16,128]{2,1,0:T(8,128)S(1)}, u32[]{:S(2)}, u32[]{:S(2)}) collective-permute-start(f32[4,16,128]{2,1,0:T(8,128)} %get-tuple-element.62.refs_5_), channel_id=1, source_target_pairs={{0,1},{1,0},{2,3},{3,2},{4,5},{5,4},{6,7},{7,6},{8,9},{9,8},{10,11... | collective-permute-start | bytes 98312 | tf_op jit(solution)/shard_map/ppermute | solution.py:82
  159.4 7.5 %collective-permute-start.26 = (f32[4,16,128]{2,1,0:T(8,128)}, f32[4,16,128]{2,1,0:T(8,128)S(1)}, u32[]{:S(2)}, u32[]{:S(2)}) collective-permute-start(f32[4,16,128]{2,1,0:T(8,128)} %get-tuple-element.62.refs_5_), channel_id=1, source_target_pairs={{0,2},{1,3},{2,0},{3,1},{4,6},{5,7},{6,4},{7,5},{8,10},{9,11},{10,... | collective-permute-start | bytes 98312 | tf_op jit(solution)/shard_map/ppermute | solution.py:82
  160.9 6.0 %collective-permute-start.27 = (f32[4,16,128]{2,1,0:T(8,128)}, f32[4,16,128]{2,1,0:T(8,128)S(1)}, u32[]{:S(2)}, u32[]{:S(2)}) collective-permute-start(f32[4,16,128]{2,1,0:T(8,128)} %get-tuple-element.62.refs_5_), channel_id=1, source_target_pairs={{0,3},{1,2},{2,1},{3,0},{4,7},{5,6},{6,5},{7,4},{8,11},{9,10},{10,... | collective-permute-start | bytes 98312 | tf_op jit(solution)/shard_map/ppermute | solution.py:82
  (16 other events, 63.6 us)

commit v3 on v2

--- a/solution.py
+++ b/solution.py
@@ -43,7 +43,8 @@
         if array.dtype == jnp.int32:
             specs.append(pl.BlockSpec(memory_space=pltpu.SMEM))
         elif at is None:
-            specs.append(pl.BlockSpec(memory_space=pl.ANY))
+            array = pltpu.with_memory_space_constraint(array, pltpu.HBM)
+            specs.append(pl.BlockSpec(memory_space=pltpu.HBM))
         else:
             shape = array.shape
             if at >= 0:
@@ -125,14 +126,16 @@
     held, arrays = {}, {}
 
     def near(name, q):
-        return merging and q > 0 and name in "bc"
+        return merging and q > 0 and name in "bcd"
 
     def shape_of(pairs):
         return (len(pairs), width, depth, depth), bf16
 
     def add_bundle(name):
         found = {0: held[name]}
-        for step in steps:
+        if name == "a":
+            found |= {q: exchange(held[name], q, cols) for q in range(cols - 1, 0, -1)}
+        for step in steps if name != "a" else ():
             found |= {q ^ step: exchange(v, step, cols) for q, v in found.items()}
         for q, v in found.items():
             arrays[name, q] = pltpu.with_memory_space_constraint(v, pltpu.VMEM) if near(name, q) else v
@@ -159,20 +162,30 @@
         total = None
         for l in lower:
             for q, blocks in enumerate(groups(r, (m, l))):
-                for j in range(width):
-                    term = times_transposed(r[PANEL, l][column(r, q, j)], blocks[j])
+                for j in range(0, width, 2):
+                    pair = range(j, min(j + 2, width))
+                    term = times_transposed(
+                        jnp.concatenate([r[PANEL, l][column(r, q, i)] for i in pair], 1),
+                        jnp.concatenate([blocks[i] for i in pair], 1),
+                    )
                     total = term if total is None else total + term
         return total
 
     def spread_sums(r, terms, out_ref, slot, carried=None):
         for q in range(cols):
-            for j in range(width):
-                k = column(r, q, j)
-                total = None if carried is None else carried[k, slot]
+            for j in range(0, width, 2):
+                pair = range(j, min(j + 2, width))
+                total = None
                 for value, key in terms:
-                    term = times(value, groups(r, key)[q][j])
+                    blocks = groups(r, key)[q]
+                    term = times(value, jnp.concatenate([blocks[i] for i in pair], 1))
                     total = term if total is None else total + term
-                out_ref[k, slot] = total.astype(out_ref.dtype)
+                for s, i in enumerate(pair):
+                    k = column(r, q, i)
+                    part = total[:, s * depth : (s + 1) * depth]
+                    if carried is not None:
+                        part = part + carried[k, slot]
+                    out_ref[k, slot] = part.astype(out_ref.dtype)
 
     def masked(r, p, at, j):
         value = r[BLOCKS][at, 0, j]
@@ -251,12 +264,15 @@
             gathered[m] = (swap(out[SEND]), ANYWHERE)
     y[top], rounded[top] = out[Y], out[V]
 
-    wanted = [(m, l) for l in merged for m in range(l + 2, levels)]
+    wanted = [(m, l) for l in reversed(merged) for m in range(l + 2, levels)]
     if merged:
+        first = [key for key in wanted if key[1] == merged[-1]]
+        fixed = {"d": first, "g": wanted[len(first) :]}
+
         def fix_body(r):
             for s in range(rows):
                 r[ALL][r[ROW][0] ^ s] = r[FAR, s][...]
-            for s, (m, l) in enumerate(wanted):
+            for n, s, m, l in [(n, s, *key) for n, keys in fixed.items() for s, key in enumerate(keys)]:
                 total = None
                 for q, blocks in enumerate(groups(r, (m, l + 1))):
                     for j in range(width):
@@ -264,17 +280,18 @@
                         total = term if total is None else total + term
                 for j in range(width):
                     raw = groups(r, (m, l))[0][j].astype(f32)
-                    r[OUT][s, j] = (raw - total[:, j * depth : (j + 1) * depth]).astype(bf16)
-
-        held["d"] = kernel_call(
+                    r[n][s, j] = (raw - total[:, j * depth : (j + 1) * depth]).astype(bf16)
+
+        held |= kernel_call(
             fix_body,
             {COL: col, ROW: row, **{(FAR, s): (v, ANYWHERE) for s, v in products.items()}}
             | need(*wanted, *[(m, l + 1) for m, l in wanted]),
-            {OUT: shape_of(wanted)}, {ALL: ((rows,) + product.shape, bf16)},
-        )[OUT]
-        add_bundle("d")
-        for s, (m, l) in enumerate(wanted):
-            place[m, l, True] = ("d", s)
+            {n: shape_of(keys) for n, keys in fixed.items()}, {ALL: ((rows,) + product.shape, bf16)},
+        )
+        for n, keys in fixed.items():
+            add_bundle(n)
+            for s, (m, l) in enumerate(keys):
+                place[m, l, True] = (n, s)
 
     lower = [(l, l + 1) for l in reversed(merged)] if merged else [(l,) for l in range(top - 2, -1, -1)]
     plan = [(top - 1,)] + lower

time: 171 us -> 165 us (0.965)
  blocking collectives: 61.7 us -> 42.1 us
  starting transfers between devices: 32.1 us -> 40 us
  waiting for transfers between devices: 35.1 us -> 41 us
  Pallas kernels: 35.1 us -> 33.2 us
    all_to_all x6 -> x4, blocking collectives: 61.7 us -> 42.1 us  [swap(): return lax.all_to_all(value, 'row', 0, 0)]
    all_to_all x2 -> x4, waiting for transfers between devices: 4.41 us -> 16.1 us  [swap(): return lax.all_to_all(value, 'row', 0, 0)]
    all_to_all x2 -> x4, starting transfers between devices: 6.7 us -> 13.4 us  [swap(): return lax.all_to_all(value, 'row', 0, 0)]
    ppermute x21 -> x24, waiting for transfers between devices: 17.8 us -> 12.1 us  [exchange(): return lax.ppermute(value, 'col', [(c, c ^ step) for c in range(size)])]
    pallas_call x16, Pallas kernels: 35.1 us -> 33.2 us  [kernel_call(): pl.pallas_call(kernel, grid=(1,), out_shape=[(pltpu.VMEM if len(s) > 2 el...]
    ppermute x21 -> x24, starting transfers between devices: 13 us -> 14.2 us  [exchange(): return lax.ppermute(value, 'col', [(c, c ^ step) for c in range(size)])]
  transfers between devices with their start and end apart: 30 -> 35, of which waited for: 11 -> 12; matrix products, arithmetic and copies ran while one was open for 0% -> 0% of each run, Pallas kernels for 13% -> 14%
where the time goes in v3:
time: 165 us; the launch traced here: 163 us
  blocking collectives  42.1 us (26%)
  waiting for transfers between devices  41 us (25%)
  starting transfers between devices  40 us (24%)
  Pallas kernels  33.2 us (20%)
  local copies, waits for them, and re-layouts  6.36 us (4%)
    all_to_all x4, blocking collectives, swap(): return lax.all_to_all(value, 'row', 0, 0)  42.1 us
    pallas_call x16, Pallas kernels, kernel_call(): pl.pallas_call(kernel, grid=(1,), out_shape=[(pltpu.VMEM if len(s) > 2 el...  33.2 us
    all_to_all x4, waiting for transfers between devices, swap(): return lax.all_to_all(value, 'row', 0, 0)  16.1 us
    ppermute x24, starting transfers between devices, exchange(): return lax.ppermute(value, 'col', [(c, c ^ step) for c in range(size)])  14.2 us
    all_to_all x4, starting transfers between devices, swap(): return lax.all_to_all(value, 'row', 0, 0)  13.4 us
    ppermute x7, waiting for transfers between devices, body_of(): lax.ppermute(v, 'row', [(r, r ^ d) for r in range(rows)])  12.8 us
    ppermute x7, starting transfers between devices, body_of(): lax.ppermute(v, 'row', [(r, r ^ d) for r in range(rows)])  12.5 us
    ppermute x24, waiting for transfers between devices, exchange(): return lax.ppermute(value, 'col', [(c, c ^ step) for c in range(size)])  12.1 us
  transfers between devices with their start and end apart: 35, of which 12 were waited for; matrix products, arithmetic and copies ran while one was open for 0% of the time, Pallas kernels for 14%

profile of v3, /device:TPU:0, one launch (start us, length us, event | category | flops | bytes accessed | tf_op | source)
XLA Modules:
  0.0 163.5 jit_solution(14585360340499360983)
XLA Ops:
  3.2 2.5 %shard_map.61 = (bf16[5,2,128,128]{3,2,1,0:T(8,128)(2,1)}, bf16[9,2,128,128]{3,2,1,0:T(8,128)(2,1)}, bf16[2,128,256]{2,1,0:T(8,128)(2,1)}) custom-call(s32[15,1,2]{2,1,0:T(1,128)S(1)} %copy.6.refs_1_.refs_0_, bf16[15,1,2,128,128]{4,3,2,1,0:T(8,128)(2,1)} %refs_1_.8, bf16[8,16,128]{2,1,0:T(8,128)(2,1)} %get-tuple-element.35.refs_2_, ...), custom_call_target="tpu_custom_call" | custom-call | tf_op jit(solution)/shard_map/pallas_call | solution.py:70
  5.6 3.0 %collective-permute-start.7 = (bf16[9,2,128,128]{3,2,1,0:T(8,128)(2,1)}, bf16[9,2,128,128]{3,2,1,0:T(8,128)(2,1)S(1)}, u32[]{:S(2)}, u32[]{:S(2)}) collective-permute-start(bf16[9,2,128,128]{3,2,1,0:T(8,128)(2,1)} %get-tuple-element.44.refs_7_.refs_11_.refs_12_.refs_13_.refs_8_.refs_14_.refs_15_.refs_17_.refs, ...), channel_id=1, source_target_pairs={{0,2},{1,3},{2,0},{3,1},{4,6},{5,7},{6,4},{7,5},{8,10},{9,11},{10,... | collective-permute-start | bytes 1769480 | tf_op jit(solution)/shard_map/ppermute | solution.py:83
  8.6 2.6 %collective-permute-start.12 = (bf16[2,128,256]{2,1,0:T(8,128)(2,1)}, bf16[2,128,256]{2,1,0:T(8,128)(2,1)S(1)}, u32[]{:S(2)}, u32[]{:S(2)}) collective-permute-start(bf16[2,128,256]{2,1,0:T(8,128)(2,1)} %get-tuple-element.52.refs_2_), channel_id=1, source_target_pairs={{0,16},{4,20},{8,24},{12,28},{16,0},{20,4},{24,8},{28,12},{1,17},{... | collective-permute-start | bytes 393224 | tf_op jit(solution)/shard_map/ppermute | solution.py:235
  13.3 9.7 %collective-permute-done.7.refs_9_.refs_10_.refs_19_.refs_7_ = bf16[9,2,128,128]{3,2,1,0:T(8,128)(2,1)S(1)} collective-permute-done((bf16[9,2,128,128]{3,2,1,0:T(8,128)(2,1)}, bf16[9,2,128,128]{3,2,1,0:T(8,128)(2,1)S(1)}, u32[]{:S(2)}, u32[]{:S(2)}) %collective-permute-start.7) | collective-permute-done | bytes 589856 | tf_op jit(solution)/shard_map/ppermute | solution.py:83
  26.6 2.8 %collective-permute-done.15.refs_6_ = bf16[2,128,256]{2,1,0:T(8,128)(2,1)S(1)} collective-permute-done((bf16[2,128,256]{2,1,0:T(8,128)(2,1)}, bf16[2,128,256]{2,1,0:T(8,128)(2,1)S(1)}, u32[]{:S(2)}, u32[]{:S(2)}) %collective-permute-start.15) | collective-permute-done | bytes 131104 | tf_op jit(solution)/shard_map/ppermute | solution.py:235
  31.7 3.0 %collective-permute-done.16.refs_7_ = bf16[2,128,256]{2,1,0:T(8,128)(2,1)S(1)} collective-permute-done((bf16[2,128,256]{2,1,0:T(8,128)(2,1)S(1)}, bf16[2,128,256]{2,1,0:T(8,128)(2,1)S(1)}, u32[]{:S(2)}, u32[]{:S(2)}) %collective-permute-start.16) | collective-permute-done | bytes 131104 | tf_op jit(solution)/shard_map/ppermute | solution.py:235
  36.9 3.5 %collective-permute-done.17.refs_8_ = bf16[2,128,256]{2,1,0:T(8,128)(2,1)S(1)} collective-permute-done((bf16[2,128,256]{2,1,0:T(8,128)(2,1)S(1)}, bf16[2,128,256]{2,1,0:T(8,128)(2,1)S(1)}, u32[]{:S(2)}, u32[]{:S(2)}) %collective-permute-start.17) | collective-permute-done | bytes 131104 | tf_op jit(solution)/shard_map/ppermute | solution.py:235
  42.5 3.5 %collective-permute-done.18.refs_9_ = bf16[2,128,256]{2,1,0:T(8,128)(2,1)S(1)} collective-permute-done((bf16[2,128,256]{2,1,0:T(8,128)(2,1)S(1)}, bf16[2,128,256]{2,1,0:T(8,128)(2,1)S(1)}, u32[]{:S(2)}, u32[]{:S(2)}) %collective-permute-start.18) | collective-permute-done | bytes 131104 | tf_op jit(solution)/shard_map/ppermute | solution.py:235
  50.3 2.9 %shard_map.68 = (bf16[2,2,128,128]{3,2,1,0:T(8,128)(2,1)}, bf16[4,2,128,128]{3,2,1,0:T(8,128)(2,1)}) custom-call(s32[1]{0:T(128)} %bitcast.refs_0_, s32[1]{0:T(128)} %bitcast.3.refs_1_, bf16[2,128,256]{2,1,0:T(8,128)(2,1)S(1)} %copy-done.1, bf16[2,128,256]{2,1,0:T(8,128)(2,1)S(1)} %collective-permute-done.12.refs_3_, ...), custom_call_target="tpu_custom_call" | custom-call | tf_op jit(solution)/shard_map/pallas_call | solution.py:70
  56.6 12.3 %all_to_all.40.refs_3_ = bf16[8,16,128]{2,1,0:T(8,128)(2,1)S(1)} all-to-all(bf16[8,16,128]{2,1,0:T(8,128)(2,1)S(1)} %copy-done.8), channel_id=1, replica_groups=mesh['row'=8,'col'=4] {'row'}, dimensions={0} | all-to-all | bytes 65536 | tf_op jit(solution)/shard_map/all_to_all | solution.py:117
  70.8 3.3 %all-to-all-start.1 = ((bf16[8,16,128]{2,1,0:T(8,128)(2,1)}), bf16[8,16,128]{2,1,0:T(8,128)(2,1)S(1)}, u32[]{:S(2)}, u32[]{:S(2)}) async-start(bf16[8,16,128]{2,1,0:T(8,128)(2,1)} %get-tuple-element.38), calls=%async_computation.1 | async-start | bytes 65536 | tf_op jit(solution)/shard_map/all_to_all | solution.py:117
  74.8 6.0 %all-to-all-done.1.refs_4_ = bf16[8,16,128]{2,1,0:T(8,128)(2,1)S(1)} async-done(((bf16[8,16,128]{2,1,0:T(8,128)(2,1)}), bf16[8,16,128]{2,1,0:T(8,128)(2,1)S(1)}, u32[]{:S(2)}, u32[]{:S(2)}) %all-to-all-start.1) | async-done | bytes 32800 | tf_op jit(solution)/shard_map/all_to_all | solution.py:117
  83.0 9.9 %all_to_all.41.refs_5_ = bf16[8,16,128]{2,1,0:T(8,128)(2,1)S(1)} all-to-all(bf16[8,16,128]{2,1,0:T(8,128)(2,1)} %get-tuple-element.41), channel_id=1, replica_groups=mesh['row'=8,'col'=4] {'row'}, dimensions={0} | all-to-all | bytes 65536 | tf_op jit(solution)/shard_map/all_to_all | solution.py:117
  95.2 3.3 %all-to-all-start.3 = ((bf16[8,16,128]{2,1,0:T(8,128)(2,1)}), bf16[8,16,128]{2,1,0:T(8,128)(2,1)S(1)}, u32[]{:S(2)}, u32[]{:S(2)}) async-start(bf16[8,16,128]{2,1,0:T(8,128)(2,1)} %get-tuple-element.43), calls=%async_computation.3 | async-start | bytes 65536 | tf_op jit(solution)/shard_map/all_to_all | solution.py:117
  99.7 5.5 %all-to-all-done.3.refs_6_ = bf16[8,16,128]{2,1,0:T(8,128)(2,1)S(1)} async-done(((bf16[8,16,128]{2,1,0:T(8,128)(2,1)}), bf16[8,16,128]{2,1,0:T(8,128)(2,1)S(1)}, u32[]{:S(2)}, u32[]{:S(2)}) %all-to-all-start.3) | async-done | bytes 32800 | tf_op jit(solution)/shard_map/all_to_all | solution.py:117
  105.2 2.4 %shard_map.64 = (f32[16,128]{1,0:T(8,128)}, bf16[8,16,128]{2,1,0:T(8,128)(2,1)}) custom-call(s32[1]{0:T(128)} %bitcast.refs_0_, f32[6,1,64,128]{3,2,1,0:T(8,128)} %refs_1_.12, f32[6,1,128,128]{3,2,1,0:T(8,128)} %refs_3_.7, bf16[8,16,128]{2,1,0:T(8,128)(2,1)S(1)} %all_to_all.40.refs_3_, bf16[8,16,128]{2,1,0:T(8,128)(2,1)S(1)} %all-to-all-done.1.refs_4_, ...), custom_call_target="tpu_custom_call" | custom-call | tf_op jit(solution)/shard_map/pallas_call | solution.py:70
  107.6 9.9 %all_to_all.42.refs_7_ = bf16[8,16,128]{2,1,0:T(8,128)(2,1)S(1)} all-to-all(bf16[8,16,128]{2,1,0:T(8,128)(2,1)} %get-tuple-element.46), channel_id=1, replica_groups=mesh['row'=8,'col'=4] {'row'}, dimensions={0} | all-to-all | bytes 65536 | tf_op jit(solution)/shard_map/all_to_all | solution.py:117
  117.5 2.9 %shard_map.65 = (f32[16,128]{1,0:T(8,128)}, f32[16,128]{1,0:T(8,128)}, bf16[16,128]{1,0:T(8,128)(2,1)}, bf16[8,1,16,128]{3,2,1,0:T(8,128)(2,1)}) custom-call(s32[1]{0:T(128)} %bitcast.refs_0_, f32[6,1,64,128]{3,2,1,0:T(8,128)} %refs_1_.12, f32[6,1,128,128]{3,2,1,0:T(8,128)} %refs_3_.7, bf16[8,16,128]{2,1,0:T(8,128)(2,1)S(1)} %all_to_all.40.refs_3_, ...), custom_call_target="tpu_custom_call" | custom-call | tf_op jit(solution)/shard_map/pallas_call | solution.py:70
  120.4 9.9 %all_to_all.43.refs_1_ = bf16[8,1,16,128]{3,2,1,0:T(8,128)(2,1)S(1)} all-to-all(bf16[8,1,16,128]{3,2,1,0:T(8,128)(2,1)} %get-tuple-element.50), channel_id=1, replica_groups=mesh['row'=8,'col'=4] {'row'}, dimensions={0} | all-to-all | bytes 65536 | tf_op jit(solution)/shard_map/all_to_all | solution.py:117
  132.6 3.4 %all-to-all-start.6 = ((bf16[8,2,16,128]{3,2,1,0:T(8,128)(2,1)}), bf16[8,2,16,128]{3,2,1,0:T(8,128)(2,1)S(1)}, u32[]{:S(2)}, u32[]{:S(2)}) async-start(bf16[8,2,16,128]{3,2,1,0:T(8,128)(2,1)} %get-tuple-element.54), calls=%async_computation.6 | async-start | bytes 131072 | tf_op jit(solution)/shard_map/all_to_all | solution.py:117
  135.9 2.3 %shard_map.70 = (f32[8,2,16,128]{3,2,1,0:T(8,128)}, f32[8,128]{1,0:T(8,128)}) custom-call(s32[1]{0:T(128)} %bitcast.refs_0_, bf16[16,128]{1,0:T(8,128)(2,1)} %get-tuple-element.55.refs_1_, bf16[16,128]{1,0:T(8,128)(2,1)} %get-tuple-element.51.refs_4_.refs_2_, f32[16,128]{1,0:T(8,128)} %get-tuple-element.37.refs_1_.refs_3_.refs_5_, ...), custom_call_target="tpu_custom_call" | custom-call | tf_op jit(solution)/shard_map/pallas_call | solution.py:70
  138.3 4.5 %all-to-all-done.6.refs_1_ = bf16[8,2,16,128]{3,2,1,0:T(8,128)(2,1)S(1)} async-done(((bf16[8,2,16,128]{3,2,1,0:T(8,128)(2,1)}), bf16[8,2,16,128]{3,2,1,0:T(8,128)(2,1)S(1)}, u32[]{:S(2)}, u32[]{:S(2)}) %all-to-all-start.6) | async-done | bytes 65568 | tf_op jit(solution)/shard_map/all_to_all | solution.py:117
  142.8 2.3 %shard_map.71 = (f32[16,128]{1,0:T(8,128)}, f32[16,128]{1,0:T(8,128)}, bf16[16,128]{1,0:T(8,128)(2,1)}, bf16[16,128]{1,0:T(8,128)(2,1)}, bf16[8,2,16,128]{3,2,1,0:T(8,128)(2,1)}) custom-call(s32[1]{0:T(128)} %bitcast.refs_0_, bf16[8,2,16,128]{3,2,1,0:T(8,128)(2,1)S(1)} %all-to-all-done.6.refs_1_, f32[6,1,128,128]{3,2,1,0:T(8,128)} %refs_3_.7, ...), custom_call_target="tpu_custom_call" | custom-call | tf_op jit(solution)/shard_map/pallas_call | solution.py:70
  145.1 3.4 %all-to-all-start.7 = ((bf16[8,2,16,128]{3,2,1,0:T(8,128)(2,1)}), bf16[8,2,16,128]{3,2,1,0:T(8,128)(2,1)S(1)}, u32[]{:S(2)}, u32[]{:S(2)}) async-start(bf16[8,2,16,128]{3,2,1,0:T(8,128)(2,1)} %get-tuple-element.58), calls=%async_computation.7 | async-start | bytes 131072 | tf_op jit(solution)/shard_map/all_to_all | solution.py:117
  (87 shorter events, 47.7 us)
Async XLA Ops:
  5.6 17.4 %collective-permute-start.7 = (bf16[9,2,128,128]{3,2,1,0:T(8,128)(2,1)}, bf16[9,2,128,128]{3,2,1,0:T(8,128)(2,1)S(1)}, u32[]{:S(2)}, u32[]{:S(2)}) collective-permute-start(bf16[9,2,128,128]{3,2,1,0:T(8,128)(2,1)} %get-tuple-element.44.refs_7_.refs_11_.refs_12_.refs_13_.refs_8_.refs_14_.refs_15_.refs_17_.refs, ...), channel_id=1, source_target_pairs={{0,2},{1,3},{2,0},{3,1},{4,6},{5,7},{6,4},{7,5},{8,10},{9,11},{10,... | collective-permute-start | bytes 1769480 | tf_op jit(solution)/shard_map/ppermute | solution.py:83
  8.6 14.4 %collective-permute-start.12 = (bf16[2,128,256]{2,1,0:T(8,128)(2,1)}, bf16[2,128,256]{2,1,0:T(8,128)(2,1)S(1)}, u32[]{:S(2)}, u32[]{:S(2)}) collective-permute-start(bf16[2,128,256]{2,1,0:T(8,128)(2,1)} %get-tuple-element.52.refs_2_), channel_id=1, source_target_pairs={{0,16},{4,20},{8,24},{12,28},{16,0},{20,4},{24,8},{28,12},{1,17},{... | collective-permute-start | bytes 393224 | tf_op jit(solution)/shard_map/ppermute | solution.py:235
  11.2 19.9 %collective-permute-start.4 = (bf16[5,2,128,128]{3,2,1,0:T(8,128)(2,1)}, bf16[5,2,128,128]{3,2,1,0:T(8,128)(2,1)S(1)}, u32[]{:S(2)}, u32[]{:S(2)}) collective-permute-start(bf16[5,2,128,128]{3,2,1,0:T(8,128)(2,1)} %get-tuple-element.39.refs_5_.refs_9_.refs_6_.refs_10_.refs_11_.refs_14_.refs_15_.refs_16_.refs_7_), channel_id=1, source_target_pairs={{0,2},{1,3},{2,0},{3,1},{4,6},{5,7},{6,4},{7,5},{8,10},{9,11},{10,... | collective-permute-start | bytes 983048 | tf_op jit(solution)/shard_map/ppermute | solution.py:83
  11.7 13.3 %collective-permute-start.13 = (bf16[2,128,256]{2,1,0:T(8,128)(2,1)}, bf16[2,128,256]{2,1,0:T(8,128)(2,1)S(1)}, u32[]{:S(2)}, u32[]{:S(2)}) collective-permute-start(bf16[2,128,256]{2,1,0:T(8,128)(2,1)} %get-tuple-element.52.refs_2_), channel_id=1, source_target_pairs={{0,8},{4,12},{8,0},{12,4},{16,24},{20,28},{24,16},{28,20},{1,9},{5... | collective-permute-start | bytes 393224 | tf_op jit(solution)/shard_map/ppermute | solution.py:235
  13.3 33.3 %collective-permute-start.6 = (bf16[9,2,128,128]{3,2,1,0:T(8,128)(2,1)}, bf16[9,2,128,128]{3,2,1,0:T(8,128)(2,1)S(1)}, u32[]{:S(2)}, u32[]{:S(2)}) collective-permute-start(bf16[9,2,128,128]{3,2,1,0:T(8,128)(2,1)} %get-tuple-element.44.refs_7_.refs_11_.refs_12_.refs_13_.refs_8_.refs_14_.refs_15_.refs_17_.refs, ...), channel_id=1, source_target_pairs={{0,1},{1,0},{2,3},{3,2},{4,5},{5,4},{6,7},{7,6},{8,9},{9,8},{10,11... | collective-permute-start | bytes 1769480 | tf_op jit(solution)/shard_map/ppermute | solution.py:83
  23.0 23.6 %collective-permute-start.8 = (bf16[9,2,128,128]{3,2,1,0:T(8,128)(2,1)S(1)}, bf16[9,2,128,128]{3,2,1,0:T(8,128)(2,1)S(1)}, u32[]{:S(2)}, u32[]{:S(2)}) collective-permute-start(bf16[9,2,128,128]{3,2,1,0:T(8,128)(2,1)S(1)} %collective-permute-done.7.refs_9_.refs_10_.refs_19_.refs_7_), channel_id=1, source_target_pairs={{0,1},{1,0},{2,3},{3,2},{4,5},{5,4},{6,7},{7,6},{8,9},{9,8},{10,11... | collective-permute-start | bytes 1769480 | tf_op jit(solution)/shard_map/ppermute | solution.py:83
  31.2 11.3 %collective-permute-start.3 = (bf16[5,2,128,128]{3,2,1,0:T(8,128)(2,1)}, bf16[5,2,128,128]{3,2,1,0:T(8,128)(2,1)S(1)}, u32[]{:S(2)}, u32[]{:S(2)}) collective-permute-start(bf16[5,2,128,128]{3,2,1,0:T(8,128)(2,1)} %get-tuple-element.39.refs_5_.refs_9_.refs_6_.refs_10_.refs_11_.refs_14_.refs_15_.refs_16_.refs_7_), channel_id=1, source_target_pairs={{0,1},{1,0},{2,3},{3,2},{4,5},{5,4},{6,7},{7,6},{8,9},{9,8},{10,11... | collective-permute-start | bytes 983048 | tf_op jit(solution)/shard_map/ppermute | solution.py:83
  31.2 15.5 %collective-permute-start.5 = (bf16[5,2,128,128]{3,2,1,0:T(8,128)(2,1)S(1)}, bf16[5,2,128,128]{3,2,1,0:T(8,128)(2,1)S(1)}, u32[]{:S(2)}, u32[]{:S(2)}) collective-permute-start(bf16[5,2,128,128]{3,2,1,0:T(8,128)(2,1)S(1)} %collective-permute-done.4.refs_7_.refs_8_.refs_12_.refs_17_.refs_9_), channel_id=1, source_target_pairs={{0,1},{1,0},{2,3},{3,2},{4,5},{5,4},{6,7},{7,6},{8,9},{9,8},{10,11... | collective-permute-start | bytes 983048 | tf_op jit(solution)/shard_map/ppermute | solution.py:83
  53.2 45.5 %collective-permute-start.23 = (bf16[4,2,128,128]{3,2,1,0:T(8,128)(2,1)}, bf16[4,2,128,128]{3,2,1,0:T(8,128)(2,1)}, u32[]{:S(2)}, u32[]{:S(2)}) collective-permute-start(bf16[4,2,128,128]{3,2,1,0:T(8,128)(2,1)} %get-tuple-element.56.refs_10_.refs_14_.refs_12_.refs_16_), channel_id=1, source_target_pairs={{0,2},{1,3},{2,0},{3,1},{4,6},{5,7},{6,4},{7,5},{8,10},{9,11},{10,... | collective-permute-start | bytes 786440 | tf_op jit(solution)/shard_map/ppermute | solution.py:83
  54.7 14.1 %collective-permute-start = (bf16[1,2,128,128]{3,2,1,0:T(8,128)(2,1)S(1)}, bf16[1,2,128,128]{3,2,1,0:T(8,128)(2,1)S(1)}, u32[]{:S(2)}, u32[]{:S(2)}) collective-permute-start(bf16[1,2,128,128]{3,2,1,0:T(8,128)(2,1)S(1)} %copy-done), channel_id=1, source_target_pairs={{0,1},{1,0},{2,3},{3,2},{4,5},{5,4},{6,7},{7,6},{8,9},{9,8},{10,11... | collective-permute-start | bytes 196616 | tf_op jit(solution)/shard_map/ppermute | solution.py:83
  54.7 14.1 %collective-permute-start.1 = (bf16[1,2,128,128]{3,2,1,0:T(8,128)(2,1)S(1)}, bf16[1,2,128,128]{3,2,1,0:T(8,128)(2,1)S(1)}, u32[]{:S(2)}, u32[]{:S(2)}) collective-permute-start(bf16[1,2,128,128]{3,2,1,0:T(8,128)(2,1)S(1)} %copy-done), channel_id=1, source_target_pairs={{0,2},{1,3},{2,0},{3,1},{4,6},{5,7},{6,4},{7,5},{8,10},{9,11},{10,... | collective-permute-start | bytes 196616 | tf_op jit(solution)/shard_map/ppermute | solution.py:83
  55.2 13.6 %collective-permute-start.2 = (bf16[1,2,128,128]{3,2,1,0:T(8,128)(2,1)S(1)}, bf16[1,2,128,128]{3,2,1,0:T(8,128)(2,1)S(1)}, u32[]{:S(2)}, u32[]{:S(2)}) collective-permute-start(bf16[1,2,128,128]{3,2,1,0:T(8,128)(2,1)S(1)} %copy-done), channel_id=1, source_target_pairs={{0,3},{1,2},{2,1},{3,0},{4,7},{5,6},{6,5},{7,4},{8,11},{9,10},{10,... | collective-permute-start | bytes 196616 | tf_op jit(solution)/shard_map/ppermute | solution.py:83
  70.8 10.0 %all-to-all-start.1 = ((bf16[8,16,128]{2,1,0:T(8,128)(2,1)}), bf16[8,16,128]{2,1,0:T(8,128)(2,1)S(1)}, u32[]{:S(2)}, u32[]{:S(2)}) async-start(bf16[8,16,128]{2,1,0:T(8,128)(2,1)} %get-tuple-element.38), calls=%async_computation.1 | async-start | bytes 65536 | tf_op jit(solution)/shard_map/all_to_all | solution.py:117
  74.2 25.0 %collective-permute-start.20 = (bf16[2,2,128,128]{3,2,1,0:T(8,128)(2,1)}, bf16[2,2,128,128]{3,2,1,0:T(8,128)(2,1)S(1)}, u32[]{:S(2)}, u32[]{:S(2)}) collective-permute-start(bf16[2,2,128,128]{3,2,1,0:T(8,128)(2,1)} %get-tuple-element.53.refs_11_.refs_20_), channel_id=1, source_target_pairs={{0,2},{1,3},{2,0},{3,1},{4,6},{5,7},{6,4},{7,5},{8,10},{9,11},{10,... | collective-permute-start | bytes 393224 | tf_op jit(solution)/shard_map/ppermute | solution.py:83
  95.2 10.0 %all-to-all-start.3 = ((bf16[8,16,128]{2,1,0:T(8,128)(2,1)}), bf16[8,16,128]{2,1,0:T(8,128)(2,1)S(1)}, u32[]{:S(2)}, u32[]{:S(2)}) async-start(bf16[8,16,128]{2,1,0:T(8,128)(2,1)} %get-tuple-element.43), calls=%async_computation.3 | async-start | bytes 65536 | tf_op jit(solution)/shard_map/all_to_all | solution.py:117
  98.6 37.4 %collective-permute-start.22 = (bf16[4,2,128,128]{3,2,1,0:T(8,128)(2,1)}, bf16[4,2,128,128]{3,2,1,0:T(8,128)(2,1)}, u32[]{:S(2)}, u32[]{:S(2)}) collective-permute-start(bf16[4,2,128,128]{3,2,1,0:T(8,128)(2,1)} %get-tuple-element.56.refs_10_.refs_14_.refs_12_.refs_16_), channel_id=1, source_target_pairs={{0,1},{1,0},{2,3},{3,2},{4,5},{5,4},{6,7},{7,6},{8,9},{9,8},{10,11... | collective-permute-start | bytes 786440 | tf_op jit(solution)/shard_map/ppermute | solution.py:83
  98.7 37.3 %collective-permute-start.24 = (bf16[4,2,128,128]{3,2,1,0:T(8,128)(2,1)}, bf16[4,2,128,128]{3,2,1,0:T(8,128)(2,1)}, u32[]{:S(2)}, u32[]{:S(2)}) collective-permute-start(bf16[4,2,128,128]{3,2,1,0:T(8,128)(2,1)} %collective-permute-done.23.refs_12_.refs_16_.refs_14_.refs_18_), channel_id=1, source_target_pairs={{0,1},{1,0},{2,3},{3,2},{4,5},{5,4},{6,7},{7,6},{8,9},{9,8},{10,11... | collective-permute-start | bytes 786440 | tf_op jit(solution)/shard_map/ppermute | solution.py:83
  99.1 31.2 %collective-permute-start.19 = (bf16[2,2,128,128]{3,2,1,0:T(8,128)(2,1)}, bf16[2,2,128,128]{3,2,1,0:T(8,128)(2,1)S(1)}, u32[]{:S(2)}, u32[]{:S(2)}) collective-permute-start(bf16[2,2,128,128]{3,2,1,0:T(8,128)(2,1)} %get-tuple-element.53.refs_11_.refs_20_), channel_id=1, source_target_pairs={{0,1},{1,0},{2,3},{3,2},{4,5},{5,4},{6,7},{7,6},{8,9},{9,8},{10,11... | collective-permute-start | bytes 393224 | tf_op jit(solution)/shard_map/ppermute | solution.py:83
  99.2 31.1 %collective-permute-start.21 = (bf16[2,2,128,128]{3,2,1,0:T(8,128)(2,1)S(1)}, bf16[2,2,128,128]{3,2,1,0:T(8,128)(2,1)S(1)}, u32[]{:S(2)}, u32[]{:S(2)}) collective-permute-start(bf16[2,2,128,128]{3,2,1,0:T(8,128)(2,1)S(1)} %collective-permute-done.20.refs_13_), channel_id=1, source_target_pairs={{0,1},{1,0},{2,3},{3,2},{4,5},{5,4},{6,7},{7,6},{8,9},{9,8},{10,11... | collective-permute-start | bytes 393224 | tf_op jit(solution)/shard_map/ppermute | solution.py:83
  132.6 10.2 %all-to-all-start.6 = ((bf16[8,2,16,128]{3,2,1,0:T(8,128)(2,1)}), bf16[8,2,16,128]{3,2,1,0:T(8,128)(2,1)S(1)}, u32[]{:S(2)}, u32[]{:S(2)}) async-start(bf16[8,2,16,128]{3,2,1,0:T(8,128)(2,1)} %get-tuple-element.54), calls=%async_computation.6 | async-start | bytes 131072 | tf_op jit(solution)/shard_map/all_to_all | solution.py:117
  145.1 10.2 %all-to-all-start.7 = ((bf16[8,2,16,128]{3,2,1,0:T(8,128)(2,1)}), bf16[8,2,16,128]{3,2,1,0:T(8,128)(2,1)S(1)}, u32[]{:S(2)}, u32[]{:S(2)}) async-start(bf16[8,2,16,128]{3,2,1,0:T(8,128)(2,1)} %get-tuple-element.58), calls=%async_computation.7 | async-start | bytes 131072 | tf_op jit(solution)/shard_map/all_to_all | solution.py:117
  150.4 6.6 %collective-permute-start.11 = (f32[6,16,128]{2,1,0:T(8,128)}, f32[6,16,128]{2,1,0:T(8,128)S(1)}, u32[]{:S(2)}, u32[]{:S(2)}) collective-permute-start(f32[6,16,128]{2,1,0:T(8,128)} %get-tuple-element.48.refs_1_), channel_id=1, source_target_pairs={{0,3},{1,2},{2,1},{3,0},{4,7},{5,6},{6,5},{7,4},{8,11},{9,10},{10,... | collective-permute-start | bytes 147464 | tf_op jit(solution)/shard_map/ppermute | solution.py:83
  150.4 6.9 %collective-permute-start.9 = (f32[6,16,128]{2,1,0:T(8,128)}, f32[6,16,128]{2,1,0:T(8,128)S(1)}, u32[]{:S(2)}, u32[]{:S(2)}) collective-permute-start(f32[6,16,128]{2,1,0:T(8,128)} %get-tuple-element.48.refs_1_), channel_id=1, source_target_pairs={{0,1},{1,0},{2,3},{3,2},{4,5},{5,4},{6,7},{7,6},{8,9},{9,8},{10,11... | collective-permute-start | bytes 147464 | tf_op jit(solution)/shard_map/ppermute | solution.py:83
  153.4 7.0 %collective-permute-start.29 = (f32[4,16,128]{2,1,0:T(8,128)}, f32[4,16,128]{2,1,0:T(8,128)S(1)}, u32[]{:S(2)}, u32[]{:S(2)}) collective-permute-start(f32[4,16,128]{2,1,0:T(8,128)} %get-tuple-element.64.refs_5_), channel_id=1, source_target_pairs={{0,2},{1,3},{2,0},{3,1},{4,6},{5,7},{6,4},{7,5},{8,10},{9,11},{10,... | collective-permute-start | bytes 98312 | tf_op jit(solution)/shard_map/ppermute | solution.py:83
  (21 other events, 71.2 us)

commit v4 on v3

--- a/solution.py
+++ b/solution.py
@@ -41,6 +41,8 @@
     for value in ins.values():
         array, at = value if isinstance(value, tuple) else (value, -1)
         if array.dtype == jnp.int32:
+            if array.size > 1:
+                array = pltpu.with_memory_space_constraint(array, pltpu.HBM)
             specs.append(pl.BlockSpec(memory_space=pltpu.SMEM))
         elif at is None:
             array = pltpu.with_memory_space_constraint(array, pltpu.HBM)
@@ -92,6 +94,7 @@
     width = factor_blocks.shape[2]
     chunk = rhs // cols
     top = levels - 1
+    pattern = jnp.transpose(pattern, (1, 2, 0))
     col = lax.axis_index("col").reshape(1).astype(jnp.int32)
     row = lax.axis_index("row").reshape(1).astype(jnp.int32)
     panel, sent = (chunk, depth), (rows, chunk, depth)
@@ -101,8 +104,8 @@
     merged = range(0, top - 1, 2) if merging else ()
     steps = [1 << s for s in reversed(range((cols - 1).bit_length()))]
 
-    COL, ROW, PATTERN, BLOCKS, WAIT, ARRIVED, CARRY, SEND, OUT, ALL = range(10)
-    INV, RIGHT, PANEL, X, Y, V, _, FAR = range(10, 18)
+    COL, ROW, PATTERN, BLOCKS, WAIT, ARRIVED, CARRY, SEND, OUT, ALL, STACK = range(11)
+    INV, RIGHT, PANEL, X, Y, V, FAR = range(11, 18)
 
     def inv(*ms):
         return {(INV, m): (inverses, m) for m in ms}
@@ -189,7 +192,7 @@
 
     def masked(r, p, at, j):
         value = r[BLOCKS][at, 0, j]
-        return jnp.where(r[PATTERN][p, 0, j] != 0, value, jnp.zeros_like(value))
+        return jnp.where(r[PATTERN][0, j, p] != 0, value, jnp.zeros_like(value))
 
     def first_body(r):
         value = times_transposed(own(r, 0), r[INV, 0][0, 0], FINE)
@@ -243,10 +246,13 @@
     for m in range(1, levels):
         def solve_body(r):
             value = times_transposed(own(r, m) - sum_over(r, m, range(m)), r[INV, m][0, 0], FINE)
-            r[X][...] = value
             if m < top:
+                r[X][...] = value
                 send_all(r, value.astype(bf16))
                 return
+            for l in range(top):
+                r[STACK][l] = r[X, l][...]
+            r[STACK][top] = value
             result = times(value, r[INV, m][0, 0], FINE)
             r[Y][...] = result
             r[V][...] = result.astype(bf16)
@@ -254,15 +260,18 @@
 
         outs = {X: (panel, f32), SEND: (sent, bf16)}
         if m == top:
-            outs = {X: (panel, f32), Y: (panel, f32), V: (panel, bf16), SEND: ((rows, 1, chunk, depth), bf16)}
+            outs = {STACK: ((levels,) + panel, f32), Y: (panel, f32), V: (panel, bf16)}
+            outs |= {SEND: ((rows, 1, chunk, depth), bf16)}
         out = kernel_call(
             solve_body,
-            {COL: col, **right(m), **inv(m), **panels(range(m)), **need(*[(m, l) for l in range(m)])}, outs,
+            {COL: col, **right(m), **inv(m), **panels(range(m)), **need(*[(m, l) for l in range(m)])}
+            | {(X, l): x[l] for l in range(top) if m == top}, outs,
         )
-        x[m] = out[X]
         if m < top:
+            x[m] = out[X]
             gathered[m] = (swap(out[SEND]), ANYWHERE)
     y[top], rounded[top] = out[Y], out[V]
+    solved = out[STACK]
 
     wanted = [(m, l) for l in reversed(merged) for m in range(l + 2, levels)]
     if merged:
@@ -305,6 +314,7 @@
     for s, done in enumerate(plan):
         targets = plan[s + 1] if s + 1 < len(plan) else ()
         upper = range(done[-1] + 1, levels)
+        stacks = s + 2 == len(plan)
         arrived = (swap(out[SEND]), ANYWHERE)
         slots = (rows, max(len(targets), 1), chunk, depth)
         ins = {COL: col, ARRIVED: arrived, **inv(*done), **{(X, m): x[m] for m in done}}
@@ -339,34 +349,36 @@
                 if not targets:
                     r[OUT][slot] = result
                     continue
-                r[Y, m][...] = result
+                if stacks:
+                    r[STACK][m - len(targets)] = result
+                else:
+                    r[Y, m][...] = result
                 values[m] = result.astype(bf16)
                 r[V, m][...] = values[m]
+            for m in upper if stacks else ():
+                r[STACK][m - len(targets)] = r[Y, m][...]
             folded = carry_terms(r) if targets and s == 0 else {}
             for slot, l in enumerate(targets):
                 spread_sums(r, terms_for(l, values) + folded.get(l, []), r[SEND], slot, r.get(CARRY))
 
         if targets:
-            outs = {(Y, m): (panel, f32) for m in done} | {(V, m): (panel, bf16) for m in done} | {SEND: (slots, bf16)}
+            outs = {(V, m): (panel, bf16) for m in done} | {SEND: (slots, bf16)}
+            if stacks:
+                outs[STACK] = ((levels - len(targets),) + panel, f32)
+                ins |= {(Y, m): y[m] for m in upper}
+            else:
+                outs |= {(Y, m): (panel, f32) for m in done}
         else:
             outs = {OUT: ((len(done),) + panel, f32)}
         out = kernel_call(step_body, ins, outs)
         if targets:
             for m in done:
-                y[m], rounded[m] = out[Y, m], out[V, m]
+                y[m], rounded[m] = out.get((Y, m)), out[V, m]
+            high = out.get(STACK)
 
     def pieces(value):
         found = {q: exchange(value, q, cols) for q in range(cols - 1, 0, -1)}
         return [value] + [found[q] for q in range(1, cols)]
-
-    def stacked(values):
-        def stack_body(r):
-            for s in range(len(values)):
-                r[OUT][s] = r[X, s][...]
-
-        return kernel_call(
-            stack_body, {(X, s): v for s, v in enumerate(values)}, {OUT: ((len(values),) + panel, f32)}
-        )[OUT]
 
     def joined(*runs):
         def join_body(r):
@@ -381,9 +393,9 @@
         ins = {(X, s, q): (v, ANYWHERE if q else -1) for s, run in enumerate(runs) for q, v in enumerate(run)}
         return kernel_call(join_body, {COL: col, **ins}, {OUT: ((levels, rhs, depth), f32)})[OUT][:, None]
 
-    high = pieces(stacked([y[m] for m in range(len(plan[-1]), levels)]))
-    forward = joined(pieces(stacked([x[m] for m in range(levels)])))
-    return forward, joined(pieces(out[OUT]), high)
+    last = pieces(out[OUT])
+    forward = joined(pieces(solved))
+    return forward, joined(last, pieces(high))
 
 
 def solution(mesh):

time: 165 us -> 165 us (level)
  waiting for transfers between devices: 41 us -> 46.7 us
  Pallas kernels: 33.2 us -> 30.5 us
  local copies, waits for them, and re-layouts: 6.36 us -> 4.03 us
    ppermute x7, waiting for transfers between devices: 12.8 us -> 16.1 us  [body_of(): lax.ppermute(v, 'row', [(r, r ^ d) for r in range(rows)])]
    all_to_all x4, waiting for transfers between devices: 16.1 us -> 19.1 us  [swap(): return lax.all_to_all(value, 'row', 0, 0)]
    pallas_call x16 -> x14, Pallas kernels: 33.2 us -> 30.5 us  [kernel_call(): pl.pallas_call(kernel, grid=(1,), out_shape=[(pltpu.VMEM if len(s) > 2 el...]
    unnamed x21 -> x18, local copies, waits for them, and re-layouts: 6.36 us -> 4.03 us
  transfers between devices with their start and end apart: 35 -> 35, of which waited for: 12 -> 10; matrix products, arithmetic and copies ran while one was open for 0% -> 0% of each run, Pallas kernels for 14% -> 12%
where the time goes in v4:
time: 165 us; the launch traced here: 164 us
  waiting for transfers between devices  46.7 us (28%)
  blocking collectives  42.4 us (26%)
  starting transfers between devices  39.4 us (24%)
  Pallas kernels  30.5 us (18%)
  local copies, waits for them, and re-layouts  4.03 us (2%)
    all_to_all x4, blocking collectives, swap(): return lax.all_to_all(value, 'row', 0, 0)  42.4 us
    pallas_call x14, Pallas kernels, kernel_call(): pl.pallas_call(kernel, grid=(1,), out_shape=[(pltpu.VMEM if len(s) > 2 el...  30.5 us
    all_to_all x4, waiting for transfers between devices, swap(): return lax.all_to_all(value, 'row', 0, 0)  19.1 us
    ppermute x7, waiting for transfers between devices, body_of(): lax.ppermute(v, 'row', [(r, r ^ d) for r in range(rows)])  16.1 us
    ppermute x24, starting transfers between devices, exchange(): return lax.ppermute(value, 'col', [(c, c ^ step) for c in range(size)])  14.4 us
    all_to_all x4, starting transfers between devices, swap(): return lax.all_to_all(value, 'row', 0, 0)  13.5 us
    ppermute x24, waiting for transfers between devices, exchange(): return lax.ppermute(value, 'col', [(c, c ^ step) for c in range(size)])  11.5 us
    ppermute x7, starting transfers between devices, body_of(): lax.ppermute(v, 'row', [(r, r ^ d) for r in range(rows)])  11.4 us
  transfers between devices with their start and end apart: 35, of which 10 were waited for; matrix products, arithmetic and copies ran while one was open for 0% of the time, Pallas kernels for 12%

profile of v4, /device:TPU:0, one launch (start us, length us, event | category | flops | bytes accessed | tf_op | source)
XLA Modules:
  0.0 163.9 jit_solution(17800627612350368869)
XLA Ops:
  2.4 2.5 %shard_map.61 = (bf16[5,2,128,128]{3,2,1,0:T(8,128)(2,1)}, bf16[9,2,128,128]{3,2,1,0:T(8,128)(2,1)}, bf16[2,128,256]{2,1,0:T(8,128)(2,1)}) custom-call(s32[1,2,15]{2,1,0:T(2,128)} %bitcast.10, bf16[15,1,2,128,128]{4,3,2,1,0:T(8,128)(2,1)} %refs_1_.7, bf16[8,16,128]{2,1,0:T(8,128)(2,1)} %get-tuple-element.31.refs_2_, f32[6,1,128,128]{3,2,1,0:T(8,128)} %refs_3_.7, ...), custom_call_target="tpu_custom_call" | custom-call | tf_op jit(solution)/shard_map/pallas_call | solution.py:72
  4.9 3.0 %collective-permute-start.7 = (bf16[9,2,128,128]{3,2,1,0:T(8,128)(2,1)}, bf16[9,2,128,128]{3,2,1,0:T(8,128)(2,1)S(1)}, u32[]{:S(2)}, u32[]{:S(2)}) collective-permute-start(bf16[9,2,128,128]{3,2,1,0:T(8,128)(2,1)} %get-tuple-element.37.refs_7_.refs_11_.refs_12_.refs_13_.refs_8_.refs_14_.refs_15_.refs_17_.refs, ...), channel_id=1, source_target_pairs={{0,2},{1,3},{2,0},{3,1},{4,6},{5,7},{6,4},{7,5},{8,10},{9,11},{10,... | collective-permute-start | bytes 1769480 | tf_op jit(solution)/shard_map/ppermute | solution.py:85
  11.4 10.8 %collective-permute-done.7.refs_9_.refs_10_.refs_19_.refs_7_ = bf16[9,2,128,128]{3,2,1,0:T(8,128)(2,1)S(1)} collective-permute-done((bf16[9,2,128,128]{3,2,1,0:T(8,128)(2,1)}, bf16[9,2,128,128]{3,2,1,0:T(8,128)(2,1)S(1)}, u32[]{:S(2)}, u32[]{:S(2)}) %collective-permute-start.7) | collective-permute-done | bytes 589856 | tf_op jit(solution)/shard_map/ppermute | solution.py:85
  22.3 3.1 %collective-permute-start.12 = (bf16[2,128,256]{2,1,0:T(8,128)(2,1)}, bf16[2,128,256]{2,1,0:T(8,128)(2,1)S(1)}, u32[]{:S(2)}, u32[]{:S(2)}) collective-permute-start(bf16[2,128,256]{2,1,0:T(8,128)(2,1)} %get-tuple-element.48.refs_2_), channel_id=1, source_target_pairs={{0,16},{4,20},{8,24},{12,28},{16,0},{20,4},{24,8},{28,12},{1,17},{... | collective-permute-start | bytes 393224 | tf_op jit(solution)/shard_map/ppermute | solution.py:238
  26.8 5.7 %collective-permute-done.12.refs_3_ = bf16[2,128,256]{2,1,0:T(8,128)(2,1)S(1)} collective-permute-done((bf16[2,128,256]{2,1,0:T(8,128)(2,1)}, bf16[2,128,256]{2,1,0:T(8,128)(2,1)S(1)}, u32[]{:S(2)}, u32[]{:S(2)}) %collective-permute-start.12) | collective-permute-done | bytes 131104 | tf_op jit(solution)/shard_map/ppermute | solution.py:238
  34.6 3.3 %collective-permute-done.16.refs_7_ = bf16[2,128,256]{2,1,0:T(8,128)(2,1)S(1)} collective-permute-done((bf16[2,128,256]{2,1,0:T(8,128)(2,1)S(1)}, bf16[2,128,256]{2,1,0:T(8,128)(2,1)S(1)}, u32[]{:S(2)}, u32[]{:S(2)}) %collective-permute-start.16) | collective-permute-done | bytes 131104 | tf_op jit(solution)/shard_map/ppermute | solution.py:238
  39.5 4.0 %collective-permute-done.14.refs_5_ = bf16[2,128,256]{2,1,0:T(8,128)(2,1)S(1)} collective-permute-done((bf16[2,128,256]{2,1,0:T(8,128)(2,1)S(1)}, bf16[2,128,256]{2,1,0:T(8,128)(2,1)S(1)}, u32[]{:S(2)}, u32[]{:S(2)}) %collective-permute-start.14) | collective-permute-done | bytes 131104 | tf_op jit(solution)/shard_map/ppermute | solution.py:238
  45.4 3.2 %collective-permute-done.18.refs_9_ = bf16[2,128,256]{2,1,0:T(8,128)(2,1)} collective-permute-done((bf16[2,128,256]{2,1,0:T(8,128)(2,1)S(1)}, bf16[2,128,256]{2,1,0:T(8,128)(2,1)}, u32[]{:S(2)}, u32[]{:S(2)}) %collective-permute-start.18) | collective-permute-done | bytes 131104 | tf_op jit(solution)/shard_map/ppermute | solution.py:238
  51.3 2.9 %shard_map.67 = (bf16[2,2,128,128]{3,2,1,0:T(8,128)(2,1)}, bf16[4,2,128,128]{3,2,1,0:T(8,128)(2,1)}) custom-call(s32[1]{0:T(128)} %bitcast.refs_0_, s32[1]{0:T(128)} %bitcast.4.refs_1_, bf16[2,128,256]{2,1,0:T(8,128)(2,1)S(1)} %copy-done.1, bf16[2,128,256]{2,1,0:T(8,128)(2,1)S(1)} %collective-permute-done.12.refs_3_, ...), custom_call_target="tpu_custom_call" | custom-call | tf_op jit(solution)/shard_map/pallas_call | solution.py:72
  57.4 12.6 %all_to_all.40.refs_3_ = bf16[8,16,128]{2,1,0:T(8,128)(2,1)S(1)} all-to-all(bf16[8,16,128]{2,1,0:T(8,128)(2,1)S(1)} %copy-done.6), channel_id=1, replica_groups=mesh['row'=8,'col'=4] {'row'}, dimensions={0} | all-to-all | bytes 65536 | tf_op jit(solution)/shard_map/all_to_all | solution.py:120
  72.0 3.3 %all-to-all-start.1 = ((bf16[8,16,128]{2,1,0:T(8,128)(2,1)}), bf16[8,16,128]{2,1,0:T(8,128)(2,1)S(1)}, u32[]{:S(2)}, u32[]{:S(2)}) async-start(bf16[8,16,128]{2,1,0:T(8,128)(2,1)} %get-tuple-element.33), calls=%async_computation.1 | async-start | bytes 65536 | tf_op jit(solution)/shard_map/all_to_all | solution.py:120
  75.9 6.1 %all-to-all-done.1.refs_4_ = bf16[8,16,128]{2,1,0:T(8,128)(2,1)S(1)} async-done(((bf16[8,16,128]{2,1,0:T(8,128)(2,1)}), bf16[8,16,128]{2,1,0:T(8,128)(2,1)S(1)}, u32[]{:S(2)}, u32[]{:S(2)}) %all-to-all-start.1) | async-done | bytes 32800 | tf_op jit(solution)/shard_map/all_to_all | solution.py:120
  84.1 9.9 %all_to_all.41.refs_5_ = bf16[8,16,128]{2,1,0:T(8,128)(2,1)S(1)} all-to-all(bf16[8,16,128]{2,1,0:T(8,128)(2,1)} %get-tuple-element.35), channel_id=1, replica_groups=mesh['row'=8,'col'=4] {'row'}, dimensions={0} | all-to-all | bytes 65536 | tf_op jit(solution)/shard_map/all_to_all | solution.py:120
  96.4 3.3 %all-to-all-start.3 = ((bf16[8,16,128]{2,1,0:T(8,128)(2,1)}), bf16[8,16,128]{2,1,0:T(8,128)(2,1)S(1)}, u32[]{:S(2)}, u32[]{:S(2)}) async-start(bf16[8,16,128]{2,1,0:T(8,128)(2,1)} %get-tuple-element.36), calls=%async_computation.3 | async-start | bytes 65536 | tf_op jit(solution)/shard_map/all_to_all | solution.py:120
  100.8 5.5 %all-to-all-done.3.refs_6_ = bf16[8,16,128]{2,1,0:T(8,128)(2,1)S(1)} async-done(((bf16[8,16,128]{2,1,0:T(8,128)(2,1)}), bf16[8,16,128]{2,1,0:T(8,128)(2,1)S(1)}, u32[]{:S(2)}, u32[]{:S(2)}) %all-to-all-start.3) | async-done | bytes 32800 | tf_op jit(solution)/shard_map/all_to_all | solution.py:120
  106.3 2.4 %shard_map.64 = (f32[16,128]{1,0:T(8,128)}, bf16[8,16,128]{2,1,0:T(8,128)(2,1)}) custom-call(s32[1]{0:T(128)} %bitcast.refs_0_, f32[6,1,64,128]{3,2,1,0:T(8,128)} %refs_1_.11, f32[6,1,128,128]{3,2,1,0:T(8,128)} %refs_3_.7, bf16[8,16,128]{2,1,0:T(8,128)(2,1)S(1)} %all_to_all.40.refs_3_, bf16[8,16,128]{2,1,0:T(8,128)(2,1)S(1)} %all-to-all-done.1.refs_4_, ...), custom_call_target="tpu_custom_call" | custom-call | tf_op jit(solution)/shard_map/pallas_call | solution.py:72
  108.7 9.9 %all_to_all.42.refs_7_ = bf16[8,16,128]{2,1,0:T(8,128)(2,1)S(1)} all-to-all(bf16[8,16,128]{2,1,0:T(8,128)(2,1)} %get-tuple-element.38), channel_id=1, replica_groups=mesh['row'=8,'col'=4] {'row'}, dimensions={0} | all-to-all | bytes 65536 | tf_op jit(solution)/shard_map/all_to_all | solution.py:120
  118.6 3.0 %shard_map.65 = (f32[6,16,128]{2,1,0:T(8,128)}, f32[16,128]{1,0:T(8,128)}, bf16[16,128]{1,0:T(8,128)(2,1)}, bf16[8,1,16,128]{3,2,1,0:T(8,128)(2,1)}) custom-call(s32[1]{0:T(128)} %bitcast.refs_0_, f32[6,1,64,128]{3,2,1,0:T(8,128)} %refs_1_.11, f32[6,1,128,128]{3,2,1,0:T(8,128)} %refs_3_.7, bf16[8,16,128]{2,1,0:T(8,128)(2,1)S(1)} %all_to_all.40.refs_3_, ...), custom_call_target="tpu_custom_call" | custom-call | tf_op jit(solution)/shard_map/pallas_call | solution.py:72
  121.6 9.9 %all_to_all.43.refs_1_ = bf16[8,1,16,128]{3,2,1,0:T(8,128)(2,1)S(1)} all-to-all(bf16[8,1,16,128]{3,2,1,0:T(8,128)(2,1)} %get-tuple-element.46), channel_id=1, replica_groups=mesh['row'=8,'col'=4] {'row'}, dimensions={0} | all-to-all | bytes 65536 | tf_op jit(solution)/shard_map/all_to_all | solution.py:120
  133.7 3.4 %all-to-all-start.6 = ((bf16[8,2,16,128]{3,2,1,0:T(8,128)(2,1)}), bf16[8,2,16,128]{3,2,1,0:T(8,128)(2,1)S(1)}, u32[]{:S(2)}, u32[]{:S(2)}) async-start(bf16[8,2,16,128]{3,2,1,0:T(8,128)(2,1)} %get-tuple-element.50), calls=%async_computation.6 | async-start | bytes 131072 | tf_op jit(solution)/shard_map/all_to_all | solution.py:120
  139.5 4.5 %all-to-all-done.6.refs_1_ = bf16[8,2,16,128]{3,2,1,0:T(8,128)(2,1)S(1)} async-done(((bf16[8,2,16,128]{3,2,1,0:T(8,128)(2,1)}), bf16[8,2,16,128]{3,2,1,0:T(8,128)(2,1)S(1)}, u32[]{:S(2)}, u32[]{:S(2)}) %all-to-all-start.6) | async-done | bytes 65568 | tf_op jit(solution)/shard_map/all_to_all | solution.py:120
  143.9 2.3 %shard_map.70 = (bf16[16,128]{1,0:T(8,128)(2,1)}, bf16[16,128]{1,0:T(8,128)(2,1)}, bf16[8,2,16,128]{3,2,1,0:T(8,128)(2,1)}, f32[4,16,128]{2,1,0:T(8,128)}) custom-call(s32[1]{0:T(128)} %bitcast.refs_0_, bf16[8,2,16,128]{3,2,1,0:T(8,128)(2,1)S(1)} %all-to-all-done.6.refs_1_, f32[6,1,128,128]{3,2,1,0:T(8,128)} %refs_3_.7, f32[6,1,128,128]{3,2,1,0:T(8,128)} %refs_3_.7, ...), custom_call_target="tpu_custom_call" | custom-call | tf_op jit(solution)/shard_map/pallas_call | solution.py:72
  146.3 3.5 %all-to-all-start.7 = ((bf16[8,2,16,128]{3,2,1,0:T(8,128)(2,1)}), bf16[8,2,16,128]{3,2,1,0:T(8,128)(2,1)S(1)}, u32[]{:S(2)}, u32[]{:S(2)}) async-start(bf16[8,2,16,128]{3,2,1,0:T(8,128)(2,1)} %get-tuple-element.56), calls=%async_computation.7 | async-start | bytes 131072 | tf_op jit(solution)/shard_map/all_to_all | solution.py:120
  153.6 3.0 %all-to-all-done.7.refs_1_ = bf16[8,2,16,128]{3,2,1,0:T(8,128)(2,1)S(1)} async-done(((bf16[8,2,16,128]{3,2,1,0:T(8,128)(2,1)}), bf16[8,2,16,128]{3,2,1,0:T(8,128)(2,1)S(1)}, u32[]{:S(2)}, u32[]{:S(2)}) %all-to-all-start.7) | async-done | bytes 65568 | tf_op jit(solution)/shard_map/all_to_all | solution.py:120
  (82 shorter events, 41.9 us)
Async XLA Ops:
  4.9 17.4 %collective-permute-start.7 = (bf16[9,2,128,128]{3,2,1,0:T(8,128)(2,1)}, bf16[9,2,128,128]{3,2,1,0:T(8,128)(2,1)S(1)}, u32[]{:S(2)}, u32[]{:S(2)}) collective-permute-start(bf16[9,2,128,128]{3,2,1,0:T(8,128)(2,1)} %get-tuple-element.37.refs_7_.refs_11_.refs_12_.refs_13_.refs_8_.refs_14_.refs_15_.refs_17_.refs, ...), channel_id=1, source_target_pairs={{0,2},{1,3},{2,0},{3,1},{4,6},{5,7},{6,4},{7,5},{8,10},{9,11},{10,... | collective-permute-start | bytes 1769480 | tf_op jit(solution)/shard_map/ppermute | solution.py:85
  7.9 14.4 %collective-permute-start.15 = (bf16[2,128,256]{2,1,0:T(8,128)(2,1)}, bf16[2,128,256]{2,1,0:T(8,128)(2,1)S(1)}, u32[]{:S(2)}, u32[]{:S(2)}) collective-permute-start(bf16[2,128,256]{2,1,0:T(8,128)(2,1)} %get-tuple-element.48.refs_2_), channel_id=1, source_target_pairs={{0,4},{4,0},{8,12},{12,8},{16,20},{20,16},{24,28},{28,24},{1,5},{5... | collective-permute-start | bytes 393224 | tf_op jit(solution)/shard_map/ppermute | solution.py:238
  9.4 24.7 %collective-permute-start.4 = (bf16[5,2,128,128]{3,2,1,0:T(8,128)(2,1)}, bf16[5,2,128,128]{3,2,1,0:T(8,128)(2,1)S(1)}, u32[]{:S(2)}, u32[]{:S(2)}) collective-permute-start(bf16[5,2,128,128]{3,2,1,0:T(8,128)(2,1)} %get-tuple-element.34.refs_5_.refs_9_.refs_6_.refs_10_.refs_11_.refs_14_.refs_15_.refs_16_.refs_7_), channel_id=1, source_target_pairs={{0,2},{1,3},{2,0},{3,1},{4,6},{5,7},{6,4},{7,5},{8,10},{9,11},{10,... | collective-permute-start | bytes 983048 | tf_op jit(solution)/shard_map/ppermute | solution.py:85
  9.9 15.5 %collective-permute-start.13 = (bf16[2,128,256]{2,1,0:T(8,128)(2,1)}, bf16[2,128,256]{2,1,0:T(8,128)(2,1)S(1)}, u32[]{:S(2)}, u32[]{:S(2)}) collective-permute-start(bf16[2,128,256]{2,1,0:T(8,128)(2,1)} %get-tuple-element.48.refs_2_), channel_id=1, source_target_pairs={{0,8},{4,12},{8,0},{12,4},{16,24},{20,28},{24,16},{28,20},{1,9},{5... | collective-permute-start | bytes 393224 | tf_op jit(solution)/shard_map/ppermute | solution.py:238
  11.4 37.1 %collective-permute-start.6 = (bf16[9,2,128,128]{3,2,1,0:T(8,128)(2,1)}, bf16[9,2,128,128]{3,2,1,0:T(8,128)(2,1)S(1)}, u32[]{:S(2)}, u32[]{:S(2)}) collective-permute-start(bf16[9,2,128,128]{3,2,1,0:T(8,128)(2,1)} %get-tuple-element.37.refs_7_.refs_11_.refs_12_.refs_13_.refs_8_.refs_14_.refs_15_.refs_17_.refs, ...), channel_id=1, source_target_pairs={{0,1},{1,0},{2,3},{3,2},{4,5},{5,4},{6,7},{7,6},{8,9},{9,8},{10,11... | collective-permute-start | bytes 1769480 | tf_op jit(solution)/shard_map/ppermute | solution.py:85
  22.2 26.3 %collective-permute-start.8 = (bf16[9,2,128,128]{3,2,1,0:T(8,128)(2,1)S(1)}, bf16[9,2,128,128]{3,2,1,0:T(8,128)(2,1)S(1)}, u32[]{:S(2)}, u32[]{:S(2)}) collective-permute-start(bf16[9,2,128,128]{3,2,1,0:T(8,128)(2,1)S(1)} %collective-permute-done.7.refs_9_.refs_10_.refs_19_.refs_7_), channel_id=1, source_target_pairs={{0,1},{1,0},{2,3},{3,2},{4,5},{5,4},{6,7},{7,6},{8,9},{9,8},{10,11... | collective-permute-start | bytes 1769480 | tf_op jit(solution)/shard_map/ppermute | solution.py:85
  22.3 10.3 %collective-permute-start.12 = (bf16[2,128,256]{2,1,0:T(8,128)(2,1)}, bf16[2,128,256]{2,1,0:T(8,128)(2,1)S(1)}, u32[]{:S(2)}, u32[]{:S(2)}) collective-permute-start(bf16[2,128,256]{2,1,0:T(8,128)(2,1)} %get-tuple-element.48.refs_2_), channel_id=1, source_target_pairs={{0,16},{4,20},{8,24},{12,28},{16,0},{20,4},{24,8},{28,12},{1,17},{... | collective-permute-start | bytes 393224 | tf_op jit(solution)/shard_map/ppermute | solution.py:238
  25.4 8.7 %collective-permute-start.17 = (bf16[2,128,256]{2,1,0:T(8,128)(2,1)S(1)}, bf16[2,128,256]{2,1,0:T(8,128)(2,1)S(1)}, u32[]{:S(2)}, u32[]{:S(2)}) collective-permute-start(bf16[2,128,256]{2,1,0:T(8,128)(2,1)S(1)} %collective-permute-done.13.refs_4_), channel_id=1, source_target_pairs={{0,4},{4,0},{8,12},{12,8},{16,20},{20,16},{24,28},{28,24},{1,5},{5... | collective-permute-start | bytes 393224 | tf_op jit(solution)/shard_map/ppermute | solution.py:238
  34.1 11.3 %collective-permute-start.3 = (bf16[5,2,128,128]{3,2,1,0:T(8,128)(2,1)}, bf16[5,2,128,128]{3,2,1,0:T(8,128)(2,1)S(1)}, u32[]{:S(2)}, u32[]{:S(2)}) collective-permute-start(bf16[5,2,128,128]{3,2,1,0:T(8,128)(2,1)} %get-tuple-element.34.refs_5_.refs_9_.refs_6_.refs_10_.refs_11_.refs_14_.refs_15_.refs_16_.refs_7_), channel_id=1, source_target_pairs={{0,1},{1,0},{2,3},{3,2},{4,5},{5,4},{6,7},{7,6},{8,9},{9,8},{10,11... | collective-permute-start | bytes 983048 | tf_op jit(solution)/shard_map/ppermute | solution.py:85
  34.1 14.5 %collective-permute-start.5 = (bf16[5,2,128,128]{3,2,1,0:T(8,128)(2,1)S(1)}, bf16[5,2,128,128]{3,2,1,0:T(8,128)(2,1)S(1)}, u32[]{:S(2)}, u32[]{:S(2)}) collective-permute-start(bf16[5,2,128,128]{3,2,1,0:T(8,128)(2,1)S(1)} %collective-permute-done.4.refs_7_.refs_8_.refs_12_.refs_17_.refs_9_), channel_id=1, source_target_pairs={{0,1},{1,0},{2,3},{3,2},{4,5},{5,4},{6,7},{7,6},{8,9},{9,8},{10,11... | collective-permute-start | bytes 983048 | tf_op jit(solution)/shard_map/ppermute | solution.py:85
  54.2 45.5 %collective-permute-start.23 = (bf16[4,2,128,128]{3,2,1,0:T(8,128)(2,1)}, bf16[4,2,128,128]{3,2,1,0:T(8,128)(2,1)}, u32[]{:S(2)}, u32[]{:S(2)}) collective-permute-start(bf16[4,2,128,128]{3,2,1,0:T(8,128)(2,1)} %get-tuple-element.52.refs_10_.refs_14_.refs_12_.refs_16_), channel_id=1, source_target_pairs={{0,2},{1,3},{2,0},{3,1},{4,6},{5,7},{6,4},{7,5},{8,10},{9,11},{10,... | collective-permute-start | bytes 786440 | tf_op jit(solution)/shard_map/ppermute | solution.py:85
  55.5 14.5 %collective-permute-start.2 = (bf16[1,2,128,128]{3,2,1,0:T(8,128)(2,1)S(1)}, bf16[1,2,128,128]{3,2,1,0:T(8,128)(2,1)S(1)}, u32[]{:S(2)}, u32[]{:S(2)}) collective-permute-start(bf16[1,2,128,128]{3,2,1,0:T(8,128)(2,1)S(1)} %copy-done), channel_id=1, source_target_pairs={{0,3},{1,2},{2,1},{3,0},{4,7},{5,6},{6,5},{7,4},{8,11},{9,10},{10,... | collective-permute-start | bytes 196616 | tf_op jit(solution)/shard_map/ppermute | solution.py:85
  55.5 14.5 %collective-permute-start.1 = (bf16[1,2,128,128]{3,2,1,0:T(8,128)(2,1)S(1)}, bf16[1,2,128,128]{3,2,1,0:T(8,128)(2,1)S(1)}, u32[]{:S(2)}, u32[]{:S(2)}) collective-permute-start(bf16[1,2,128,128]{3,2,1,0:T(8,128)(2,1)S(1)} %copy-done), channel_id=1, source_target_pairs={{0,2},{1,3},{2,0},{3,1},{4,6},{5,7},{6,4},{7,5},{8,10},{9,11},{10,... | collective-permute-start | bytes 196616 | tf_op jit(solution)/shard_map/ppermute | solution.py:85
  56.3 13.7 %collective-permute-start = (bf16[1,2,128,128]{3,2,1,0:T(8,128)(2,1)S(1)}, bf16[1,2,128,128]{3,2,1,0:T(8,128)(2,1)S(1)}, u32[]{:S(2)}, u32[]{:S(2)}) collective-permute-start(bf16[1,2,128,128]{3,2,1,0:T(8,128)(2,1)S(1)} %copy-done), channel_id=1, source_target_pairs={{0,1},{1,0},{2,3},{3,2},{4,5},{5,4},{6,7},{7,6},{8,9},{9,8},{10,11... | collective-permute-start | bytes 196616 | tf_op jit(solution)/shard_map/ppermute | solution.py:85
  72.0 10.0 %all-to-all-start.1 = ((bf16[8,16,128]{2,1,0:T(8,128)(2,1)}), bf16[8,16,128]{2,1,0:T(8,128)(2,1)S(1)}, u32[]{:S(2)}, u32[]{:S(2)}) async-start(bf16[8,16,128]{2,1,0:T(8,128)(2,1)} %get-tuple-element.33), calls=%async_computation.1 | async-start | bytes 65536 | tf_op jit(solution)/shard_map/all_to_all | solution.py:120
  75.3 25.0 %collective-permute-start.20 = (bf16[2,2,128,128]{3,2,1,0:T(8,128)(2,1)}, bf16[2,2,128,128]{3,2,1,0:T(8,128)(2,1)S(1)}, u32[]{:S(2)}, u32[]{:S(2)}) collective-permute-start(bf16[2,2,128,128]{3,2,1,0:T(8,128)(2,1)} %get-tuple-element.49.refs_11_.refs_20_), channel_id=1, source_target_pairs={{0,2},{1,3},{2,0},{3,1},{4,6},{5,7},{6,4},{7,5},{8,10},{9,11},{10,... | collective-permute-start | bytes 393224 | tf_op jit(solution)/shard_map/ppermute | solution.py:85
  96.4 10.0 %all-to-all-start.3 = ((bf16[8,16,128]{2,1,0:T(8,128)(2,1)}), bf16[8,16,128]{2,1,0:T(8,128)(2,1)S(1)}, u32[]{:S(2)}, u32[]{:S(2)}) async-start(bf16[8,16,128]{2,1,0:T(8,128)(2,1)} %get-tuple-element.36), calls=%async_computation.3 | async-start | bytes 65536 | tf_op jit(solution)/shard_map/all_to_all | solution.py:120
  99.7 37.4 %collective-permute-start.22 = (bf16[4,2,128,128]{3,2,1,0:T(8,128)(2,1)}, bf16[4,2,128,128]{3,2,1,0:T(8,128)(2,1)}, u32[]{:S(2)}, u32[]{:S(2)}) collective-permute-start(bf16[4,2,128,128]{3,2,1,0:T(8,128)(2,1)} %get-tuple-element.52.refs_10_.refs_14_.refs_12_.refs_16_), channel_id=1, source_target_pairs={{0,1},{1,0},{2,3},{3,2},{4,5},{5,4},{6,7},{7,6},{8,9},{9,8},{10,11... | collective-permute-start | bytes 786440 | tf_op jit(solution)/shard_map/ppermute | solution.py:85
  99.8 37.3 %collective-permute-start.24 = (bf16[4,2,128,128]{3,2,1,0:T(8,128)(2,1)}, bf16[4,2,128,128]{3,2,1,0:T(8,128)(2,1)}, u32[]{:S(2)}, u32[]{:S(2)}) collective-permute-start(bf16[4,2,128,128]{3,2,1,0:T(8,128)(2,1)} %collective-permute-done.23.refs_12_.refs_16_.refs_14_.refs_18_), channel_id=1, source_target_pairs={{0,1},{1,0},{2,3},{3,2},{4,5},{5,4},{6,7},{7,6},{8,9},{9,8},{10,11... | collective-permute-start | bytes 786440 | tf_op jit(solution)/shard_map/ppermute | solution.py:85
  100.3 31.3 %collective-permute-start.19 = (bf16[2,2,128,128]{3,2,1,0:T(8,128)(2,1)}, bf16[2,2,128,128]{3,2,1,0:T(8,128)(2,1)S(1)}, u32[]{:S(2)}, u32[]{:S(2)}) collective-permute-start(bf16[2,2,128,128]{3,2,1,0:T(8,128)(2,1)} %get-tuple-element.49.refs_11_.refs_20_), channel_id=1, source_target_pairs={{0,1},{1,0},{2,3},{3,2},{4,5},{5,4},{6,7},{7,6},{8,9},{9,8},{10,11... | collective-permute-start | bytes 393224 | tf_op jit(solution)/shard_map/ppermute | solution.py:85
  100.4 31.2 %collective-permute-start.21 = (bf16[2,2,128,128]{3,2,1,0:T(8,128)(2,1)S(1)}, bf16[2,2,128,128]{3,2,1,0:T(8,128)(2,1)S(1)}, u32[]{:S(2)}, u32[]{:S(2)}) collective-permute-start(bf16[2,2,128,128]{3,2,1,0:T(8,128)(2,1)S(1)} %collective-permute-done.20.refs_13_), channel_id=1, source_target_pairs={{0,1},{1,0},{2,3},{3,2},{4,5},{5,4},{6,7},{7,6},{8,9},{9,8},{10,11... | collective-permute-start | bytes 393224 | tf_op jit(solution)/shard_map/ppermute | solution.py:85
  133.7 10.2 %all-to-all-start.6 = ((bf16[8,2,16,128]{3,2,1,0:T(8,128)(2,1)}), bf16[8,2,16,128]{3,2,1,0:T(8,128)(2,1)S(1)}, u32[]{:S(2)}, u32[]{:S(2)}) async-start(bf16[8,2,16,128]{3,2,1,0:T(8,128)(2,1)} %get-tuple-element.50), calls=%async_computation.6 | async-start | bytes 131072 | tf_op jit(solution)/shard_map/all_to_all | solution.py:120
  146.3 10.3 %all-to-all-start.7 = ((bf16[8,2,16,128]{3,2,1,0:T(8,128)(2,1)}), bf16[8,2,16,128]{3,2,1,0:T(8,128)(2,1)S(1)}, u32[]{:S(2)}, u32[]{:S(2)}) async-start(bf16[8,2,16,128]{3,2,1,0:T(8,128)(2,1)} %get-tuple-element.56), calls=%async_computation.7 | async-start | bytes 131072 | tf_op jit(solution)/shard_map/all_to_all | solution.py:120
  152.1 9.6 %collective-permute-start.29 = (f32[4,16,128]{2,1,0:T(8,128)S(1)}, f32[4,16,128]{2,1,0:T(8,128)S(1)}, u32[]{:S(2)}, u32[]{:S(2)}) collective-permute-start(f32[4,16,128]{2,1,0:T(8,128)S(1)} %copy-done.8), channel_id=1, source_target_pairs={{0,2},{1,3},{2,0},{3,1},{4,6},{5,7},{6,4},{7,5},{8,10},{9,11},{10,... | collective-permute-start | bytes 98312 | tf_op jit(solution)/shard_map/ppermute | solution.py:85
  (20 other events, 85.0 us)

commit v5 on v4

--- a/solution.py
+++ b/solution.py
@@ -284,8 +284,12 @@
             for n, s, m, l in [(n, s, *key) for n, keys in fixed.items() for s, key in enumerate(keys)]:
                 total = None
                 for q, blocks in enumerate(groups(r, (m, l + 1))):
-                    for j in range(width):
-                        term = times(blocks[j], r[ALL][column(r, q, j), l // 2])
+                    for j in range(0, width, 2):
+                        pair = range(j, min(j + 2, width))
+                        term = times(
+                            jnp.concatenate([blocks[i] for i in pair], 1),
+                            jnp.concatenate([r[ALL][column(r, q, i), l // 2] for i in pair], 0),
+                        )
                         total = term if total is None else total + term
                 for j in range(width):
                     raw = groups(r, (m, l))[0][j].astype(f32)

time: 165 us -> 165 us (level)
  no operation moved by 1% of the time
where the time goes in v5:
time: 165 us; the launch traced here: 163 us
  waiting for transfers between devices  46.7 us (28%)
  blocking collectives  42.4 us (26%)
  starting transfers between devices  39.4 us (24%)
  Pallas kernels  30.1 us (18%)
  local copies, waits for them, and re-layouts  4.03 us (2%)
    all_to_all x4, blocking collectives, swap(): return lax.all_to_all(value, 'row', 0, 0)  42.4 us
    pallas_call x14, Pallas kernels, kernel_call(): pl.pallas_call(kernel, grid=(1,), out_shape=[(pltpu.VMEM if len(s) > 2 el...  30.1 us
    all_to_all x4, waiting for transfers between devices, swap(): return lax.all_to_all(value, 'row', 0, 0)  19.1 us
    ppermute x7, waiting for transfers between devices, body_of(): lax.ppermute(v, 'row', [(r, r ^ d) for r in range(rows)])  16.1 us
    ppermute x24, starting transfers between devices, exchange(): return lax.ppermute(value, 'col', [(c, c ^ step) for c in range(size)])  14.4 us
    all_to_all x4, starting transfers between devices, swap(): return lax.all_to_all(value, 'row', 0, 0)  13.5 us
    ppermute x24, waiting for transfers between devices, exchange(): return lax.ppermute(value, 'col', [(c, c ^ step) for c in range(size)])  11.5 us
    ppermute x7, starting transfers between devices, body_of(): lax.ppermute(v, 'row', [(r, r ^ d) for r in range(rows)])  11.4 us
  transfers between devices with their start and end apart: 35, of which 10 were waited for; matrix products, arithmetic and copies ran while one was open for 0% of the time, Pallas kernels for 12%

profile of v5, /device:TPU:0, one launch (start us, length us, event | category | flops | bytes accessed | tf_op | source)
XLA Modules:
  0.0 163.5 jit_solution(13653657685243109625)
XLA Ops:
  2.4 2.5 %shard_map.61 = (bf16[5,2,128,128]{3,2,1,0:T(8,128)(2,1)}, bf16[9,2,128,128]{3,2,1,0:T(8,128)(2,1)}, bf16[2,128,256]{2,1,0:T(8,128)(2,1)}) custom-call(s32[1,2,15]{2,1,0:T(2,128)} %bitcast.10, bf16[15,1,2,128,128]{4,3,2,1,0:T(8,128)(2,1)} %refs_1_.7, bf16[8,16,128]{2,1,0:T(8,128)(2,1)} %get-tuple-element.31.refs_2_, f32[6,1,128,128]{3,2,1,0:T(8,128)} %refs_3_.7, ...), custom_call_target="tpu_custom_call" | custom-call | tf_op jit(solution)/shard_map/pallas_call | solution.py:72
  4.9 3.0 %collective-permute-start.7 = (bf16[9,2,128,128]{3,2,1,0:T(8,128)(2,1)}, bf16[9,2,128,128]{3,2,1,0:T(8,128)(2,1)S(1)}, u32[]{:S(2)}, u32[]{:S(2)}) collective-permute-start(bf16[9,2,128,128]{3,2,1,0:T(8,128)(2,1)} %get-tuple-element.37.refs_7_.refs_11_.refs_12_.refs_13_.refs_8_.refs_14_.refs_15_.refs_17_.refs, ...), channel_id=1, source_target_pairs={{0,2},{1,3},{2,0},{3,1},{4,6},{5,7},{6,4},{7,5},{8,10},{9,11},{10,... | collective-permute-start | bytes 1769480 | tf_op jit(solution)/shard_map/ppermute | solution.py:85
  11.4 10.8 %collective-permute-done.7.refs_9_.refs_10_.refs_19_.refs_7_ = bf16[9,2,128,128]{3,2,1,0:T(8,128)(2,1)S(1)} collective-permute-done((bf16[9,2,128,128]{3,2,1,0:T(8,128)(2,1)}, bf16[9,2,128,128]{3,2,1,0:T(8,128)(2,1)S(1)}, u32[]{:S(2)}, u32[]{:S(2)}) %collective-permute-start.7) | collective-permute-done | bytes 589856 | tf_op jit(solution)/shard_map/ppermute | solution.py:85
  22.3 3.1 %collective-permute-start.12 = (bf16[2,128,256]{2,1,0:T(8,128)(2,1)}, bf16[2,128,256]{2,1,0:T(8,128)(2,1)S(1)}, u32[]{:S(2)}, u32[]{:S(2)}) collective-permute-start(bf16[2,128,256]{2,1,0:T(8,128)(2,1)} %get-tuple-element.48.refs_2_), channel_id=1, source_target_pairs={{0,16},{4,20},{8,24},{12,28},{16,0},{20,4},{24,8},{28,12},{1,17},{... | collective-permute-start | bytes 393224 | tf_op jit(solution)/shard_map/ppermute | solution.py:238
  26.8 5.7 %collective-permute-done.12.refs_3_ = bf16[2,128,256]{2,1,0:T(8,128)(2,1)S(1)} collective-permute-done((bf16[2,128,256]{2,1,0:T(8,128)(2,1)}, bf16[2,128,256]{2,1,0:T(8,128)(2,1)S(1)}, u32[]{:S(2)}, u32[]{:S(2)}) %collective-permute-start.12) | collective-permute-done | bytes 131104 | tf_op jit(solution)/shard_map/ppermute | solution.py:238
  34.6 3.3 %collective-permute-done.16.refs_7_ = bf16[2,128,256]{2,1,0:T(8,128)(2,1)S(1)} collective-permute-done((bf16[2,128,256]{2,1,0:T(8,128)(2,1)S(1)}, bf16[2,128,256]{2,1,0:T(8,128)(2,1)S(1)}, u32[]{:S(2)}, u32[]{:S(2)}) %collective-permute-start.16) | collective-permute-done | bytes 131104 | tf_op jit(solution)/shard_map/ppermute | solution.py:238
  39.5 4.0 %collective-permute-done.14.refs_5_ = bf16[2,128,256]{2,1,0:T(8,128)(2,1)S(1)} collective-permute-done((bf16[2,128,256]{2,1,0:T(8,128)(2,1)S(1)}, bf16[2,128,256]{2,1,0:T(8,128)(2,1)S(1)}, u32[]{:S(2)}, u32[]{:S(2)}) %collective-permute-start.14) | collective-permute-done | bytes 131104 | tf_op jit(solution)/shard_map/ppermute | solution.py:238
  45.4 3.2 %collective-permute-done.18.refs_9_ = bf16[2,128,256]{2,1,0:T(8,128)(2,1)} collective-permute-done((bf16[2,128,256]{2,1,0:T(8,128)(2,1)S(1)}, bf16[2,128,256]{2,1,0:T(8,128)(2,1)}, u32[]{:S(2)}, u32[]{:S(2)}) %collective-permute-start.18) | collective-permute-done | bytes 131104 | tf_op jit(solution)/shard_map/ppermute | solution.py:238
  51.3 2.6 %shard_map.67 = (bf16[2,2,128,128]{3,2,1,0:T(8,128)(2,1)}, bf16[4,2,128,128]{3,2,1,0:T(8,128)(2,1)}) custom-call(s32[1]{0:T(128)} %bitcast.refs_0_, s32[1]{0:T(128)} %bitcast.4.refs_1_, bf16[2,128,256]{2,1,0:T(8,128)(2,1)S(1)} %copy-done.1, bf16[2,128,256]{2,1,0:T(8,128)(2,1)S(1)} %collective-permute-done.12.refs_3_, ...), custom_call_target="tpu_custom_call" | custom-call | tf_op jit(solution)/shard_map/pallas_call | solution.py:72
  57.0 12.6 %all_to_all.40.refs_3_ = bf16[8,16,128]{2,1,0:T(8,128)(2,1)S(1)} all-to-all(bf16[8,16,128]{2,1,0:T(8,128)(2,1)S(1)} %copy-done.6), channel_id=1, replica_groups=mesh['row'=8,'col'=4] {'row'}, dimensions={0} | all-to-all | bytes 65536 | tf_op jit(solution)/shard_map/all_to_all | solution.py:120
  71.6 3.3 %all-to-all-start.1 = ((bf16[8,16,128]{2,1,0:T(8,128)(2,1)}), bf16[8,16,128]{2,1,0:T(8,128)(2,1)S(1)}, u32[]{:S(2)}, u32[]{:S(2)}) async-start(bf16[8,16,128]{2,1,0:T(8,128)(2,1)} %get-tuple-element.33), calls=%async_computation.1 | async-start | bytes 65536 | tf_op jit(solution)/shard_map/all_to_all | solution.py:120
  75.5 6.0 %all-to-all-done.1.refs_4_ = bf16[8,16,128]{2,1,0:T(8,128)(2,1)S(1)} async-done(((bf16[8,16,128]{2,1,0:T(8,128)(2,1)}), bf16[8,16,128]{2,1,0:T(8,128)(2,1)S(1)}, u32[]{:S(2)}, u32[]{:S(2)}) %all-to-all-start.1) | async-done | bytes 32800 | tf_op jit(solution)/shard_map/all_to_all | solution.py:120
  83.8 9.9 %all_to_all.41.refs_5_ = bf16[8,16,128]{2,1,0:T(8,128)(2,1)S(1)} all-to-all(bf16[8,16,128]{2,1,0:T(8,128)(2,1)} %get-tuple-element.35), channel_id=1, replica_groups=mesh['row'=8,'col'=4] {'row'}, dimensions={0} | all-to-all | bytes 65536 | tf_op jit(solution)/shard_map/all_to_all | solution.py:120
  96.0 3.3 %all-to-all-start.3 = ((bf16[8,16,128]{2,1,0:T(8,128)(2,1)}), bf16[8,16,128]{2,1,0:T(8,128)(2,1)S(1)}, u32[]{:S(2)}, u32[]{:S(2)}) async-start(bf16[8,16,128]{2,1,0:T(8,128)(2,1)} %get-tuple-element.36), calls=%async_computation.3 | async-start | bytes 65536 | tf_op jit(solution)/shard_map/all_to_all | solution.py:120
  100.4 5.5 %all-to-all-done.3.refs_6_ = bf16[8,16,128]{2,1,0:T(8,128)(2,1)S(1)} async-done(((bf16[8,16,128]{2,1,0:T(8,128)(2,1)}), bf16[8,16,128]{2,1,0:T(8,128)(2,1)S(1)}, u32[]{:S(2)}, u32[]{:S(2)}) %all-to-all-start.3) | async-done | bytes 32800 | tf_op jit(solution)/shard_map/all_to_all | solution.py:120
  106.0 2.4 %shard_map.64 = (f32[16,128]{1,0:T(8,128)}, bf16[8,16,128]{2,1,0:T(8,128)(2,1)}) custom-call(s32[1]{0:T(128)} %bitcast.refs_0_, f32[6,1,64,128]{3,2,1,0:T(8,128)} %refs_1_.11, f32[6,1,128,128]{3,2,1,0:T(8,128)} %refs_3_.7, bf16[8,16,128]{2,1,0:T(8,128)(2,1)S(1)} %all_to_all.40.refs_3_, bf16[8,16,128]{2,1,0:T(8,128)(2,1)S(1)} %all-to-all-done.1.refs_4_, ...), custom_call_target="tpu_custom_call" | custom-call | tf_op jit(solution)/shard_map/pallas_call | solution.py:72
  108.3 9.9 %all_to_all.42.refs_7_ = bf16[8,16,128]{2,1,0:T(8,128)(2,1)S(1)} all-to-all(bf16[8,16,128]{2,1,0:T(8,128)(2,1)} %get-tuple-element.38), channel_id=1, replica_groups=mesh['row'=8,'col'=4] {'row'}, dimensions={0} | all-to-all | bytes 65536 | tf_op jit(solution)/shard_map/all_to_all | solution.py:120
  118.3 3.0 %shard_map.65 = (f32[6,16,128]{2,1,0:T(8,128)}, f32[16,128]{1,0:T(8,128)}, bf16[16,128]{1,0:T(8,128)(2,1)}, bf16[8,1,16,128]{3,2,1,0:T(8,128)(2,1)}) custom-call(s32[1]{0:T(128)} %bitcast.refs_0_, f32[6,1,64,128]{3,2,1,0:T(8,128)} %refs_1_.11, f32[6,1,128,128]{3,2,1,0:T(8,128)} %refs_3_.7, bf16[8,16,128]{2,1,0:T(8,128)(2,1)S(1)} %all_to_all.40.refs_3_, ...), custom_call_target="tpu_custom_call" | custom-call | tf_op jit(solution)/shard_map/pallas_call | solution.py:72
  121.2 9.9 %all_to_all.43.refs_1_ = bf16[8,1,16,128]{3,2,1,0:T(8,128)(2,1)S(1)} all-to-all(bf16[8,1,16,128]{3,2,1,0:T(8,128)(2,1)} %get-tuple-element.46), channel_id=1, replica_groups=mesh['row'=8,'col'=4] {'row'}, dimensions={0} | all-to-all | bytes 65536 | tf_op jit(solution)/shard_map/all_to_all | solution.py:120
  133.4 3.4 %all-to-all-start.6 = ((bf16[8,2,16,128]{3,2,1,0:T(8,128)(2,1)}), bf16[8,2,16,128]{3,2,1,0:T(8,128)(2,1)S(1)}, u32[]{:S(2)}, u32[]{:S(2)}) async-start(bf16[8,2,16,128]{3,2,1,0:T(8,128)(2,1)} %get-tuple-element.50), calls=%async_computation.6 | async-start | bytes 131072 | tf_op jit(solution)/shard_map/all_to_all | solution.py:120
  139.1 4.5 %all-to-all-done.6.refs_1_ = bf16[8,2,16,128]{3,2,1,0:T(8,128)(2,1)S(1)} async-done(((bf16[8,2,16,128]{3,2,1,0:T(8,128)(2,1)}), bf16[8,2,16,128]{3,2,1,0:T(8,128)(2,1)S(1)}, u32[]{:S(2)}, u32[]{:S(2)}) %all-to-all-start.6) | async-done | bytes 65568 | tf_op jit(solution)/shard_map/all_to_all | solution.py:120
  143.6 2.3 %shard_map.70 = (bf16[16,128]{1,0:T(8,128)(2,1)}, bf16[16,128]{1,0:T(8,128)(2,1)}, bf16[8,2,16,128]{3,2,1,0:T(8,128)(2,1)}, f32[4,16,128]{2,1,0:T(8,128)}) custom-call(s32[1]{0:T(128)} %bitcast.refs_0_, bf16[8,2,16,128]{3,2,1,0:T(8,128)(2,1)S(1)} %all-to-all-done.6.refs_1_, f32[6,1,128,128]{3,2,1,0:T(8,128)} %refs_3_.7, f32[6,1,128,128]{3,2,1,0:T(8,128)} %refs_3_.7, ...), custom_call_target="tpu_custom_call" | custom-call | tf_op jit(solution)/shard_map/pallas_call | solution.py:72
  145.9 3.5 %all-to-all-start.7 = ((bf16[8,2,16,128]{3,2,1,0:T(8,128)(2,1)}), bf16[8,2,16,128]{3,2,1,0:T(8,128)(2,1)S(1)}, u32[]{:S(2)}, u32[]{:S(2)}) async-start(bf16[8,2,16,128]{3,2,1,0:T(8,128)(2,1)} %get-tuple-element.56), calls=%async_computation.7 | async-start | bytes 131072 | tf_op jit(solution)/shard_map/all_to_all | solution.py:120
  153.2 3.0 %all-to-all-done.7.refs_1_ = bf16[8,2,16,128]{3,2,1,0:T(8,128)(2,1)S(1)} async-done(((bf16[8,2,16,128]{3,2,1,0:T(8,128)(2,1)}), bf16[8,2,16,128]{3,2,1,0:T(8,128)(2,1)S(1)}, u32[]{:S(2)}, u32[]{:S(2)}) %all-to-all-start.7) | async-done | bytes 65568 | tf_op jit(solution)/shard_map/all_to_all | solution.py:120
  (82 shorter events, 41.9 us)
Async XLA Ops:
  4.9 17.4 %collective-permute-start.7 = (bf16[9,2,128,128]{3,2,1,0:T(8,128)(2,1)}, bf16[9,2,128,128]{3,2,1,0:T(8,128)(2,1)S(1)}, u32[]{:S(2)}, u32[]{:S(2)}) collective-permute-start(bf16[9,2,128,128]{3,2,1,0:T(8,128)(2,1)} %get-tuple-element.37.refs_7_.refs_11_.refs_12_.refs_13_.refs_8_.refs_14_.refs_15_.refs_17_.refs, ...), channel_id=1, source_target_pairs={{0,2},{1,3},{2,0},{3,1},{4,6},{5,7},{6,4},{7,5},{8,10},{9,11},{10,... | collective-permute-start | bytes 1769480 | tf_op jit(solution)/shard_map/ppermute | solution.py:85
  7.9 14.4 %collective-permute-start.15 = (bf16[2,128,256]{2,1,0:T(8,128)(2,1)}, bf16[2,128,256]{2,1,0:T(8,128)(2,1)S(1)}, u32[]{:S(2)}, u32[]{:S(2)}) collective-permute-start(bf16[2,128,256]{2,1,0:T(8,128)(2,1)} %get-tuple-element.48.refs_2_), channel_id=1, source_target_pairs={{0,4},{4,0},{8,12},{12,8},{16,20},{20,16},{24,28},{28,24},{1,5},{5... | collective-permute-start | bytes 393224 | tf_op jit(solution)/shard_map/ppermute | solution.py:238
  9.4 24.7 %collective-permute-start.4 = (bf16[5,2,128,128]{3,2,1,0:T(8,128)(2,1)}, bf16[5,2,128,128]{3,2,1,0:T(8,128)(2,1)S(1)}, u32[]{:S(2)}, u32[]{:S(2)}) collective-permute-start(bf16[5,2,128,128]{3,2,1,0:T(8,128)(2,1)} %get-tuple-element.34.refs_5_.refs_9_.refs_6_.refs_10_.refs_11_.refs_14_.refs_15_.refs_16_.refs_7_), channel_id=1, source_target_pairs={{0,2},{1,3},{2,0},{3,1},{4,6},{5,7},{6,4},{7,5},{8,10},{9,11},{10,... | collective-permute-start | bytes 983048 | tf_op jit(solution)/shard_map/ppermute | solution.py:85
  9.9 15.5 %collective-permute-start.13 = (bf16[2,128,256]{2,1,0:T(8,128)(2,1)}, bf16[2,128,256]{2,1,0:T(8,128)(2,1)S(1)}, u32[]{:S(2)}, u32[]{:S(2)}) collective-permute-start(bf16[2,128,256]{2,1,0:T(8,128)(2,1)} %get-tuple-element.48.refs_2_), channel_id=1, source_target_pairs={{0,8},{4,12},{8,0},{12,4},{16,24},{20,28},{24,16},{28,20},{1,9},{5... | collective-permute-start | bytes 393224 | tf_op jit(solution)/shard_map/ppermute | solution.py:238
  11.4 37.1 %collective-permute-start.6 = (bf16[9,2,128,128]{3,2,1,0:T(8,128)(2,1)}, bf16[9,2,128,128]{3,2,1,0:T(8,128)(2,1)S(1)}, u32[]{:S(2)}, u32[]{:S(2)}) collective-permute-start(bf16[9,2,128,128]{3,2,1,0:T(8,128)(2,1)} %get-tuple-element.37.refs_7_.refs_11_.refs_12_.refs_13_.refs_8_.refs_14_.refs_15_.refs_17_.refs, ...), channel_id=1, source_target_pairs={{0,1},{1,0},{2,3},{3,2},{4,5},{5,4},{6,7},{7,6},{8,9},{9,8},{10,11... | collective-permute-start | bytes 1769480 | tf_op jit(solution)/shard_map/ppermute | solution.py:85
  22.2 26.3 %collective-permute-start.8 = (bf16[9,2,128,128]{3,2,1,0:T(8,128)(2,1)S(1)}, bf16[9,2,128,128]{3,2,1,0:T(8,128)(2,1)S(1)}, u32[]{:S(2)}, u32[]{:S(2)}) collective-permute-start(bf16[9,2,128,128]{3,2,1,0:T(8,128)(2,1)S(1)} %collective-permute-done.7.refs_9_.refs_10_.refs_19_.refs_7_), channel_id=1, source_target_pairs={{0,1},{1,0},{2,3},{3,2},{4,5},{5,4},{6,7},{7,6},{8,9},{9,8},{10,11... | collective-permute-start | bytes 1769480 | tf_op jit(solution)/shard_map/ppermute | solution.py:85
  22.3 10.3 %collective-permute-start.12 = (bf16[2,128,256]{2,1,0:T(8,128)(2,1)}, bf16[2,128,256]{2,1,0:T(8,128)(2,1)S(1)}, u32[]{:S(2)}, u32[]{:S(2)}) collective-permute-start(bf16[2,128,256]{2,1,0:T(8,128)(2,1)} %get-tuple-element.48.refs_2_), channel_id=1, source_target_pairs={{0,16},{4,20},{8,24},{12,28},{16,0},{20,4},{24,8},{28,12},{1,17},{... | collective-permute-start | bytes 393224 | tf_op jit(solution)/shard_map/ppermute | solution.py:238
  25.4 8.7 %collective-permute-start.17 = (bf16[2,128,256]{2,1,0:T(8,128)(2,1)S(1)}, bf16[2,128,256]{2,1,0:T(8,128)(2,1)S(1)}, u32[]{:S(2)}, u32[]{:S(2)}) collective-permute-start(bf16[2,128,256]{2,1,0:T(8,128)(2,1)S(1)} %collective-permute-done.13.refs_4_), channel_id=1, source_target_pairs={{0,4},{4,0},{8,12},{12,8},{16,20},{20,16},{24,28},{28,24},{1,5},{5... | collective-permute-start | bytes 393224 | tf_op jit(solution)/shard_map/ppermute | solution.py:238
  34.1 11.3 %collective-permute-start.3 = (bf16[5,2,128,128]{3,2,1,0:T(8,128)(2,1)}, bf16[5,2,128,128]{3,2,1,0:T(8,128)(2,1)S(1)}, u32[]{:S(2)}, u32[]{:S(2)}) collective-permute-start(bf16[5,2,128,128]{3,2,1,0:T(8,128)(2,1)} %get-tuple-element.34.refs_5_.refs_9_.refs_6_.refs_10_.refs_11_.refs_14_.refs_15_.refs_16_.refs_7_), channel_id=1, source_target_pairs={{0,1},{1,0},{2,3},{3,2},{4,5},{5,4},{6,7},{7,6},{8,9},{9,8},{10,11... | collective-permute-start | bytes 983048 | tf_op jit(solution)/shard_map/ppermute | solution.py:85
  34.1 14.5 %collective-permute-start.5 = (bf16[5,2,128,128]{3,2,1,0:T(8,128)(2,1)S(1)}, bf16[5,2,128,128]{3,2,1,0:T(8,128)(2,1)S(1)}, u32[]{:S(2)}, u32[]{:S(2)}) collective-permute-start(bf16[5,2,128,128]{3,2,1,0:T(8,128)(2,1)S(1)} %collective-permute-done.4.refs_7_.refs_8_.refs_12_.refs_17_.refs_9_), channel_id=1, source_target_pairs={{0,1},{1,0},{2,3},{3,2},{4,5},{5,4},{6,7},{7,6},{8,9},{9,8},{10,11... | collective-permute-start | bytes 983048 | tf_op jit(solution)/shard_map/ppermute | solution.py:85
  53.9 45.5 %collective-permute-start.23 = (bf16[4,2,128,128]{3,2,1,0:T(8,128)(2,1)}, bf16[4,2,128,128]{3,2,1,0:T(8,128)(2,1)}, u32[]{:S(2)}, u32[]{:S(2)}) collective-permute-start(bf16[4,2,128,128]{3,2,1,0:T(8,128)(2,1)} %get-tuple-element.52.refs_10_.refs_14_.refs_12_.refs_16_), channel_id=1, source_target_pairs={{0,2},{1,3},{2,0},{3,1},{4,6},{5,7},{6,4},{7,5},{8,10},{9,11},{10,... | collective-permute-start | bytes 786440 | tf_op jit(solution)/shard_map/ppermute | solution.py:85
  55.2 14.5 %collective-permute-start.2 = (bf16[1,2,128,128]{3,2,1,0:T(8,128)(2,1)S(1)}, bf16[1,2,128,128]{3,2,1,0:T(8,128)(2,1)S(1)}, u32[]{:S(2)}, u32[]{:S(2)}) collective-permute-start(bf16[1,2,128,128]{3,2,1,0:T(8,128)(2,1)S(1)} %copy-done), channel_id=1, source_target_pairs={{0,3},{1,2},{2,1},{3,0},{4,7},{5,6},{6,5},{7,4},{8,11},{9,10},{10,... | collective-permute-start | bytes 196616 | tf_op jit(solution)/shard_map/ppermute | solution.py:85
  55.2 14.5 %collective-permute-start.1 = (bf16[1,2,128,128]{3,2,1,0:T(8,128)(2,1)S(1)}, bf16[1,2,128,128]{3,2,1,0:T(8,128)(2,1)S(1)}, u32[]{:S(2)}, u32[]{:S(2)}) collective-permute-start(bf16[1,2,128,128]{3,2,1,0:T(8,128)(2,1)S(1)} %copy-done), channel_id=1, source_target_pairs={{0,2},{1,3},{2,0},{3,1},{4,6},{5,7},{6,4},{7,5},{8,10},{9,11},{10,... | collective-permute-start | bytes 196616 | tf_op jit(solution)/shard_map/ppermute | solution.py:85
  55.9 13.7 %collective-permute-start = (bf16[1,2,128,128]{3,2,1,0:T(8,128)(2,1)S(1)}, bf16[1,2,128,128]{3,2,1,0:T(8,128)(2,1)S(1)}, u32[]{:S(2)}, u32[]{:S(2)}) collective-permute-start(bf16[1,2,128,128]{3,2,1,0:T(8,128)(2,1)S(1)} %copy-done), channel_id=1, source_target_pairs={{0,1},{1,0},{2,3},{3,2},{4,5},{5,4},{6,7},{7,6},{8,9},{9,8},{10,11... | collective-permute-start | bytes 196616 | tf_op jit(solution)/shard_map/ppermute | solution.py:85
  71.6 10.0 %all-to-all-start.1 = ((bf16[8,16,128]{2,1,0:T(8,128)(2,1)}), bf16[8,16,128]{2,1,0:T(8,128)(2,1)S(1)}, u32[]{:S(2)}, u32[]{:S(2)}) async-start(bf16[8,16,128]{2,1,0:T(8,128)(2,1)} %get-tuple-element.33), calls=%async_computation.1 | async-start | bytes 65536 | tf_op jit(solution)/shard_map/all_to_all | solution.py:120
  75.0 25.0 %collective-permute-start.20 = (bf16[2,2,128,128]{3,2,1,0:T(8,128)(2,1)}, bf16[2,2,128,128]{3,2,1,0:T(8,128)(2,1)S(1)}, u32[]{:S(2)}, u32[]{:S(2)}) collective-permute-start(bf16[2,2,128,128]{3,2,1,0:T(8,128)(2,1)} %get-tuple-element.49.refs_11_.refs_20_), channel_id=1, source_target_pairs={{0,2},{1,3},{2,0},{3,1},{4,6},{5,7},{6,4},{7,5},{8,10},{9,11},{10,... | collective-permute-start | bytes 393224 | tf_op jit(solution)/shard_map/ppermute | solution.py:85
  96.0 10.0 %all-to-all-start.3 = ((bf16[8,16,128]{2,1,0:T(8,128)(2,1)}), bf16[8,16,128]{2,1,0:T(8,128)(2,1)S(1)}, u32[]{:S(2)}, u32[]{:S(2)}) async-start(bf16[8,16,128]{2,1,0:T(8,128)(2,1)} %get-tuple-element.36), calls=%async_computation.3 | async-start | bytes 65536 | tf_op jit(solution)/shard_map/all_to_all | solution.py:120
  99.3 37.4 %collective-permute-start.22 = (bf16[4,2,128,128]{3,2,1,0:T(8,128)(2,1)}, bf16[4,2,128,128]{3,2,1,0:T(8,128)(2,1)}, u32[]{:S(2)}, u32[]{:S(2)}) collective-permute-start(bf16[4,2,128,128]{3,2,1,0:T(8,128)(2,1)} %get-tuple-element.52.refs_10_.refs_14_.refs_12_.refs_16_), channel_id=1, source_target_pairs={{0,1},{1,0},{2,3},{3,2},{4,5},{5,4},{6,7},{7,6},{8,9},{9,8},{10,11... | collective-permute-start | bytes 786440 | tf_op jit(solution)/shard_map/ppermute | solution.py:85
  99.4 37.3 %collective-permute-start.24 = (bf16[4,2,128,128]{3,2,1,0:T(8,128)(2,1)}, bf16[4,2,128,128]{3,2,1,0:T(8,128)(2,1)}, u32[]{:S(2)}, u32[]{:S(2)}) collective-permute-start(bf16[4,2,128,128]{3,2,1,0:T(8,128)(2,1)} %collective-permute-done.23.refs_12_.refs_16_.refs_14_.refs_18_), channel_id=1, source_target_pairs={{0,1},{1,0},{2,3},{3,2},{4,5},{5,4},{6,7},{7,6},{8,9},{9,8},{10,11... | collective-permute-start | bytes 786440 | tf_op jit(solution)/shard_map/ppermute | solution.py:85
  99.9 31.3 %collective-permute-start.19 = (bf16[2,2,128,128]{3,2,1,0:T(8,128)(2,1)}, bf16[2,2,128,128]{3,2,1,0:T(8,128)(2,1)S(1)}, u32[]{:S(2)}, u32[]{:S(2)}) collective-permute-start(bf16[2,2,128,128]{3,2,1,0:T(8,128)(2,1)} %get-tuple-element.49.refs_11_.refs_20_), channel_id=1, source_target_pairs={{0,1},{1,0},{2,3},{3,2},{4,5},{5,4},{6,7},{7,6},{8,9},{9,8},{10,11... | collective-permute-start | bytes 393224 | tf_op jit(solution)/shard_map/ppermute | solution.py:85
  100.0 31.2 %collective-permute-start.21 = (bf16[2,2,128,128]{3,2,1,0:T(8,128)(2,1)S(1)}, bf16[2,2,128,128]{3,2,1,0:T(8,128)(2,1)S(1)}, u32[]{:S(2)}, u32[]{:S(2)}) collective-permute-start(bf16[2,2,128,128]{3,2,1,0:T(8,128)(2,1)S(1)} %collective-permute-done.20.refs_13_), channel_id=1, source_target_pairs={{0,1},{1,0},{2,3},{3,2},{4,5},{5,4},{6,7},{7,6},{8,9},{9,8},{10,11... | collective-permute-start | bytes 393224 | tf_op jit(solution)/shard_map/ppermute | solution.py:85
  133.4 10.2 %all-to-all-start.6 = ((bf16[8,2,16,128]{3,2,1,0:T(8,128)(2,1)}), bf16[8,2,16,128]{3,2,1,0:T(8,128)(2,1)S(1)}, u32[]{:S(2)}, u32[]{:S(2)}) async-start(bf16[8,2,16,128]{3,2,1,0:T(8,128)(2,1)} %get-tuple-element.50), calls=%async_computation.6 | async-start | bytes 131072 | tf_op jit(solution)/shard_map/all_to_all | solution.py:120
  145.9 10.3 %all-to-all-start.7 = ((bf16[8,2,16,128]{3,2,1,0:T(8,128)(2,1)}), bf16[8,2,16,128]{3,2,1,0:T(8,128)(2,1)S(1)}, u32[]{:S(2)}, u32[]{:S(2)}) async-start(bf16[8,2,16,128]{3,2,1,0:T(8,128)(2,1)} %get-tuple-element.56), calls=%async_computation.7 | async-start | bytes 131072 | tf_op jit(solution)/shard_map/all_to_all | solution.py:120
  151.7 9.6 %collective-permute-start.29 = (f32[4,16,128]{2,1,0:T(8,128)S(1)}, f32[4,16,128]{2,1,0:T(8,128)S(1)}, u32[]{:S(2)}, u32[]{:S(2)}) collective-permute-start(f32[4,16,128]{2,1,0:T(8,128)S(1)} %copy-done.8), channel_id=1, source_target_pairs={{0,2},{1,3},{2,0},{3,1},{4,6},{5,7},{6,4},{7,5},{8,10},{9,11},{10,... | collective-permute-start | bytes 98312 | tf_op jit(solution)/shard_map/ppermute | solution.py:85
  (20 other events, 84.3 us)

commit v6 on v5

--- a/solution.py
+++ b/solution.py
@@ -7,7 +7,6 @@
 from jax.experimental.pallas import tpu as pltpu
 from jax.sharding import PartitionSpec as P
 
-FINE = lax.Precision.HIGHEST
 MERGE_BYTES = 24 << 20
 f32, bf16 = jnp.float32, jnp.bfloat16
 ANYWHERE = -2
@@ -17,21 +16,29 @@
     return higher * (higher - 1) // 2 + lower_level
 
 
-def times_transposed(v, g, precision=None):
-    return lax.dot_general(
-        v, g, (((1,), (1,)), ((), ())), precision=precision, preferred_element_type=f32
-    )
-
-
-def times(v, g, precision=None):
-    return lax.dot_general(
-        v, g, (((1,), (0,)), ((), ())), precision=precision, preferred_element_type=f32
-    )
+def times_transposed(v, g):
+    return lax.dot_general(v, g, (((1,), (1,)), ((), ())), preferred_element_type=f32)
+
+
+def times(v, g):
+    return lax.dot_general(v, g, (((1,), (0,)), ((), ())), preferred_element_type=f32)
+
+
+def halves(d):
+    high = d.astype(bf16)
+    return high, (d - high.astype(f32)).astype(bf16)
+
+
+def fine(product, v, d):
+    (v_high, v_low), (d_high, d_low) = halves(v), halves(d)
+    rows = v.shape[0]
+    both = jnp.concatenate([v_high, v_low], 0)
+    large, small = product(both, d_high), product(both, d_low)
+    return large[:rows] + (large[rows:] + (small[:rows] + small[rows:]))
 
 
 def split_product(d, g):
-    high = d.astype(bf16)
-    low = (d - high.astype(f32)).astype(bf16)
+    high, low = halves(d)
     return times(high, g) + times(low, g)
 
 
@@ -195,7 +202,7 @@
         return jnp.where(r[PATTERN][0, j, p] != 0, value, jnp.zeros_like(value))
 
     def first_body(r):
-        value = times_transposed(own(r, 0), r[INV, 0][0, 0], FINE)
+        value = fine(times_transposed, own(r, 0), r[INV, 0][0, 0])
         r[X][...] = value
         send_all(r, value.astype(bf16))
         for j in range(width):
@@ -245,7 +252,7 @@
 
     for m in range(1, levels):
         def solve_body(r):
-            value = times_transposed(own(r, m) - sum_over(r, m, range(m)), r[INV, m][0, 0], FINE)
+            value = fine(times_transposed, own(r, m) - sum_over(r, m, range(m)), r[INV, m][0, 0])
             if m < top:
                 r[X][...] = value
                 send_all(r, value.astype(bf16))
@@ -253,7 +260,7 @@
             for l in range(top):
                 r[STACK][l] = r[X, l][...]
             r[STACK][top] = value
-            result = times(value, r[INV, m][0, 0], FINE)
+            result = fine(times, value, r[INV, m][0, 0])
             r[Y][...] = result
             r[V][...] = result.astype(bf16)
             spread_sums(r, [(result.astype(bf16), (m, m - 1))], r[SEND], 0)
@@ -329,7 +336,7 @@
                 values = {m: r[V, m][...] for m in upper}
                 terms = {l: terms_for(l, values) for l in targets}
                 for m in odds:
-                    own_part = times(r[X, m][...], r[INV, m][0, 0], FINE).astype(bf16)
+                    own_part = fine(times, r[X, m][...], r[INV, m][0, 0]).astype(bf16)
                     terms[m - 1].append((own_part, (m, m - 1)))
                 return terms
 
@@ -349,7 +356,7 @@
                 total = r[ARRIVED][0, slot].astype(f32)
                 for k in range(1, rows):
                     total = total + r[ARRIVED][k, slot].astype(f32)
-                result = times(r[X, m][...] - total, r[INV, m][0, 0], FINE)
+                result = fine(times, r[X, m][...] - total, r[INV, m][0, 0])
                 if not targets:
                     r[OUT][slot] = result
                     continue

time: 165 us -> 164 us (level)
  transfers between devices with their start and end apart: 35 -> 35, of which waited for: 10 -> 10; matrix products, arithmetic and copies ran while one was open for 0% -> 0% of each run, Pallas kernels for 12% -> 11%
where the time goes in v6:
time: 164 us; the launch traced here: 162 us
  waiting for transfers between devices  46.9 us (29%)
  blocking collectives  42.4 us (26%)
  starting transfers between devices  39.4 us (24%)
  Pallas kernels  28.7 us (18%)
  local copies, waits for them, and re-layouts  4.03 us (2%)
    all_to_all x4, blocking collectives, swap(): return lax.all_to_all(value, 'row', 0, 0)  42.4 us
    pallas_call x14, Pallas kernels, kernel_call(): pl.pallas_call(kernel, grid=(1,), out_shape=[(pltpu.VMEM if len(s) > 2 el...  28.7 us
    all_to_all x4, waiting for transfers between devices, swap(): return lax.all_to_all(value, 'row', 0, 0)  19.2 us
    ppermute x7, waiting for transfers between devices, body_of(): lax.ppermute(v, 'row', [(r, r ^ d) for r in range(rows)])  16.1 us
    ppermute x24, starting transfers between devices, exchange(): return lax.ppermute(value, 'col', [(c, c ^ step) for c in range(size)])  14.4 us
    all_to_all x4, starting transfers between devices, swap(): return lax.all_to_all(value, 'row', 0, 0)  13.5 us
    ppermute x24, waiting for transfers between devices, exchange(): return lax.ppermute(value, 'col', [(c, c ^ step) for c in range(size)])  11.5 us
    ppermute x7, starting transfers between devices, body_of(): lax.ppermute(v, 'row', [(r, r ^ d) for r in range(rows)])  11.4 us
  transfers between devices with their start and end apart: 35, of which 10 were waited for; matrix products, arithmetic and copies ran while one was open for 0% of the time, Pallas kernels for 11%

profile of v6, /device:TPU:0, one launch (start us, length us, event | category | flops | bytes accessed | tf_op | source)
XLA Modules:
  0.0 162.2 jit_solution(15891225716858793456)
XLA Ops:
  2.3 2.5 %shard_map.61 = (bf16[5,2,128,128]{3,2,1,0:T(8,128)(2,1)}, bf16[9,2,128,128]{3,2,1,0:T(8,128)(2,1)}, bf16[2,128,256]{2,1,0:T(8,128)(2,1)}) custom-call(s32[1,2,15]{2,1,0:T(2,128)} %bitcast.10, bf16[15,1,2,128,128]{4,3,2,1,0:T(8,128)(2,1)} %refs_1_.7, bf16[8,16,128]{2,1,0:T(8,128)(2,1)} %get-tuple-element.31.refs_2_, f32[6,1,128,128]{3,2,1,0:T(8,128)} %refs_3_.7, ...), custom_call_target="tpu_custom_call" | custom-call | tf_op jit(solution)/shard_map/pallas_call | solution.py:79
  4.8 3.0 %collective-permute-start.7 = (bf16[9,2,128,128]{3,2,1,0:T(8,128)(2,1)}, bf16[9,2,128,128]{3,2,1,0:T(8,128)(2,1)S(1)}, u32[]{:S(2)}, u32[]{:S(2)}) collective-permute-start(bf16[9,2,128,128]{3,2,1,0:T(8,128)(2,1)} %get-tuple-element.37.refs_7_.refs_11_.refs_12_.refs_13_.refs_8_.refs_14_.refs_15_.refs_17_.refs, ...), channel_id=1, source_target_pairs={{0,2},{1,3},{2,0},{3,1},{4,6},{5,7},{6,4},{7,5},{8,10},{9,11},{10,... | collective-permute-start | bytes 1769480 | tf_op jit(solution)/shard_map/ppermute | solution.py:92
  11.4 10.8 %collective-permute-done.7.refs_9_.refs_10_.refs_19_.refs_7_ = bf16[9,2,128,128]{3,2,1,0:T(8,128)(2,1)S(1)} collective-permute-done((bf16[9,2,128,128]{3,2,1,0:T(8,128)(2,1)}, bf16[9,2,128,128]{3,2,1,0:T(8,128)(2,1)S(1)}, u32[]{:S(2)}, u32[]{:S(2)}) %collective-permute-start.7) | collective-permute-done | bytes 589856 | tf_op jit(solution)/shard_map/ppermute | solution.py:92
  22.2 3.1 %collective-permute-start.12 = (bf16[2,128,256]{2,1,0:T(8,128)(2,1)}, bf16[2,128,256]{2,1,0:T(8,128)(2,1)S(1)}, u32[]{:S(2)}, u32[]{:S(2)}) collective-permute-start(bf16[2,128,256]{2,1,0:T(8,128)(2,1)} %get-tuple-element.48.refs_2_), channel_id=1, source_target_pairs={{0,16},{4,20},{8,24},{12,28},{16,0},{20,4},{24,8},{28,12},{1,17},{... | collective-permute-start | bytes 393224 | tf_op jit(solution)/shard_map/ppermute | solution.py:245
  26.8 5.7 %collective-permute-done.12.refs_3_ = bf16[2,128,256]{2,1,0:T(8,128)(2,1)S(1)} collective-permute-done((bf16[2,128,256]{2,1,0:T(8,128)(2,1)}, bf16[2,128,256]{2,1,0:T(8,128)(2,1)S(1)}, u32[]{:S(2)}, u32[]{:S(2)}) %collective-permute-start.12) | collective-permute-done | bytes 131104 | tf_op jit(solution)/shard_map/ppermute | solution.py:245
  34.5 3.3 %collective-permute-done.16.refs_7_ = bf16[2,128,256]{2,1,0:T(8,128)(2,1)S(1)} collective-permute-done((bf16[2,128,256]{2,1,0:T(8,128)(2,1)S(1)}, bf16[2,128,256]{2,1,0:T(8,128)(2,1)S(1)}, u32[]{:S(2)}, u32[]{:S(2)}) %collective-permute-start.16) | collective-permute-done | bytes 131104 | tf_op jit(solution)/shard_map/ppermute | solution.py:245
  39.4 4.0 %collective-permute-done.14.refs_5_ = bf16[2,128,256]{2,1,0:T(8,128)(2,1)S(1)} collective-permute-done((bf16[2,128,256]{2,1,0:T(8,128)(2,1)S(1)}, bf16[2,128,256]{2,1,0:T(8,128)(2,1)S(1)}, u32[]{:S(2)}, u32[]{:S(2)}) %collective-permute-start.14) | collective-permute-done | bytes 131104 | tf_op jit(solution)/shard_map/ppermute | solution.py:245
  45.4 3.2 %collective-permute-done.18.refs_9_ = bf16[2,128,256]{2,1,0:T(8,128)(2,1)} collective-permute-done((bf16[2,128,256]{2,1,0:T(8,128)(2,1)S(1)}, bf16[2,128,256]{2,1,0:T(8,128)(2,1)}, u32[]{:S(2)}, u32[]{:S(2)}) %collective-permute-start.18) | collective-permute-done | bytes 131104 | tf_op jit(solution)/shard_map/ppermute | solution.py:245
  51.2 2.6 %shard_map.67 = (bf16[2,2,128,128]{3,2,1,0:T(8,128)(2,1)}, bf16[4,2,128,128]{3,2,1,0:T(8,128)(2,1)}) custom-call(s32[1]{0:T(128)} %bitcast.refs_0_, s32[1]{0:T(128)} %bitcast.4.refs_1_, bf16[2,128,256]{2,1,0:T(8,128)(2,1)S(1)} %copy-done.1, bf16[2,128,256]{2,1,0:T(8,128)(2,1)S(1)} %collective-permute-done.12.refs_3_, ...), custom_call_target="tpu_custom_call" | custom-call | tf_op jit(solution)/shard_map/pallas_call | solution.py:79
  57.0 12.6 %all_to_all.40.refs_3_ = bf16[8,16,128]{2,1,0:T(8,128)(2,1)S(1)} all-to-all(bf16[8,16,128]{2,1,0:T(8,128)(2,1)S(1)} %copy-done.6), channel_id=1, replica_groups=mesh['row'=8,'col'=4] {'row'}, dimensions={0} | all-to-all | bytes 65536 | tf_op jit(solution)/shard_map/all_to_all | solution.py:127
  71.4 3.3 %all-to-all-start.1 = ((bf16[8,16,128]{2,1,0:T(8,128)(2,1)}), bf16[8,16,128]{2,1,0:T(8,128)(2,1)S(1)}, u32[]{:S(2)}, u32[]{:S(2)}) async-start(bf16[8,16,128]{2,1,0:T(8,128)(2,1)} %get-tuple-element.33), calls=%async_computation.1 | async-start | bytes 65536 | tf_op jit(solution)/shard_map/all_to_all | solution.py:127
  75.3 6.1 %all-to-all-done.1.refs_4_ = bf16[8,16,128]{2,1,0:T(8,128)(2,1)S(1)} async-done(((bf16[8,16,128]{2,1,0:T(8,128)(2,1)}), bf16[8,16,128]{2,1,0:T(8,128)(2,1)S(1)}, u32[]{:S(2)}, u32[]{:S(2)}) %all-to-all-start.1) | async-done | bytes 32800 | tf_op jit(solution)/shard_map/all_to_all | solution.py:127
  83.4 9.9 %all_to_all.41.refs_5_ = bf16[8,16,128]{2,1,0:T(8,128)(2,1)S(1)} all-to-all(bf16[8,16,128]{2,1,0:T(8,128)(2,1)} %get-tuple-element.35), channel_id=1, replica_groups=mesh['row'=8,'col'=4] {'row'}, dimensions={0} | all-to-all | bytes 65536 | tf_op jit(solution)/shard_map/all_to_all | solution.py:127
  95.4 3.3 %all-to-all-start.3 = ((bf16[8,16,128]{2,1,0:T(8,128)(2,1)}), bf16[8,16,128]{2,1,0:T(8,128)(2,1)S(1)}, u32[]{:S(2)}, u32[]{:S(2)}) async-start(bf16[8,16,128]{2,1,0:T(8,128)(2,1)} %get-tuple-element.36), calls=%async_computation.3 | async-start | bytes 65536 | tf_op jit(solution)/shard_map/all_to_all | solution.py:127
  99.9 5.5 %all-to-all-done.3.refs_6_ = bf16[8,16,128]{2,1,0:T(8,128)(2,1)S(1)} async-done(((bf16[8,16,128]{2,1,0:T(8,128)(2,1)}), bf16[8,16,128]{2,1,0:T(8,128)(2,1)S(1)}, u32[]{:S(2)}, u32[]{:S(2)}) %all-to-all-start.3) | async-done | bytes 32800 | tf_op jit(solution)/shard_map/all_to_all | solution.py:127
  107.6 9.9 %all_to_all.42.refs_7_ = bf16[8,16,128]{2,1,0:T(8,128)(2,1)S(1)} all-to-all(bf16[8,16,128]{2,1,0:T(8,128)(2,1)} %get-tuple-element.38), channel_id=1, replica_groups=mesh['row'=8,'col'=4] {'row'}, dimensions={0} | all-to-all | bytes 65536 | tf_op jit(solution)/shard_map/all_to_all | solution.py:127
  117.5 2.7 %shard_map.65 = (f32[6,16,128]{2,1,0:T(8,128)}, f32[16,128]{1,0:T(8,128)}, bf16[16,128]{1,0:T(8,128)(2,1)}, bf16[8,1,16,128]{3,2,1,0:T(8,128)(2,1)}) custom-call(s32[1]{0:T(128)} %bitcast.refs_0_, f32[6,1,64,128]{3,2,1,0:T(8,128)} %refs_1_.11, f32[6,1,128,128]{3,2,1,0:T(8,128)} %refs_3_.7, bf16[8,16,128]{2,1,0:T(8,128)(2,1)S(1)} %all_to_all.40.refs_3_, ...), custom_call_target="tpu_custom_call" | custom-call | tf_op jit(solution)/shard_map/pallas_call | solution.py:79
  120.2 9.9 %all_to_all.43.refs_1_ = bf16[8,1,16,128]{3,2,1,0:T(8,128)(2,1)S(1)} all-to-all(bf16[8,1,16,128]{3,2,1,0:T(8,128)(2,1)} %get-tuple-element.46), channel_id=1, replica_groups=mesh['row'=8,'col'=4] {'row'}, dimensions={0} | all-to-all | bytes 65536 | tf_op jit(solution)/shard_map/all_to_all | solution.py:127
  132.2 3.4 %all-to-all-start.6 = ((bf16[8,2,16,128]{3,2,1,0:T(8,128)(2,1)}), bf16[8,2,16,128]{3,2,1,0:T(8,128)(2,1)S(1)}, u32[]{:S(2)}, u32[]{:S(2)}) async-start(bf16[8,2,16,128]{3,2,1,0:T(8,128)(2,1)} %get-tuple-element.50), calls=%async_computation.6 | async-start | bytes 131072 | tf_op jit(solution)/shard_map/all_to_all | solution.py:127
  135.6 2.2 %shard_map.69 = (f32[8,2,16,128]{3,2,1,0:T(8,128)}, f32[8,128]{1,0:T(8,128)}) custom-call(s32[1]{0:T(128)} %bitcast.refs_0_, bf16[16,128]{1,0:T(8,128)(2,1)} %get-tuple-element.51.refs_1_, bf16[16,128]{1,0:T(8,128)(2,1)} %get-tuple-element.47.refs_4_.refs_2_, f32[16,128]{1,0:T(8,128)} %get-tuple-element.40.refs_17_.refs_3_.refs_5_, ...), custom_call_target="tpu_custom_call" | custom-call | tf_op jit(solution)/shard_map/pallas_call | solution.py:79
  137.8 4.6 %all-to-all-done.6.refs_1_ = bf16[8,2,16,128]{3,2,1,0:T(8,128)(2,1)S(1)} async-done(((bf16[8,2,16,128]{3,2,1,0:T(8,128)(2,1)}), bf16[8,2,16,128]{3,2,1,0:T(8,128)(2,1)S(1)}, u32[]{:S(2)}, u32[]{:S(2)}) %all-to-all-start.6) | async-done | bytes 65568 | tf_op jit(solution)/shard_map/all_to_all | solution.py:127
  142.4 2.3 %shard_map.70 = (bf16[16,128]{1,0:T(8,128)(2,1)}, bf16[16,128]{1,0:T(8,128)(2,1)}, bf16[8,2,16,128]{3,2,1,0:T(8,128)(2,1)}, f32[4,16,128]{2,1,0:T(8,128)}) custom-call(s32[1]{0:T(128)} %bitcast.refs_0_, bf16[8,2,16,128]{3,2,1,0:T(8,128)(2,1)S(1)} %all-to-all-done.6.refs_1_, f32[6,1,128,128]{3,2,1,0:T(8,128)} %refs_3_.7, f32[6,1,128,128]{3,2,1,0:T(8,128)} %refs_3_.7, ...), custom_call_target="tpu_custom_call" | custom-call | tf_op jit(solution)/shard_map/pallas_call | solution.py:79
  144.7 3.5 %all-to-all-start.7 = ((bf16[8,2,16,128]{3,2,1,0:T(8,128)(2,1)}), bf16[8,2,16,128]{3,2,1,0:T(8,128)(2,1)S(1)}, u32[]{:S(2)}, u32[]{:S(2)}) async-start(bf16[8,2,16,128]{3,2,1,0:T(8,128)(2,1)} %get-tuple-element.56), calls=%async_computation.7 | async-start | bytes 131072 | tf_op jit(solution)/shard_map/all_to_all | solution.py:127
  152.0 3.0 %all-to-all-done.7.refs_1_ = bf16[8,2,16,128]{3,2,1,0:T(8,128)(2,1)S(1)} async-done(((bf16[8,2,16,128]{3,2,1,0:T(8,128)(2,1)}), bf16[8,2,16,128]{3,2,1,0:T(8,128)(2,1)S(1)}, u32[]{:S(2)}, u32[]{:S(2)}) %all-to-all-start.7) | async-done | bytes 65568 | tf_op jit(solution)/shard_map/all_to_all | solution.py:127
  (82 shorter events, 41.0 us)
Async XLA Ops:
  4.8 17.4 %collective-permute-start.7 = (bf16[9,2,128,128]{3,2,1,0:T(8,128)(2,1)}, bf16[9,2,128,128]{3,2,1,0:T(8,128)(2,1)S(1)}, u32[]{:S(2)}, u32[]{:S(2)}) collective-permute-start(bf16[9,2,128,128]{3,2,1,0:T(8,128)(2,1)} %get-tuple-element.37.refs_7_.refs_11_.refs_12_.refs_13_.refs_8_.refs_14_.refs_15_.refs_17_.refs, ...), channel_id=1, source_target_pairs={{0,2},{1,3},{2,0},{3,1},{4,6},{5,7},{6,4},{7,5},{8,10},{9,11},{10,... | collective-permute-start | bytes 1769480 | tf_op jit(solution)/shard_map/ppermute | solution.py:92
  7.8 14.4 %collective-permute-start.15 = (bf16[2,128,256]{2,1,0:T(8,128)(2,1)}, bf16[2,128,256]{2,1,0:T(8,128)(2,1)S(1)}, u32[]{:S(2)}, u32[]{:S(2)}) collective-permute-start(bf16[2,128,256]{2,1,0:T(8,128)(2,1)} %get-tuple-element.48.refs_2_), channel_id=1, source_target_pairs={{0,4},{4,0},{8,12},{12,8},{16,20},{20,16},{24,28},{28,24},{1,5},{5... | collective-permute-start | bytes 393224 | tf_op jit(solution)/shard_map/ppermute | solution.py:245
  9.3 24.7 %collective-permute-start.4 = (bf16[5,2,128,128]{3,2,1,0:T(8,128)(2,1)}, bf16[5,2,128,128]{3,2,1,0:T(8,128)(2,1)S(1)}, u32[]{:S(2)}, u32[]{:S(2)}) collective-permute-start(bf16[5,2,128,128]{3,2,1,0:T(8,128)(2,1)} %get-tuple-element.34.refs_5_.refs_9_.refs_6_.refs_10_.refs_11_.refs_14_.refs_15_.refs_16_.refs_7_), channel_id=1, source_target_pairs={{0,2},{1,3},{2,0},{3,1},{4,6},{5,7},{6,4},{7,5},{8,10},{9,11},{10,... | collective-permute-start | bytes 983048 | tf_op jit(solution)/shard_map/ppermute | solution.py:92
  9.8 15.5 %collective-permute-start.13 = (bf16[2,128,256]{2,1,0:T(8,128)(2,1)}, bf16[2,128,256]{2,1,0:T(8,128)(2,1)S(1)}, u32[]{:S(2)}, u32[]{:S(2)}) collective-permute-start(bf16[2,128,256]{2,1,0:T(8,128)(2,1)} %get-tuple-element.48.refs_2_), channel_id=1, source_target_pairs={{0,8},{4,12},{8,0},{12,4},{16,24},{20,28},{24,16},{28,20},{1,9},{5... | collective-permute-start | bytes 393224 | tf_op jit(solution)/shard_map/ppermute | solution.py:245
  11.4 37.1 %collective-permute-start.6 = (bf16[9,2,128,128]{3,2,1,0:T(8,128)(2,1)}, bf16[9,2,128,128]{3,2,1,0:T(8,128)(2,1)S(1)}, u32[]{:S(2)}, u32[]{:S(2)}) collective-permute-start(bf16[9,2,128,128]{3,2,1,0:T(8,128)(2,1)} %get-tuple-element.37.refs_7_.refs_11_.refs_12_.refs_13_.refs_8_.refs_14_.refs_15_.refs_17_.refs, ...), channel_id=1, source_target_pairs={{0,1},{1,0},{2,3},{3,2},{4,5},{5,4},{6,7},{7,6},{8,9},{9,8},{10,11... | collective-permute-start | bytes 1769480 | tf_op jit(solution)/shard_map/ppermute | solution.py:92
  22.2 26.3 %collective-permute-start.8 = (bf16[9,2,128,128]{3,2,1,0:T(8,128)(2,1)S(1)}, bf16[9,2,128,128]{3,2,1,0:T(8,128)(2,1)S(1)}, u32[]{:S(2)}, u32[]{:S(2)}) collective-permute-start(bf16[9,2,128,128]{3,2,1,0:T(8,128)(2,1)S(1)} %collective-permute-done.7.refs_9_.refs_10_.refs_19_.refs_7_), channel_id=1, source_target_pairs={{0,1},{1,0},{2,3},{3,2},{4,5},{5,4},{6,7},{7,6},{8,9},{9,8},{10,11... | collective-permute-start | bytes 1769480 | tf_op jit(solution)/shard_map/ppermute | solution.py:92
  22.2 10.3 %collective-permute-start.12 = (bf16[2,128,256]{2,1,0:T(8,128)(2,1)}, bf16[2,128,256]{2,1,0:T(8,128)(2,1)S(1)}, u32[]{:S(2)}, u32[]{:S(2)}) collective-permute-start(bf16[2,128,256]{2,1,0:T(8,128)(2,1)} %get-tuple-element.48.refs_2_), channel_id=1, source_target_pairs={{0,16},{4,20},{8,24},{12,28},{16,0},{20,4},{24,8},{28,12},{1,17},{... | collective-permute-start | bytes 393224 | tf_op jit(solution)/shard_map/ppermute | solution.py:245
  25.3 8.7 %collective-permute-start.17 = (bf16[2,128,256]{2,1,0:T(8,128)(2,1)S(1)}, bf16[2,128,256]{2,1,0:T(8,128)(2,1)S(1)}, u32[]{:S(2)}, u32[]{:S(2)}) collective-permute-start(bf16[2,128,256]{2,1,0:T(8,128)(2,1)S(1)} %collective-permute-done.13.refs_4_), channel_id=1, source_target_pairs={{0,4},{4,0},{8,12},{12,8},{16,20},{20,16},{24,28},{28,24},{1,5},{5... | collective-permute-start | bytes 393224 | tf_op jit(solution)/shard_map/ppermute | solution.py:245
  34.0 11.3 %collective-permute-start.3 = (bf16[5,2,128,128]{3,2,1,0:T(8,128)(2,1)}, bf16[5,2,128,128]{3,2,1,0:T(8,128)(2,1)S(1)}, u32[]{:S(2)}, u32[]{:S(2)}) collective-permute-start(bf16[5,2,128,128]{3,2,1,0:T(8,128)(2,1)} %get-tuple-element.34.refs_5_.refs_9_.refs_6_.refs_10_.refs_11_.refs_14_.refs_15_.refs_16_.refs_7_), channel_id=1, source_target_pairs={{0,1},{1,0},{2,3},{3,2},{4,5},{5,4},{6,7},{7,6},{8,9},{9,8},{10,11... | collective-permute-start | bytes 983048 | tf_op jit(solution)/shard_map/ppermute | solution.py:92
  34.0 14.5 %collective-permute-start.5 = (bf16[5,2,128,128]{3,2,1,0:T(8,128)(2,1)S(1)}, bf16[5,2,128,128]{3,2,1,0:T(8,128)(2,1)S(1)}, u32[]{:S(2)}, u32[]{:S(2)}) collective-permute-start(bf16[5,2,128,128]{3,2,1,0:T(8,128)(2,1)S(1)} %collective-permute-done.4.refs_7_.refs_8_.refs_12_.refs_17_.refs_9_), channel_id=1, source_target_pairs={{0,1},{1,0},{2,3},{3,2},{4,5},{5,4},{6,7},{7,6},{8,9},{9,8},{10,11... | collective-permute-start | bytes 983048 | tf_op jit(solution)/shard_map/ppermute | solution.py:92
  53.8 45.0 %collective-permute-start.23 = (bf16[4,2,128,128]{3,2,1,0:T(8,128)(2,1)}, bf16[4,2,128,128]{3,2,1,0:T(8,128)(2,1)}, u32[]{:S(2)}, u32[]{:S(2)}) collective-permute-start(bf16[4,2,128,128]{3,2,1,0:T(8,128)(2,1)} %get-tuple-element.52.refs_10_.refs_14_.refs_12_.refs_16_), channel_id=1, source_target_pairs={{0,2},{1,3},{2,0},{3,1},{4,6},{5,7},{6,4},{7,5},{8,10},{9,11},{10,... | collective-permute-start | bytes 786440 | tf_op jit(solution)/shard_map/ppermute | solution.py:92
  55.1 14.5 %collective-permute-start.2 = (bf16[1,2,128,128]{3,2,1,0:T(8,128)(2,1)S(1)}, bf16[1,2,128,128]{3,2,1,0:T(8,128)(2,1)S(1)}, u32[]{:S(2)}, u32[]{:S(2)}) collective-permute-start(bf16[1,2,128,128]{3,2,1,0:T(8,128)(2,1)S(1)} %copy-done), channel_id=1, source_target_pairs={{0,3},{1,2},{2,1},{3,0},{4,7},{5,6},{6,5},{7,4},{8,11},{9,10},{10,... | collective-permute-start | bytes 196616 | tf_op jit(solution)/shard_map/ppermute | solution.py:92
  55.1 14.5 %collective-permute-start.1 = (bf16[1,2,128,128]{3,2,1,0:T(8,128)(2,1)S(1)}, bf16[1,2,128,128]{3,2,1,0:T(8,128)(2,1)S(1)}, u32[]{:S(2)}, u32[]{:S(2)}) collective-permute-start(bf16[1,2,128,128]{3,2,1,0:T(8,128)(2,1)S(1)} %copy-done), channel_id=1, source_target_pairs={{0,2},{1,3},{2,0},{3,1},{4,6},{5,7},{6,4},{7,5},{8,10},{9,11},{10,... | collective-permute-start | bytes 196616 | tf_op jit(solution)/shard_map/ppermute | solution.py:92
  55.8 13.7 %collective-permute-start = (bf16[1,2,128,128]{3,2,1,0:T(8,128)(2,1)S(1)}, bf16[1,2,128,128]{3,2,1,0:T(8,128)(2,1)S(1)}, u32[]{:S(2)}, u32[]{:S(2)}) collective-permute-start(bf16[1,2,128,128]{3,2,1,0:T(8,128)(2,1)S(1)} %copy-done), channel_id=1, source_target_pairs={{0,1},{1,0},{2,3},{3,2},{4,5},{5,4},{6,7},{7,6},{8,9},{9,8},{10,11... | collective-permute-start | bytes 196616 | tf_op jit(solution)/shard_map/ppermute | solution.py:92
  71.4 10.0 %all-to-all-start.1 = ((bf16[8,16,128]{2,1,0:T(8,128)(2,1)}), bf16[8,16,128]{2,1,0:T(8,128)(2,1)S(1)}, u32[]{:S(2)}, u32[]{:S(2)}) async-start(bf16[8,16,128]{2,1,0:T(8,128)(2,1)} %get-tuple-element.33), calls=%async_computation.1 | async-start | bytes 65536 | tf_op jit(solution)/shard_map/all_to_all | solution.py:127
  74.8 24.6 %collective-permute-start.20 = (bf16[2,2,128,128]{3,2,1,0:T(8,128)(2,1)}, bf16[2,2,128,128]{3,2,1,0:T(8,128)(2,1)S(1)}, u32[]{:S(2)}, u32[]{:S(2)}) collective-permute-start(bf16[2,2,128,128]{3,2,1,0:T(8,128)(2,1)} %get-tuple-element.49.refs_11_.refs_20_), channel_id=1, source_target_pairs={{0,2},{1,3},{2,0},{3,1},{4,6},{5,7},{6,4},{7,5},{8,10},{9,11},{10,... | collective-permute-start | bytes 393224 | tf_op jit(solution)/shard_map/ppermute | solution.py:92
  95.4 10.0 %all-to-all-start.3 = ((bf16[8,16,128]{2,1,0:T(8,128)(2,1)}), bf16[8,16,128]{2,1,0:T(8,128)(2,1)S(1)}, u32[]{:S(2)}, u32[]{:S(2)}) async-start(bf16[8,16,128]{2,1,0:T(8,128)(2,1)} %get-tuple-element.36), calls=%async_computation.3 | async-start | bytes 65536 | tf_op jit(solution)/shard_map/all_to_all | solution.py:127
  98.8 36.8 %collective-permute-start.22 = (bf16[4,2,128,128]{3,2,1,0:T(8,128)(2,1)}, bf16[4,2,128,128]{3,2,1,0:T(8,128)(2,1)}, u32[]{:S(2)}, u32[]{:S(2)}) collective-permute-start(bf16[4,2,128,128]{3,2,1,0:T(8,128)(2,1)} %get-tuple-element.52.refs_10_.refs_14_.refs_12_.refs_16_), channel_id=1, source_target_pairs={{0,1},{1,0},{2,3},{3,2},{4,5},{5,4},{6,7},{7,6},{8,9},{9,8},{10,11... | collective-permute-start | bytes 786440 | tf_op jit(solution)/shard_map/ppermute | solution.py:92
  98.8 36.7 %collective-permute-start.24 = (bf16[4,2,128,128]{3,2,1,0:T(8,128)(2,1)}, bf16[4,2,128,128]{3,2,1,0:T(8,128)(2,1)}, u32[]{:S(2)}, u32[]{:S(2)}) collective-permute-start(bf16[4,2,128,128]{3,2,1,0:T(8,128)(2,1)} %collective-permute-done.23.refs_12_.refs_16_.refs_14_.refs_18_), channel_id=1, source_target_pairs={{0,1},{1,0},{2,3},{3,2},{4,5},{5,4},{6,7},{7,6},{8,9},{9,8},{10,11... | collective-permute-start | bytes 786440 | tf_op jit(solution)/shard_map/ppermute | solution.py:92
  99.3 30.8 %collective-permute-start.19 = (bf16[2,2,128,128]{3,2,1,0:T(8,128)(2,1)}, bf16[2,2,128,128]{3,2,1,0:T(8,128)(2,1)S(1)}, u32[]{:S(2)}, u32[]{:S(2)}) collective-permute-start(bf16[2,2,128,128]{3,2,1,0:T(8,128)(2,1)} %get-tuple-element.49.refs_11_.refs_20_), channel_id=1, source_target_pairs={{0,1},{1,0},{2,3},{3,2},{4,5},{5,4},{6,7},{7,6},{8,9},{9,8},{10,11... | collective-permute-start | bytes 393224 | tf_op jit(solution)/shard_map/ppermute | solution.py:92
  99.4 30.7 %collective-permute-start.21 = (bf16[2,2,128,128]{3,2,1,0:T(8,128)(2,1)S(1)}, bf16[2,2,128,128]{3,2,1,0:T(8,128)(2,1)S(1)}, u32[]{:S(2)}, u32[]{:S(2)}) collective-permute-start(bf16[2,2,128,128]{3,2,1,0:T(8,128)(2,1)S(1)} %collective-permute-done.20.refs_13_), channel_id=1, source_target_pairs={{0,1},{1,0},{2,3},{3,2},{4,5},{5,4},{6,7},{7,6},{8,9},{9,8},{10,11... | collective-permute-start | bytes 393224 | tf_op jit(solution)/shard_map/ppermute | solution.py:92
  132.2 10.2 %all-to-all-start.6 = ((bf16[8,2,16,128]{3,2,1,0:T(8,128)(2,1)}), bf16[8,2,16,128]{3,2,1,0:T(8,128)(2,1)S(1)}, u32[]{:S(2)}, u32[]{:S(2)}) async-start(bf16[8,2,16,128]{3,2,1,0:T(8,128)(2,1)} %get-tuple-element.50), calls=%async_computation.6 | async-start | bytes 131072 | tf_op jit(solution)/shard_map/all_to_all | solution.py:127
  144.7 10.3 %all-to-all-start.7 = ((bf16[8,2,16,128]{3,2,1,0:T(8,128)(2,1)}), bf16[8,2,16,128]{3,2,1,0:T(8,128)(2,1)S(1)}, u32[]{:S(2)}, u32[]{:S(2)}) async-start(bf16[8,2,16,128]{3,2,1,0:T(8,128)(2,1)} %get-tuple-element.56), calls=%async_computation.7 | async-start | bytes 131072 | tf_op jit(solution)/shard_map/all_to_all | solution.py:127
  150.5 9.5 %collective-permute-start.29 = (f32[4,16,128]{2,1,0:T(8,128)S(1)}, f32[4,16,128]{2,1,0:T(8,128)S(1)}, u32[]{:S(2)}, u32[]{:S(2)}) collective-permute-start(f32[4,16,128]{2,1,0:T(8,128)S(1)} %copy-done.8), channel_id=1, source_target_pairs={{0,2},{1,3},{2,0},{3,1},{4,6},{5,7},{6,4},{7,5},{8,10},{9,11},{10,... | collective-permute-start | bytes 98312 | tf_op jit(solution)/shard_map/ppermute | solution.py:92
  (20 other events, 84.0 us)
